TPU v7x, 32 devices: a whole 2x2x4 slice. The times are simulated.
32 devices in a mesh: batch: 8 (over y, x, core), seq: 4 (over z).
Axes of the slice: x: 2, y: 2, z: 4, core: 2. Of those that a mesh axis runs over, the one named last changes fastest.
Arguments:
- tokens: bfloat16 [8, 1024, 2048], P('batch', 'seq'), may hold values from -6 to 6
- segments: int32 [8, 1024], P('batch'), may hold values from 0 to 7, never falling along the last dimension, each value on 1 to 512 neighbouring positions
- valid_count: int32 [8], P('batch'), may hold values from 256 to 1024, as said below
- cotangent: bfloat16 [8, 1024, 2048], P('batch', 'seq'), may hold values from -6 to 6
- w_qkv: bfloat16 [2048, 6144], P(('batch', 'seq')), may hold values from -0.125 to 0.125
- w_out: bfloat16 [2048, 2048], P(None, ('batch', 'seq')), may hold values from -0.125 to 0.125
- w_up: bfloat16 [2048, 8192], P(('batch', 'seq')), may hold values from -0.125 to 0.125
- w_down: bfloat16 [8192, 2048], P(None, ('batch', 'seq')), may hold values from -0.0625 to 0.0625
- gain_attn: bfloat16 [2048], P(('batch', 'seq')), may hold values from 0.5 to 1.5
- bias_attn: bfloat16 [2048], P(('batch', 'seq')), may hold values from -1.1953125 to 1.1953125
- gain_mix: bfloat16 [2048], P(('batch', 'seq')), may hold values from 0.5 to 1.5
- bias_mix: bfloat16 [2048], P(('batch', 'seq')), may hold values from -1.1953125 to 1.1953125
- gain_ffn: bfloat16 [2048], P(('batch', 'seq')), may hold values from 0.5 to 1.5
- bias_ffn: bfloat16 [2048], P(('batch', 'seq')), may hold values from -1.1953125 to 1.1953125
- gain_hidden: bfloat16 [8192], P(('batch', 'seq')), may hold values from 0.5 to 1.5
- bias_hidden: bfloat16 [8192], P(('batch', 'seq')), may hold values from -1.1953125 to 1.1953125
Outputs:
- output: bfloat16 [8, 1024, 2048], P('batch', 'seq')
- grad_tokens: float32 [8, 1024, 2048], P('batch', 'seq')
- grad_w_qkv: float32 [2048, 6144], P(('batch', 'seq'))
- grad_w_out: float32 [2048, 2048], P(None, ('batch', 'seq'))
- grad_w_up: float32 [2048, 8192], P(('batch', 'seq'))
- grad_w_down: float32 [8192, 2048], P(None, ('batch', 'seq'))
- grad_gain_attn: float32 [2048], P(('batch', 'seq'))
- grad_bias_attn: float32 [2048], P(('batch', 'seq'))
- grad_gain_mix: float32 [2048], P(('batch', 'seq'))
- grad_bias_mix: float32 [2048], P(('batch', 'seq'))
- grad_gain_ffn: float32 [2048], P(('batch', 'seq'))
- grad_bias_ffn: float32 [2048], P(('batch', 'seq'))
- grad_gain_hidden: float32 [8192], P(('batch', 'seq'))
- grad_bias_hidden: float32 [8192], P(('batch', 'seq'))
Inputs may be any that keep to these rules, and one draw needn't show every extreme that they name: `segments`: in each row the segment id never falls along the slots; each id covers 1 to 512 slots. `valid_count`: in every draw some row has all 1024 slots used.
All inputs are finite; a program needn't handle non-finite values.
Results may differ from a plain program's by a relative error of at most 0.015.
Values may be sent and summed in bfloat16 or wider, within the bound.
No kernel may reach another device: no remote copies, remote signals or barrier semaphores. Data moves between devices by JAX's collectives and lax.ppermute only.
A program may use at most 640 MiB of HBM per device.

v0:
```python
import jax
import jax.numpy as jnp
from jax import lax
from jax.sharding import PartitionSpec as P

EPSILON = 1e-05


def layer_norm(values, gain, bias):
    center = values - jnp.mean(values, axis=-1, keepdims=True)
    spread = jnp.mean(center * center, axis=-1, keepdims=True)
    return center * lax.rsqrt(spread + EPSILON) * gain + bias


def hidden_norm(hidden, gain, bias):
    return layer_norm(jax.nn.gelu(hidden, approximate=False), gain, bias)


def xpos_tables(first, count, total):
    slot_pos = (first + jnp.arange(count, dtype=jnp.int32) - total // 2).astype(jnp.float32)
    index = jnp.arange(32, dtype=jnp.int32).astype(jnp.float32)
    angle = slot_pos[:, None] * jnp.exp(index * (-jnp.log(10000.0) / 32.0))[None, :]
    zeta = (index / 32.0 + 0.4) / 1.4
    growth = jnp.exp(slot_pos[:, None] * jnp.log(zeta)[None, :] / 512.0)
    return (jnp.cos(angle), jnp.sin(angle), growth)


def rotate(head_view, cosine, sine, growth):
    lower = head_view[..., :32]
    upper = head_view[..., 32:]
    cosine = cosine[:, None, :]
    sine = sine[:, None, :]
    growth = growth[:, None, :]
    return jnp.concatenate(
        [(lower * cosine - upper * sine) * growth, (upper * cosine + lower * sine) * growth],
        axis=-1,
    )


def position(raw, group, cosine, sine, growth):
    count = raw.shape[0]
    head_count = group // 64
    queries = rotate(raw[:, :group].reshape(count, head_count, 64), cosine, sine, growth)
    key_rows = rotate(
        raw[:, group : 2 * group].reshape(count, head_count, 64), cosine, sine, 1.0 / growth
    )
    return (queries, key_rows, raw[:, 2 * group :].reshape(count, head_count, 64))


def allowed_mask(query_slots, key_slots, seg_query, seg_key, valid_len):
    same = seg_query[:, None] == seg_key[None, :]
    before = key_slots[None, :] <= query_slots[:, None]
    living = (query_slots < valid_len)[:, None]
    return (key_slots[None, :] == query_slots[:, None]) | same & before & living


def shards(
    tokens,
    segments,
    valid_count,
    cotangent,
    w_qkv,
    w_out,
    w_up,
    w_down,
    gain_attn,
    bias_attn,
    gain_mix,
    bias_mix,
    gain_ffn,
    bias_ffn,
    gain_hidden,
    bias_hidden,
):
    low_type = jnp.bfloat16
    wide = jnp.float32
    width = tokens.shape[2]
    heads = width // 64
    slots = tokens.shape[1]
    length = segments.shape[1]
    seq_index = lax.axis_index("seq")
    first = seq_index * slots
    query_slots = first + jnp.arange(slots, dtype=jnp.int32)
    seg_row = segments[0]
    seg_query = lax.dynamic_slice_in_dim(seg_row, first, slots, 0)
    valid_len = valid_count[0]
    resid = tokens[0].astype(wide)
    block = min(512, length)
    offsets = jnp.arange(length // block, dtype=jnp.int32) * block
    gathered = (
        lax.all_gather(gain_attn, ("batch", "seq"), axis=0, tiled=True),
        lax.all_gather(bias_attn, ("batch", "seq"), axis=0, tiled=True),
        lax.all_gather(gain_mix, ("batch", "seq"), axis=0, tiled=True),
        lax.all_gather(bias_mix, ("batch", "seq"), axis=0, tiled=True),
        lax.all_gather(gain_ffn, ("batch", "seq"), axis=0, tiled=True),
        lax.all_gather(bias_ffn, ("batch", "seq"), axis=0, tiled=True),
        lax.all_gather(gain_hidden, ("batch", "seq"), axis=0, tiled=True),
        lax.all_gather(bias_hidden, ("batch", "seq"), axis=0, tiled=True),
    )
    vectors = [vector.astype(wide) for vector in gathered]
    living = (query_slots < valid_len).astype(wide)
    grad_out = cotangent[0].astype(wide) * living[:, None]
    grad_low = grad_out.astype(low_type)
    qkv_all, out_all = (
        lax.all_gather(w_qkv, ("batch", "seq"), axis=0, tiled=True),
        lax.all_gather(w_out, ("batch", "seq"), axis=1, tiled=True),
    )
    normed_low = layer_norm(resid, vectors[0], vectors[1]).astype(low_type)
    projected = jnp.dot(normed_low, qkv_all, preferred_element_type=wide)
    cosine, sine, growth = xpos_tables(first, slots, length)
    queries, key_rows, value_rows = position(projected, width, cosine, sine, growth)
    query_low = queries.astype(low_type)
    query_wide = query_low.astype(wide)
    key_low = key_rows.reshape(slots, width).astype(low_type)
    value_low = value_rows.reshape(slots, width).astype(low_type)
    key_all, value_all = (
        lax.all_gather(key_low, "seq", axis=0, tiled=True),
        lax.all_gather(value_low, "seq", axis=0, tiled=True),
    )

    def block_scores(key_block, key_start):
        count = key_block.shape[0]
        key_slots = key_start + jnp.arange(count, dtype=jnp.int32)
        seg_key = lax.dynamic_slice_in_dim(seg_row, key_start, count, 0)
        allowed = allowed_mask(query_slots, key_slots, seg_query, seg_key, valid_len)
        raw = (
            jnp.einsum(
                "qhd,khd->hqk",
                query_low,
                key_block.reshape(count, heads, 64),
                preferred_element_type=wide,
            )
            * 0.125
        )
        return (jnp.where(allowed[None], raw, -1e30), allowed)

    def fold_step(state, offset):
        summed_values, top, total = state
        key_block = lax.dynamic_slice_in_dim(key_all, offset, block, 0)
        value_block = lax.dynamic_slice_in_dim(value_all, offset, block, 0)
        scores, allowed = block_scores(key_block, offset)
        new_top = jnp.maximum(top, jnp.max(scores, axis=-1))
        rescale = jnp.exp(top - new_top)
        weight = jnp.where(allowed[None], jnp.exp(scores - new_top[..., None]), 0.0)
        total = total * rescale + jnp.sum(weight, axis=-1)
        summed_values = summed_values * rescale[..., None] + jnp.einsum(
            "hqk,khd->hqd", weight, value_block.reshape(block, heads, 64).astype(wide)
        )
        return ((summed_values, new_top, total), None)

    initial = (
        jnp.zeros((heads, slots, 64), wide),
        jnp.full((heads, slots), -1e30, wide),
        jnp.zeros((heads, slots), wide),
    )
    folded, unused_fold = lax.scan(fold_step, initial, offsets)
    summed_values, top, total = folded
    attended_heads = summed_values / total[..., None]
    log_total = top + jnp.log(total)
    attended = attended_heads.transpose(1, 0, 2).reshape(slots, width)
    mixed_low = layer_norm(attended, vectors[2], vectors[3]).astype(low_type)
    resid_mid = resid + jnp.dot(mixed_low, out_all, preferred_element_type=wide)
    up_all, down_all = (
        lax.all_gather(w_up, ("batch", "seq"), axis=0, tiled=True),
        lax.all_gather(w_down, ("batch", "seq"), axis=1, tiled=True),
    )
    ffn_low = layer_norm(resid_mid, vectors[4], vectors[5]).astype(low_type)
    hidden = jnp.dot(ffn_low, up_all, preferred_element_type=wide)
    hidden_low = hidden_norm(hidden, vectors[6], vectors[7]).astype(low_type)
    output = (resid_mid + jnp.dot(hidden_low, down_all, preferred_element_type=wide)).astype(
        low_type
    )
    grad_hn = jnp.dot(grad_low, down_all.T, preferred_element_type=wide)
    unused_hidden, pull_hidden = jax.vjp(hidden_norm, hidden, vectors[6], vectors[7])
    grad_hidden, grad_gain_hidden, grad_bias_hidden = pull_hidden(grad_hn)
    grad_hidden_low = grad_hidden.astype(low_type)
    up_part = jnp.dot(ffn_low.T, grad_hidden_low, preferred_element_type=wide)
    down_part = jnp.dot(grad_low.T, hidden_low, preferred_element_type=wide)
    ffn_grads = lax.psum_scatter(
        jnp.stack([up_part, down_part], axis=1), ("batch", "seq"), scatter_dimension=0, tiled=True
    )
    grad_w_up = ffn_grads[:, 0]
    grad_w_down = ffn_grads[:, 1].T
    grad_ffn_in = jnp.dot(grad_hidden_low, up_all.T, preferred_element_type=wide)
    unused_ffn, pull_ffn = jax.vjp(layer_norm, resid_mid, vectors[4], vectors[5])
    grad_mid_part, grad_gain_ffn, grad_bias_ffn = pull_ffn(grad_ffn_in)
    grad_mid = grad_out + grad_mid_part
    grad_mid_low = grad_mid.astype(low_type)
    out_term_t = jnp.dot(grad_mid_low.T, mixed_low, preferred_element_type=wide)
    grad_mixed = jnp.dot(grad_mid_low, out_all.T, preferred_element_type=wide)
    unused_mix, pull_mix = jax.vjp(layer_norm, attended, vectors[2], vectors[3])
    grad_attended, grad_gain_mix, grad_bias_mix = pull_mix(grad_mixed)
    grad_heads = grad_attended.reshape(slots, heads, 64).transpose(1, 0, 2)
    delta = jnp.sum(grad_heads * attended_heads, axis=-1)

    def back_step(grad_query, offset):
        key_block = lax.dynamic_slice_in_dim(key_all, offset, block, 0)
        value_block = lax.dynamic_slice_in_dim(value_all, offset, block, 0)
        scores, allowed = block_scores(key_block, offset)
        softmax_rows = jnp.where(allowed[None], jnp.exp(scores - log_total[..., None]), 0.0)
        grad_rows = jnp.einsum(
            "hqd,khd->hqk", grad_heads, value_block.reshape(block, heads, 64).astype(wide)
        )
        grad_raw = softmax_rows * (grad_rows - delta[..., None]) * 0.125
        key_wide = key_block.reshape(block, heads, 64).astype(wide)
        grad_query = grad_query + jnp.einsum("hqk,khd->hqd", grad_raw, key_wide)
        grad_key = jnp.einsum("hqk,qhd->khd", grad_raw, query_wide).reshape(block, width)
        grad_value = jnp.einsum("hqk,hqd->khd", softmax_rows, grad_heads).reshape(block, width)
        return (grad_query, (grad_key, grad_value))

    grad_query, key_value_terms = lax.scan(back_step, jnp.zeros((heads, slots, 64), wide), offsets)
    key_terms = key_value_terms[0].reshape(length, width)
    value_terms = key_value_terms[1].reshape(length, width)
    grad_key_own, grad_value_own = (
        lax.psum_scatter(
            key_terms.astype(jnp.bfloat16), "seq", scatter_dimension=0, tiled=True
        ).astype(jnp.float32),
        lax.psum_scatter(
            value_terms.astype(jnp.bfloat16), "seq", scatter_dimension=0, tiled=True
        ).astype(jnp.float32),
    )
    unused_pos, pull_pos = jax.vjp(
        lambda raw: position(raw, width, cosine, sine, growth), projected
    )
    grad_projected = pull_pos(
        (
            grad_query.transpose(1, 0, 2),
            grad_key_own.reshape(slots, heads, 64),
            grad_value_own.reshape(slots, heads, 64),
        )
    )[0]
    grad_proj_low = grad_projected.astype(low_type)
    qkv_term = jnp.dot(normed_low.T, grad_proj_low, preferred_element_type=wide)
    grad_normed = jnp.dot(grad_proj_low, qkv_all.T, preferred_element_type=wide)
    unused_attn, pull_attn = jax.vjp(layer_norm, resid, vectors[0], vectors[1])
    grad_resid_part, grad_gain_attn, grad_bias_attn = pull_attn(grad_normed)
    grad_tokens = grad_mid + grad_resid_part
    summed = (
        lax.psum_scatter(qkv_term, ("batch", "seq"), scatter_dimension=0, tiled=True),
        lax.psum_scatter(out_term_t, ("batch", "seq"), scatter_dimension=0, tiled=True),
        lax.psum_scatter(grad_gain_attn, ("batch", "seq"), scatter_dimension=0, tiled=True),
        lax.psum_scatter(grad_bias_attn, ("batch", "seq"), scatter_dimension=0, tiled=True),
        lax.psum_scatter(grad_gain_mix, ("batch", "seq"), scatter_dimension=0, tiled=True),
        lax.psum_scatter(grad_bias_mix, ("batch", "seq"), scatter_dimension=0, tiled=True),
        lax.psum_scatter(grad_gain_ffn, ("batch", "seq"), scatter_dimension=0, tiled=True),
        lax.psum_scatter(grad_bias_ffn, ("batch", "seq"), scatter_dimension=0, tiled=True),
        lax.psum_scatter(grad_gain_hidden, ("batch", "seq"), scatter_dimension=0, tiled=True),
        lax.psum_scatter(grad_bias_hidden, ("batch", "seq"), scatter_dimension=0, tiled=True),
    )
    grad_w_qkv = summed[0]
    grad_w_out = summed[1].T
    vector_grads = (
        summed[2],
        summed[3],
        summed[4],
        summed[5],
        summed[6],
        summed[7],
        summed[8],
        summed[9],
    )
    return (
        output[None],
        grad_tokens[None],
        grad_w_qkv,
        grad_w_out,
        grad_w_up,
        grad_w_down,
        vector_grads[0],
        vector_grads[1],
        vector_grads[2],
        vector_grads[3],
        vector_grads[4],
        vector_grads[5],
        vector_grads[6],
        vector_grads[7],
    )


def solution(mesh):
    return jax.shard_map(
        shards,
        mesh=mesh,
        in_specs=(
            P("batch", "seq", None),
            P("batch", None),
            P("batch"),
            P("batch", "seq", None),
            P(("batch", "seq"), None),
            P(None, ("batch", "seq")),
            P(("batch", "seq"), None),
            P(None, ("batch", "seq")),
            P(("batch", "seq")),
            P(("batch", "seq")),
            P(("batch", "seq")),
            P(("batch", "seq")),
            P(("batch", "seq")),
            P(("batch", "seq")),
            P(("batch", "seq")),
            P(("batch", "seq")),
        ),
        out_specs=(
            P("batch", "seq", None),
            P("batch", "seq", None),
            P(("batch", "seq"), None),
            P(None, ("batch", "seq")),
            P(("batch", "seq"), None),
            P(None, ("batch", "seq")),
            P(("batch", "seq")),
            P(("batch", "seq")),
            P(("batch", "seq")),
            P(("batch", "seq")),
            P(("batch", "seq")),
            P(("batch", "seq")),
            P(("batch", "seq")),
            P(("batch", "seq")),
        ),
        check_vma=False,
    )
```

profile of v0, /device:TPU:4, one launch (start us, length us, event | category | flops | bytes accessed | tf_op | source)
XLA Modules:
  0.0 4936.4 jit_solution(13424528410778479936)
XLA Ops:
  13.0 43.0 all-reduce.22
  59.8 108.7 %all-gather.9.cloned.1.call-done = bf16[2048,6144]{1,0:T(8,128)(2,1)} async-done(((bf16[64,6144]{1,0:T(8,128)(2,1)}), bf16[2048,6144]{1,0:T(8,128)(2,1)}) %all-gather.9.cloned.1.call-update) | async-done | bytes 25165840 | tf_op jit(solution)/shard_map/all_gather | solution.py:105
  168.5 12.0 fusion.73
  200.5 66.9 %all-gather = bf16[32,1,256]{2,1,0:T(2,128)(2,1)S(1)} all-gather(bf16[1,1,256]{2,1,0:T(2,128)(2,1)S(1)} %reshape.555), channel_id=1, replica_groups=mesh['batch'=8,'seq'=4] {'batch','seq'}, dimensions={0}, use_global_device_ids=true | all-gather | bytes 16896 | tf_op jit(solution)/shard_map/all_gather | solution.py:97
  275.3 69.9 %all-gather.11.cloned.1.call-done = bf16[1024,2048]{0,1:T(8,128)(2,1)} async-done(((bf16[256,2048]{0,1:T(8,128)(2,1)}), bf16[1024,2048]{0,1:T(8,128)(2,1)}) %all-gather.11.cloned.1.call-update) | async-done | bytes 4194320 | tf_op jit(solution)/shard_map/all_gather | solution.py:117
  345.2 55.6 %while.30 = (s32[]{:T(128)}, f32[32,256,64]{1,2,0:T(8,128)}, f32[32,256]{1,0:T(8,128)S(1)}, f32[32,256]{1,0:T(8,128)S(1)}, s32[2]{0:T(128)S(1)}, /*index=5*/s32[...) while((s32[]{:T(128)}, f32[32,256,64]{1,2,0:T(8,128)}, ...), condition=%wide.region_5.6_spmd.clone, body=%wide.region_2.5_spmd.clone.sunk | while | flops 1126475008 | bytes 136328976 | solution.py:156
  389.7 11.1 fusion.139
  405.0 18.5 all-gather.15.cloned.1.call-done
  432.0 187.8 %all-gather.17.cloned.1.call-done = bf16[2048,8192]{1,0:T(8,128)(2,1)} async-done(((bf16[64,8192]{1,0:T(8,128)(2,1)}), bf16[2048,8192]{1,0:T(8,128)(2,1)}) %all-gather.17.cloned.1.call-update) | async-done | bytes 33554448 | tf_op jit(solution)/shard_map/all_gather | solution.py:164
  619.8 33.8 fusion.81
  653.6 161.9 %all-gather.19.cloned.1.call-done = bf16[8192,2048]{0,1:T(8,128)(2,1)} async-done(((bf16[8192,64]{0,1:T(8,128)(2,1)}), bf16[8192,2048]{0,1:T(8,128)(2,1)}) %all-gather.19.cloned.1.call-update) | async-done | bytes 33554448 | tf_op jit(solution)/shard_map/all_gather | solution.py:165
  815.6 21.2 multiply_reduce_fusion.1
  836.8 10.0 multiply_reduce_fusion
  846.8 12.5 add_convert_fusion
  859.3 18.9 multiply_reduce_fusion.3
  898.6 122.0 %while.31 = (s32[]{:T(128)}, f32[32,256,64]{1,2,0:T(8,128)}, bf16[2,512,2048]{2,1,0:T(8,128)(2,1)}, bf16[2,512,2048]{2,1,0:T(8,128)(2,1)}, s32[2]{0:T(128)S(1)},...) while((s32[]{:T(128)}, f32[32,256,64]{1,2,0:T(8,128)}, ...), condition=%wide.region_20.21_spmd.clone, body=%wide.region_19.20_spmd.clone.sunk | while | flops 2736522496 | bytes 145209200 | solution.py:211
  918.0 11.5 fusion.152
  929.5 10.2 fusion.151
  977.8 11.5 fusion.152
  989.3 10.2 fusion.151
  1021.4 68.5 %all-gather.1 = bf16[32,1,256]{2,1,0:T(2,128)(2,1)S(1)} all-gather(bf16[1,1,256]{2,1,0:T(2,128)(2,1)S(1)} %reshape.557), channel_id=1, replica_groups=mesh['batch'=8,'seq'=4] {'batch','seq'}, dimensions={0}, use_global_device_ids=true | all-gather | bytes 16896 | tf_op jit(solution)/shard_map/all_gather | solution.py:98
  1090.1 26.5 convolution_bitcast_fusion.1
  1116.7 27.0 convolution_bitcast_fusion
  1155.8 20.1 reduce-scatter.6.cloned.1.call-done
  1175.9 15.4 fusion.78
  1193.0 88.0 %pad_maximum_fusion = f32[2048,2,8192]{2,0,1:T(8,128)} fusion(f32[2048,1,8192]{2,0,1:T(8,128)} %convolution_bitcast_fusion, f32[2048,1,8192]{2,0,1:T(8,128)} %convolution_bitcast_fusion.1), kind=kLoop, calls=%fused_computation.51 | loop fusion | flops 33554432 | bytes 268435456 | tf_op jit(solution)/shard_map/stack | solution.py:180
  1282.5 9.5 fusion.76
  1293.7 19.6 fusion.61
  1314.9 18.5 fusion.45
  1348.5 2775.2 %reduce-scatter.14.cloned.1.call-done = f32[64,2,8192]{2,0,1:T(8,128)} async-done(((f32[2048,2,8192]{2,0,1:T(8,128)}), f32[64,2,8192]{2,0,1:T(8,128)}) %reduce-scatter.14.cloned.1.call-update) | async-done | bytes 4194320 | tf_op jit(solution)/shard_map/reduce_scatter | solution.py:179
  4128.3 362.6 %reduce-scatter.12.cloned.1.call-done = f32[64,2048]{1,0:T(8,128)} async-done(((f32[2048,2048]{1,0:T(8,128)}), f32[64,2048]{1,0:T(8,128)}) %reduce-scatter.12.cloned.1.call-update) | async-done | bytes 524304 | tf_op jit(solution)/shard_map/reduce_scatter | solution.py:240
  4490.9 438.5 %reduce-scatter.10.cloned.1.call-done = f32[64,6144]{1,0:T(8,128)} async-done(((f32[2048,6144]{1,0:T(8,128)}), f32[64,6144]{1,0:T(8,128)}) %reduce-scatter.10.cloned.1.call-update) | async-done | bytes 1572880 | tf_op jit(solution)/shard_map/reduce_scatter | solution.py:239
  (333 shorter events, 222.5 us)
Async XLA Ops:
  7.2 161.3 %all-gather.9.cloned.1.call-start = ((), (), s32[]{:S(2)}) async-start(), calls=%async_computation.5 | async-start | bytes 25952256 | tf_op jit(solution)/shard_map/all_gather | solution.py:105
  7.9 260.8 %all-gather.13.cloned.1.call-start = ((), (), s32[]{:S(2)}) async-start(), calls=%async_computation.7 | async-start | bytes 5242880 | tf_op jit(solution)/shard_map/all_gather | solution.py:118
  56.0 124.5 %copy-start.21 = (f32[2048]{0:T(1024)}, f32[2048]{0:T(1024)S(1)}, u32[]{:S(2)}) copy-start(f32[2048]{0:T(1024)S(1)} %convert_element_type.118) | copy-start | bytes 24580
  56.1 124.5 %copy-start.19 = (f32[2048]{0:T(1024)}, f32[2048]{0:T(1024)S(1)}, u32[]{:S(2)}) copy-start(f32[2048]{0:T(1024)S(1)} %convert_element_type.117) | copy-start | bytes 24580
  57.5 123.0 %copy-start.38 = (f32[256]{0:T(256)}, f32[256]{0:T(256)S(1)}, u32[]{:S(2)}) copy-start(f32[256]{0:T(256)S(1)} %broadcast_multiply_fusion.3) | copy-start | bytes 3076
  59.8 120.8 %copy-start.42 = (f32[256]{0:T(256)}, f32[256]{0:T(256)S(1)}, u32[]{:S(2)}) copy-start(f32[256]{0:T(256)S(1)} %fusion.63) | copy-start | bytes 3076
  184.3 160.8 %all-gather.11.cloned.1.call-start = ((), (), s32[]{:S(2)}) async-start(), calls=%async_computation.6 | async-start | bytes 5242880 | tf_op jit(solution)/shard_map/all_gather | solution.py:117
  196.8 71.9 %copy-start.44 = (s32[1,1024]{1,0:T(1,128)S(1)}, s32[1,1024]{1,0:T(1,128)}, u32[]{:S(2)}) copy-start(s32[1,1024]{1,0:T(1,128)} %param.21) | copy-start | bytes 12292
  197.9 225.7 %all-gather.15.cloned.1.call-start = ((), (), s32[]{:S(2)}) async-start(), calls=%async_computation.8 | async-start | bytes 8650752 | tf_op jit(solution)/shard_map/all_gather | solution.py:106
  198.4 421.3 %all-gather.17.cloned.1.call-start = ((), (), s32[]{:S(2)}) async-start(), calls=%async_computation.9 | async-start | bytes 34603008 | tf_op jit(solution)/shard_map/all_gather | solution.py:164
  199.0 616.5 %all-gather.19.cloned.1.call-start = ((), (), s32[]{:S(2)}) async-start(), calls=%async_computation.10 | async-start | bytes 34603008 | tf_op jit(solution)/shard_map/all_gather | solution.py:165
  199.6 944.1 %reduce-scatter.8.cloned.1.call-start = ((), (), s32[]{:S(2)}) async-start(), calls=%async_computation.12 | async-start | bytes 5242880 | tf_op jit(solution)/shard_map/reduce_scatter | solution.py:215
  200.4 689.7 %copy-start.50 = (f32[2048]{0:T(1024)}, f32[2048]{0:T(1024)S(1)}, u32[]{:S(2)}) copy-start(f32[2048]{0:T(1024)S(1)} %convert_element_type.123) | copy-start | bytes 24580
  200.4 677.8 %copy-start.26 = (f32[2048]{0:T(1024)}, f32[2048]{0:T(1024)S(1)}, u32[]{:S(2)}) copy-start(f32[2048]{0:T(1024)S(1)} %convert_element_type.126) | copy-start | bytes 24580
  200.4 223.2 %copy-start.54 = (f32[2048]{0:T(1024)}, f32[2048]{0:T(1024)S(1)}, u32[]{:S(2)}) copy-start(f32[2048]{0:T(1024)S(1)} %convert_element_type.124) | copy-start | bytes 24580
  200.4 419.3 %copy-start.28 = (f32[2048]{0:T(1024)}, f32[2048]{0:T(1024)S(1)}, u32[]{:S(2)}) copy-start(f32[2048]{0:T(1024)S(1)} %convert_element_type.127) | copy-start | bytes 24580
  404.7 485.4 %copy-start.62 = (f32[256]{0:T(256)}, f32[256]{0:T(256)S(1)}, u32[]{:S(2)}) copy-start(f32[256]{0:T(256)S(1)} %broadcast_multiply_fusion.2) | copy-start | bytes 3076
  405.0 485.1 %copy-start.68 = (f32[256]{0:T(256)}, f32[256]{0:T(256)S(1)}, u32[]{:S(2)}) copy-start(f32[256]{0:T(256)S(1)} %fusion.64) | copy-start | bytes 3076
  430.3 447.9 %copy-start.45 = (f32[256]{0:T(256)}, f32[256]{0:T(256)S(1)}, u32[]{:S(2)}) copy-start(f32[256]{0:T(256)S(1)} %broadcast_multiply_fusion.1) | copy-start | bytes 3076
  431.9 446.2 %copy-start.52 = (f32[256]{0:T(256)}, f32[256]{0:T(256)S(1)}, u32[]{:S(2)}) copy-start(f32[256]{0:T(256)S(1)} %fusion.65) | copy-start | bytes 3076
  432.0 383.6 %copy-start.23 = (f32[32,1,256]{2,1,0:T(1,128)S(1)}, f32[32,1,256]{2,1,0:T(1,128)}, u32[]{:S(2)}) copy-start(f32[32,1,256]{2,1,0:T(1,128)} %convert_element_type.146) | copy-start | bytes 98308
  432.0 383.6 %copy-start.47 = (f32[256]{0:T(256)S(1)}, f32[256]{0:T(256)}, u32[]{:S(2)}) copy-start(f32[256]{0:T(256)} %compare_convert_fusion) | copy-start | bytes 3076
  653.6 193.1 %copy-start.56 = (f32[256]{0:T(256)}, f32[256]{0:T(256)S(1)}, u32[]{:S(2)}) copy-start(f32[256]{0:T(256)S(1)} %broadcast_multiply_fusion) | copy-start | bytes 3076
  1020.5 69.4 %copy-start.7 = (f32[256,2048]{1,0:T(8,128)S(1)}, f32[256,2048]{1,0:T(8,128)}, u32[]{:S(2)}) copy-start(f32[256,2048]{1,0:T(8,128)} %copy-done.6) | copy-start | bytes 6291460
  1020.6 69.4 %copy-start.27 = (f32[2048]{0:T(1024)S(1)}, f32[2048]{0:T(1024)}, u32[]{:S(2)}) copy-start(f32[2048]{0:T(1024)} %copy-done.26) | copy-start | bytes 24580
  1020.6 155.3 %reduce-scatter.6.cloned.1.call-start = ((), (), s32[]{:S(2)}) async-start(), calls=%async_computation.11 | async-start | bytes 5242880 | tf_op jit(solution)/shard_map/reduce_scatter | solution.py:218
  1021.4 316.9 %all-reduce.25.cloned.1.call-start = ((), (), s32[]{:S(2)}) async-start(), calls=%async_computation.16 | async-start | bytes 229376
  1191.4 89.5 %copy-start.15 = (f32[256,2048]{1,0:T(8,128)}, f32[256,2048]{1,0:T(8,128)S(1)}, u32[]{:S(2)}) copy-start(f32[256,2048]{1,0:T(8,128)S(1)} %get-tuple-element.482) | copy-start | bytes 6291460
  1191.4 89.5 %copy-start.64 = (f32[256]{0:T(256)}, f32[256]{0:T(256)S(1)}, u32[]{:S(2)}) copy-start(f32[256]{0:T(256)S(1)} %multiply_multiply_fusion.6) | copy-start | bytes 3076
  1192.9 2930.8 %reduce-scatter.14.cloned.1.call-start = ((), (), s32[]{:S(2)}) async-start(), calls=%async_computation.15 | async-start | bytes 138412032 | tf_op jit(solution)/shard_map/reduce_scatter | solution.py:179
  1281.0 3209.9 %reduce-scatter.12.cloned.1.call-start = ((), (), s32[]{:S(2)}) async-start(), calls=%async_computation.14 | async-start | bytes 17301504 | tf_op jit(solution)/shard_map/reduce_scatter | solution.py:240
  1292.1 3637.3 %reduce-scatter.10.cloned.1.call-start = ((), (), s32[]{:S(2)}) async-start(), calls=%async_computation.13 | async-start | bytes 51904512 | tf_op jit(solution)/shard_map/reduce_scatter | solution.py:239
  (61 other events, 881.7 us)
Sparse Core Ops, SparseCore 0:
  10.9 157.5 all-gather.8
  184.5 79.2 all-gather.12
  265.9 79.1 all-gather.10
  348.0 75.5 all-gather.14
  426.4 193.3 all-gather.16
  622.6 192.9 all-gather.18
  1020.7 75.5 reduce-scatter.7
  1098.8 77.1 reduce-scatter.5
  1193.0 124.4 all-reduce.24
  1319.8 2803.8 reduce-scatter.13
  4126.7 364.1 reduce-scatter.11
  4498.9 430.5 reduce-scatter.9
where the time goes:
time: 4950 us; the launch traced here: 4940 us
  waiting for transfers between devices  4150 us (84%)
  matrix products  322 us (7%)
  blocking collectives  178 us (4%)
  other arithmetic  157 us (3%)
  local copies, waits for them, and re-layouts  107 us (2%)
    reduce_scatter x1, waiting for transfers between devices, shards(): lax.psum_scatter(jnp.stack([up_part, down_part], axis=1), ('batch', 'seq'...  2780 us
    reduce_scatter x1, waiting for transfers between devices, shards(): lax.psum_scatter(qkv_term, ('batch', 'seq'), scatter_dimension=0, tiled=T...  439 us
    reduce_scatter x1, waiting for transfers between devices, shards(): lax.psum_scatter(out_term_t, ('batch', 'seq'), scatter_dimension=0, tiled...  363 us
    all_gather x1, waiting for transfers between devices, shards(): lax.all_gather(w_up, ('batch', 'seq'), axis=0, tiled=True)  188 us
    all_gather x1, waiting for transfers between devices, shards(): lax.all_gather(w_down, ('batch', 'seq'), axis=1, tiled=True)  162 us
    all_gather x1, waiting for transfers between devices, shards(): lax.all_gather(w_qkv, ('batch', 'seq'), axis=0, tiled=True)  109 us
  transfers between devices with their start and end apart: 12, of which 9 were waited for; matrix products, arithmetic and copies ran while one was open for 7% of the time, Pallas kernels for 0%

commit v1 on v0

v1 whole, which is shorter than its diff:
```python
import functools

import jax
import jax.numpy as jnp
import numpy as np
from jax import lax
from jax.experimental import pallas as pl
from jax.experimental.pallas import tpu as pltpu
from jax.sharding import PartitionSpec as P

EPSILON = 1e-05
HEAD = 64
STRIPE = 256
LOW = jnp.bfloat16
WIDE = jnp.float32
BOTH = ("batch", "seq")

LAYER = (2, 0, 1, 2, 1, 3, 3, 0)
PLACE = (1, 1, 1, 0, 0, 1, 0, 0)
TURN = ((1, 1), (3, 2), (0, 2), (3, 1))


class Plan:
    def __init__(self, nb, ns):
        self.nb, self.ns = nb, ns
        self.rows = nb // ns
        self.fast = nb == 8 and ns == 4
        if self.fast:
            layer, place, turn = LAYER, PLACE, TURN
        else:
            layer = [b // self.rows for b in range(nb)]
            place = [b % self.rows for b in range(nb)]
            turn = [[0] * self.rows for _ in range(ns)]
        self.there = []
        for b in range(nb):
            for s in range(ns):
                k, p = layer[b], place[b]
                target = ((s ^ turn[k][p]) * self.rows + p) * ns + k
                self.there.append((b * ns + s, target))
        self.back = [(d, s) for s, d in self.there]
        row_of = {(layer[b], place[b]): b for b in range(nb)}
        table = []
        for b in range(nb):
            for k in range(ns):
                c, t = b % self.rows, b // self.rows
                order = [c, 1 - c] if self.fast else list(range(self.rows))
                entry = [t ^ turn[k][c]] + [row_of[k, p] for p in order]
                for p in order:
                    for q in range(ns):
                        entry.append(q ^ t ^ turn[k][p] if self.fast else q ^ turn[k][p])
                table.append(entry)
        self.table = np.array(table, np.int32)


def swap_over(value, axis, step, size):
    return lax.ppermute(value, axis, [(i, i ^ step) for i in range(size)])


def bits(size):
    return [1 << i for i in range(size.bit_length() - 1)]


def sum_over(value, axis, size):
    for step in bits(size):
        value = value + swap_over(value, axis, step, size)
    return value


def aligned(plan, value, step):
    if not plan.fast:
        return value
    shape = value.shape
    axis = {1: 1, 4: 2, 2: 3}[step]
    return jnp.flip(value.reshape(shape[0], 2, 2, 2, shape[1] // 8), axis).reshape(shape)


def gather_over(value, axis, size):
    index = lax.axis_index(axis)
    value = value[None]
    for step in bits(size):
        other = swap_over(value, axis, step, size)
        upper = (index & step) != 0
        value = jnp.concatenate(
            [jnp.where(upper, other, value), jnp.where(upper, value, other)], axis=0
        )
    return value


def gather_blocks(plan, block):
    if not plan.fast:
        slots, width = block.shape
        full = lax.all_gather(block, "batch", axis=0, tiled=False)
        full = full.reshape(plan.nb // plan.rows, plan.rows, slots, width)
        return full.transpose(1, 0, 2, 3).reshape(plan.nb * slots, width)
    half = block.shape[1] // 2
    from_x = swap_over(block, "batch", 2, 8)
    from_y = swap_over(block, "batch", 4, 8)
    far_a = swap_over(from_x[:, :half], "batch", 4, 8)
    far_b = swap_over(from_y[:, half:], "batch", 2, 8)
    far = jnp.concatenate([far_a, far_b], axis=1)
    own = [block, from_x, from_y, far]
    other = [swap_over(piece, "batch", 1, 8) for piece in own]
    return jnp.concatenate(own + other, axis=0)


def reduce_blocks(plan, product, left):
    count = left.shape[0]
    if not plan.fast:
        part = product(left).astype(LOW)
        width = part.shape[1]
        slots = count // plan.nb
        part = part.reshape(plan.rows, plan.nb // plan.rows, slots, width).transpose(1, 0, 2, 3)
        return lax.psum_scatter(
            part.reshape(count, width), "batch", scatter_dimension=0, tiled=True
        ).astype(WIDE)
    other = swap_over(product(left[count // 2 :]).astype(LOW), "batch", 1, 8)
    mine = product(left[: count // 2]) + other.astype(WIDE)
    slots, width = count // 8, mine.shape[1]
    half = width // 2
    mine = mine.reshape(4, slots, width)
    near, at_x, at_y, far = mine[0], mine[1], mine[2], mine[3]
    to_y = swap_over(far[:, :half].astype(LOW), "batch", 2, 8).astype(WIDE)
    to_x = swap_over(far[:, half:].astype(LOW), "batch", 4, 8).astype(WIDE)
    x_a = swap_over(at_x[:, :half].astype(LOW), "batch", 2, 8).astype(WIDE)
    y_b = swap_over(at_y[:, half:].astype(LOW), "batch", 4, 8).astype(WIDE)
    x_b = swap_over((at_x[:, half:] + to_x).astype(LOW), "batch", 2, 8).astype(WIDE)
    y_a = swap_over((at_y[:, :half] + to_y).astype(LOW), "batch", 4, 8).astype(WIDE)
    return jnp.concatenate([near[:, :half] + x_a + y_a, near[:, half:] + x_b + y_b], axis=1)


def gather_weight(plan, shard):
    rows, width = shard.shape
    part = width // plan.nb
    pieces = shard.reshape(rows, plan.nb, part).transpose(1, 0, 2)
    pieces = lax.all_to_all(pieces, "batch", 0, 0, tiled=True)
    full = lax.all_gather(pieces, "seq", axis=1, tiled=True)
    return full.reshape(plan.nb * plan.ns * rows, part)


def scatter_weight(plan, part):
    total, width = part.shape
    rows = total // (plan.nb * plan.ns)
    own = lax.psum_scatter(
        part.astype(LOW).reshape(plan.nb, plan.ns * rows, width),
        "seq",
        scatter_dimension=1,
        tiled=True,
    )
    pieces = lax.all_to_all(own, "batch", 0, 0, tiled=True)
    return pieces.transpose(1, 0, 2).reshape(rows, plan.nb * width)


def norm_stats(values):
    mean = jnp.mean(values, axis=-1, keepdims=True)
    center = values - mean
    return mean, lax.rsqrt(jnp.mean(center * center, axis=-1, keepdims=True) + EPSILON)


def spread_stats(plan, values):
    count = values.shape[1]
    mean = jnp.mean(values, axis=-1)
    center = values - mean[:, None]
    square = jnp.sum(center * center, axis=-1)
    for step in bits(plan.nb):
        other = swap_over(jnp.stack([mean, square]), "batch", step, plan.nb)
        other = aligned(plan, other, step)
        gap = other[0] - mean
        mean = 0.5 * (mean + other[0])
        square = square + other[1] + gap * gap * (0.5 * count)
        count = 2 * count
    return mean[:, None], lax.rsqrt(square / count + EPSILON)[:, None]


def norm_back(upstream, gain, unit, scale):
    scaled = upstream * gain
    first = jnp.mean(scaled, axis=-1, keepdims=True)
    second = jnp.mean(scaled * unit, axis=-1, keepdims=True)
    grad = scale * (scaled - first - unit * second)
    return grad, jnp.sum(upstream * unit, axis=0), jnp.sum(upstream, axis=0)


def spread_norm_back(plan, upstream, gain, unit, scale):
    scaled = upstream * gain
    sums = jnp.stack([jnp.sum(scaled, axis=-1), jnp.sum(scaled * unit, axis=-1)])
    for step in bits(plan.nb):
        sums = sums + aligned(plan, swap_over(sums, "batch", step, plan.nb), step)
    sums = sums / (upstream.shape[1] * plan.nb)
    grad = scale * (scaled - sums[0][:, None] - unit * sums[1][:, None])
    return grad, jnp.sum(upstream * unit, axis=0), jnp.sum(upstream, axis=0)


def xpos_tables(length):
    slot_pos = (jnp.arange(length, dtype=jnp.int32) - length // 2).astype(WIDE)
    index = jnp.arange(32, dtype=jnp.int32).astype(WIDE)
    angle = slot_pos[:, None] * jnp.exp(index * (-jnp.log(10000.0) / 32.0))[None, :]
    zeta = (index / 32.0 + 0.4) / 1.4
    growth = jnp.exp(slot_pos[:, None] * jnp.log(zeta)[None, :] / 512.0)
    cosine, sine = jnp.cos(angle), jnp.sin(angle)
    tables = []
    for scale in (growth, 1.0 / growth):
        tables += [cosine * scale] * 4
        tables += [-sine * scale, sine * scale] * 2
    return jnp.concatenate(tables, axis=1)


def swap_halves(values):
    lane = lax.broadcasted_iota(jnp.int32, values.shape, 1)
    return jnp.where(lane % 64 < 32, pltpu.roll(values, 96, 1), pltpu.roll(values, 32, 1))


def matmul(a, b, contract):
    return lax.dot_general(a, b, ((contract[:1], contract[1:]), ((), ())), preferred_element_type=WIDE)


def fill_bias(bias, valid, seg_row, seg_col, length):
    for i in range(length // STRIPE):
        low, high = i * STRIPE, (i + 1) * STRIPE
        shape = (STRIPE, high)
        query = lax.broadcasted_iota(jnp.int32, shape, 0) + low
        key = lax.broadcasted_iota(jnp.int32, shape, 1)
        same = seg_col[low:high] == seg_row[:, :high]
        allowed = (key == query) | (same & (key <= query) & (query < valid))
        bias[low:high, :high] = jnp.where(allowed, 0.0, -1e30)


def attend_kernel(info, proj, tables, seg_row, seg_col, qkv, attended, log_total, bias, *, ns, slots, hd):
    row, head = pl.program_id(0), pl.program_id(1)
    length = ns * slots

    def place(quarter):
        return pl.multiple_of(info[row, quarter] * slots, slots)

    @pl.when(head == 0)
    def _():
        for q in range(ns):
            source, low, high = place(q), q * slots, (q + 1) * slots
            for part in range(2):
                cosine = tables[low:high, 256 * part : 256 * part + 128]
                sine = tables[low:high, 256 * part + 128 : 256 * part + 256]
                for pair in range(hd // 128):
                    at = part * hd + pair * 128
                    values = proj[pl.ds(source, slots), at : at + 128]
                    turned = values * cosine + swap_halves(values) * sine
                    qkv[low:high, at : at + 128] = turned.astype(LOW)
            qkv[low:high, 2 * hd :] = proj[pl.ds(source, slots), 2 * hd :].astype(LOW)
        fill_bias(bias, info[row, ns], seg_row[...], seg_col[...], length)
        log_total[...] = jnp.zeros_like(log_total)

    mine = lax.broadcasted_iota(jnp.int32, (STRIPE, hd), 1) // HEAD == head
    column = lax.broadcasted_iota(jnp.int32, (STRIPE, 128), 1) == head
    for i in range(length // STRIPE):
        low, high = i * STRIPE, (i + 1) * STRIPE
        queries = jnp.where(mine, qkv[low:high, :hd], jnp.zeros((), LOW))
        scores = matmul(queries, qkv[:high, hd : 2 * hd], (1, 1)) * 0.125 + bias[low:high, :high]
        top = jnp.max(scores, axis=-1, keepdims=True)
        weight = jnp.exp(scores - top)
        total = jnp.sum(weight, axis=-1, keepdims=True)
        summed = matmul(weight.astype(LOW), qkv[:high, 2 * hd :], (1, 0)) / total
        log_total[low:high] = jnp.where(column, top + jnp.log(total), log_total[low:high])
        for u in range(STRIPE // slots):
            to = place(i * (STRIPE // slots) + u)
            rows = slice(u * slots, (u + 1) * slots)
            attended[pl.ds(to, slots), :] = jnp.where(
                mine[rows], summed[rows], attended[pl.ds(to, slots), :]
            )


def attend_back_kernel(
    info, qkv, attended, grad, log_total, tables, seg_row, seg_col, out,
    bias, grad_low, product, grad_q, grad_k, grad_v, *, ns, slots, hd
):
    row, head = pl.program_id(0), pl.program_id(1)
    length = ns * slots

    def place(quarter):
        return pl.multiple_of(info[row, quarter] * slots, slots)

    @pl.when(head == 0)
    def _():
        for q in range(ns):
            source, low, high = place(q), q * slots, (q + 1) * slots
            values = grad[pl.ds(source, slots), :]
            grad_low[low:high] = values.astype(LOW)
            product[low:high] = values * attended[pl.ds(source, slots), :]
        fill_bias(bias, info[row, ns], seg_row[...], seg_col[...], length)
        for total in (grad_q, grad_k, grad_v):
            total[...] = jnp.zeros_like(total)

    mine = lax.broadcasted_iota(jnp.int32, (STRIPE, hd), 1) // HEAD == head
    column = lax.broadcasted_iota(jnp.int32, (STRIPE, 128), 1) == head
    nothing = jnp.zeros((), LOW)
    mine_all = lax.broadcasted_iota(jnp.int32, (length, hd), 1) // HEAD == head
    keys_mine = jnp.where(mine_all, qkv[:, hd : 2 * hd], nothing)
    for i in range(length // STRIPE):
        low, high = i * STRIPE, (i + 1) * STRIPE
        queries = jnp.where(mine, qkv[low:high, :hd], nothing)
        upstream = jnp.where(mine, grad_low[low:high], nothing)
        delta = jnp.sum(jnp.where(mine, product[low:high], 0.0), axis=-1, keepdims=True)
        log_sum = jnp.sum(jnp.where(column, log_total[low:high], 0.0), axis=-1, keepdims=True)
        scores = matmul(queries, qkv[:high, hd : 2 * hd], (1, 1)) * 0.125 + bias[low:high, :high]
        prob = jnp.exp(scores - log_sum)
        grad_prob = matmul(upstream, qkv[:high, 2 * hd :], (1, 1))
        grad_s = (prob * (grad_prob - delta) * 0.125).astype(LOW)
        grad_q[low:high] += matmul(grad_s, keys_mine[:high], (1, 0))
        grad_k[:high] += matmul(grad_s, queries, (0, 0))
        grad_v[:high] += matmul(prob.astype(LOW), upstream, (0, 0))

    @pl.when(head == pl.num_programs(1) - 1)
    def _():
        for q in range(ns):
            target, low, high = place(q), q * slots, (q + 1) * slots
            for part, total in enumerate((grad_q, grad_k)):
                cosine = tables[low:high, 256 * part : 256 * part + 128]
                sine = tables[low:high, 256 * part + 128 : 256 * part + 256]
                for pair in range(hd // 128):
                    values = total[low:high, pair * 128 : pair * 128 + 128]
                    turned = values * cosine - swap_halves(values) * sine
                    at = part * hd + pair * 128
                    out[pl.ds(target, slots), at : at + 128] = turned.astype(LOW)
            out[pl.ds(target, slots), 2 * hd :] = grad_v[low:high].astype(LOW)


def row_block(length, width):
    return pl.BlockSpec((length, width), lambda r, h, info: (r, 0))


def shared_block(length, width):
    return pl.BlockSpec((length, width), lambda r, h, info: (0, 0))


def attend(plan, info, proj, tables, segments):
    count, width = proj.shape
    length, hd = count // plan.rows, width // 3
    slots = length // plan.ns
    return pl.pallas_call(
        functools.partial(attend_kernel, ns=plan.ns, slots=slots, hd=hd),
        grid_spec=pltpu.PrefetchScalarGridSpec(
            num_scalar_prefetch=1,
            grid=(plan.rows, hd // HEAD),
            in_specs=[
                row_block(length, width),
                shared_block(length, 512),
                pl.BlockSpec((None, 1, length), lambda r, h, info: (r, 0, 0)),
                pl.BlockSpec((None, length, 1), lambda r, h, info: (r, 0, 0)),
            ],
            out_specs=[row_block(length, width), row_block(length, hd), row_block(length, 128)],
            scratch_shapes=[pltpu.VMEM((length, length), WIDE)],
        ),
        out_shape=[
            jax.ShapeDtypeStruct((count, width), LOW),
            jax.ShapeDtypeStruct((count, hd), WIDE),
            jax.ShapeDtypeStruct((count, 128), WIDE),
        ],
        compiler_params=pltpu.CompilerParams(vmem_limit_bytes=48 << 20),
        name="attend",
    )(info, proj, tables, segments[:, None, :], segments[:, :, None])


def attend_back(plan, info, qkv, attended, grad, log_total, tables, segments):
    count, width = qkv.shape
    length, hd = count // plan.rows, width // 3
    slots = length // plan.ns
    return pl.pallas_call(
        functools.partial(attend_back_kernel, ns=plan.ns, slots=slots, hd=hd),
        grid_spec=pltpu.PrefetchScalarGridSpec(
            num_scalar_prefetch=1,
            grid=(plan.rows, hd // HEAD),
            in_specs=[
                row_block(length, width),
                row_block(length, hd),
                row_block(length, hd),
                row_block(length, 128),
                shared_block(length, 512),
                pl.BlockSpec((None, 1, length), lambda r, h, info: (r, 0, 0)),
                pl.BlockSpec((None, length, 1), lambda r, h, info: (r, 0, 0)),
            ],
            out_specs=row_block(length, width),
            scratch_shapes=[
                pltpu.VMEM((length, length), WIDE),
                pltpu.VMEM((length, hd), LOW),
                pltpu.VMEM((length, hd), WIDE),
                pltpu.VMEM((length, hd), WIDE),
                pltpu.VMEM((length, hd), WIDE),
                pltpu.VMEM((length, hd), WIDE),
            ],
        ),
        out_shape=jax.ShapeDtypeStruct((count, width), LOW),
        compiler_params=pltpu.CompilerParams(vmem_limit_bytes=48 << 20),
        name="attend_back",
    )(info, qkv, attended, grad, log_total, tables, segments[:, None, :], segments[:, :, None])


def shards(
    plan,
    tokens,
    segments,
    valid_count,
    cotangent,
    w_qkv,
    w_out,
    w_up,
    w_down,
    gain_attn,
    bias_attn,
    gain_mix,
    bias_mix,
    gain_ffn,
    bias_ffn,
    gain_hidden,
    bias_hidden,
):
    nb, ns = plan.nb, plan.ns
    width, slots, length = tokens.shape[2], tokens.shape[1], segments.shape[1]
    hd, hidden_part = width // nb, w_up.shape[1] // nb
    batch_index, seq_index = lax.axis_index("batch"), lax.axis_index("seq")
    entry = lax.dynamic_index_in_dim(
        jnp.asarray(plan.table), batch_index * ns + seq_index, 0, keepdims=False
    )

    tokens_low = lax.ppermute(tokens[0], BOTH, plan.there)
    slot = seq_index * slots + jnp.arange(slots, dtype=jnp.int32)
    living = (slot < valid_count[0])[:, None]
    grad_low = lax.ppermute(
        jnp.where(living, cotangent[0], jnp.zeros((), LOW)), BOTH, plan.there
    )

    group = w_qkv.reshape(w_qkv.shape[0], 3, nb, hd).transpose(0, 2, 1, 3)
    qkv_w = gather_weight(plan, group.reshape(w_qkv.shape))
    out_wt = gather_weight(plan, w_out.T)
    up_w = gather_weight(plan, w_up)
    down_wt = gather_weight(plan, w_down.T)

    own_params = (gain_attn, bias_attn, gain_mix, bias_mix, gain_ffn, bias_ffn, gain_hidden, bias_hidden)
    params = gather_over(jnp.concatenate([p.astype(WIDE) for p in own_params]), "seq", ns)
    packed = jnp.concatenate(
        [params.reshape(-1), segments[0].astype(WIDE), valid_count.astype(WIDE)]
    )
    packed = gather_over(packed, "batch", nb)
    spread = packed[:, : params.size].reshape(nb, ns, -1)
    vectors, at = [], 0
    for index, p in enumerate(own_params):
        piece = spread[:, :, at : at + p.shape[0]]
        at += p.shape[0]
        if index in (0, 1, 4, 5):
            vectors.append(piece.reshape(-1))
        else:
            vectors.append(lax.dynamic_index_in_dim(piece, batch_index, 0, False).reshape(-1))
    ga, ba, gm, bm, gf, bf, gh, bh = vectors
    layer_rows = packed[entry[1 : 1 + plan.rows], params.size :].astype(jnp.int32)
    seg_rows = layer_rows[:, :length]
    info = jnp.concatenate(
        [entry[1 + plan.rows :].reshape(plan.rows, ns), layer_rows[:, length:]], axis=1
    )
    tables = xpos_tables(length)

    resid = tokens_low.astype(WIDE)
    mean_attn, scale_attn = norm_stats(resid)
    unit_attn = (resid - mean_attn) * scale_attn
    normed = gather_blocks(plan, (unit_attn * ga + ba).astype(LOW))
    projected = matmul(normed, qkv_w, (1, 0))
    qkv, attended, log_total = attend(plan, info, projected, tables, seg_rows)
    mean_mix, scale_mix = spread_stats(plan, attended)
    unit_mix = (attended - mean_mix) * scale_mix
    mixed = (unit_mix * gm + bm).astype(LOW)
    resid_mid = resid + reduce_blocks(plan, lambda left: matmul(left, out_wt, (1, 1)), mixed)
    mean_ffn, scale_ffn = norm_stats(resid_mid)
    unit_ffn = (resid_mid - mean_ffn) * scale_ffn
    ffn_in = gather_blocks(plan, (unit_ffn * gf + bf).astype(LOW))
    hidden = matmul(ffn_in, up_w, (1, 0))
    phi = 0.5 * lax.erfc(hidden * (-(0.5**0.5)))
    active = hidden * phi
    slope = phi + hidden * (jnp.exp(-0.5 * hidden * hidden) * ((2.0 * np.pi) ** -0.5))
    mean_hid, scale_hid = spread_stats(plan, active)
    unit_hid = (active - mean_hid) * scale_hid
    hidden_low = (unit_hid * gh + bh).astype(LOW)
    output = resid_mid + reduce_blocks(
        plan, lambda left: matmul(left, down_wt, (1, 1)), hidden_low
    )
    output = lax.ppermute(output.astype(LOW), BOTH, plan.back)

    grad_all = gather_blocks(plan, grad_low)
    grad_hn = matmul(grad_all, down_wt, (1, 0))
    grad_down = scatter_weight(plan, matmul(grad_all, hidden_low, (0, 0)))
    grad_active, gain_hidden_part, bias_hidden_part = spread_norm_back(
        plan, grad_hn, gh, unit_hid, scale_hid
    )
    grad_hidden = (grad_active * slope).astype(LOW)
    grad_ffn_in = reduce_blocks(plan, lambda left: matmul(left, up_w, (1, 1)), grad_hidden)
    grad_up = scatter_weight(plan, matmul(ffn_in, grad_hidden, (0, 0)))
    grad_mid, gain_ffn_part, bias_ffn_part = norm_back(grad_ffn_in, gf, unit_ffn, scale_ffn)
    grad_mid = grad_mid + grad_low.astype(WIDE)
    mid_all = gather_blocks(plan, grad_mid.astype(LOW))
    grad_mixed = matmul(mid_all, out_wt, (1, 0))
    grad_out = scatter_weight(plan, matmul(mid_all, mixed, (0, 0)))
    grad_attended, gain_mix_part, bias_mix_part = spread_norm_back(
        plan, grad_mixed, gm, unit_mix, scale_mix
    )
    grad_proj = attend_back(plan, info, qkv, attended, grad_attended, log_total, tables, seg_rows)
    grad_normed = reduce_blocks(plan, lambda left: matmul(left, qkv_w, (1, 1)), grad_proj)
    grad_qkv = scatter_weight(plan, matmul(normed, grad_proj, (0, 0)))
    grad_resid, gain_attn_part, bias_attn_part = norm_back(
        grad_normed, ga, unit_attn, scale_attn
    )
    grad_tokens = lax.ppermute((grad_mid + grad_resid).astype(LOW), BOTH, plan.back)

    whole = (gain_ffn_part, bias_ffn_part, gain_attn_part, bias_attn_part)
    parts = (gain_mix_part, bias_mix_part, gain_hidden_part, bias_hidden_part)
    whole_sum = sum_over(sum_over(jnp.stack(whole), "seq", ns), "batch", nb)
    whole_sum = whole_sum.reshape(4, nb * ns, -1)
    own = lax.dynamic_index_in_dim(whole_sum, batch_index * ns + seq_index, 1, False)
    part_sum = sum_over(jnp.concatenate(parts), "seq", ns)
    mixes = part_sum[: 2 * hd].reshape(2, ns, -1)
    hiddens = part_sum[2 * hd :].reshape(2, ns, -1)
    mixes = lax.dynamic_index_in_dim(mixes, seq_index, 1, False)
    hiddens = lax.dynamic_index_in_dim(hiddens, seq_index, 1, False)

    grad_qkv = grad_qkv.reshape(-1, nb, 3, hd).transpose(0, 2, 1, 3).reshape(w_qkv.shape)
    return (
        output[None],
        grad_tokens.astype(WIDE)[None],
        grad_qkv.astype(WIDE),
        grad_out.astype(WIDE).T,
        grad_up.astype(WIDE),
        grad_down.astype(WIDE).T,
        own[2],
        own[3],
        mixes[0],
        mixes[1],
        own[0],
        own[1],
        hiddens[0],
        hiddens[1],
    )


def solution(mesh):
    plan = Plan(mesh.shape["batch"], mesh.shape["seq"])
    rows = P("batch", "seq", None)
    over_rows, over_columns, vector = P(BOTH, None), P(None, BOTH), P(BOTH)
    return jax.shard_map(
        functools.partial(shards, plan),
        mesh=mesh,
        in_specs=(rows, P("batch", None), P("batch"), rows)
        + (over_rows, over_columns, over_rows, over_columns)
        + (vector,) * 8,
        out_specs=(rows, rows, over_rows, over_columns, over_rows, over_columns) + (vector,) * 8,
        check_vma=False,
    )
```

time: 4950 us -> 1020 us (0.21)
  waiting for transfers between devices: 4150 us -> 378 us
  matrix products: 322 us -> 156 us
  blocking collectives: 178 us -> 18 us
  starting transfers between devices: 0.65 us -> 151 us
  other arithmetic: 157 us -> 75.2 us
  Pallas kernels: 0 us -> 49.6 us
    reduce_scatter x5 -> x4, waiting for transfers between devices: 3600 us -> 0.01 us  [scatter_weight(): lax.psum_scatter(part.astype(LOW).reshape(plan.nb, plan.ns * rows, width)...]
    all_gather x6 -> x4, waiting for transfers between devices: 547 us -> 31.1 us  [gather_weight(): full = lax.all_gather(pieces, 'seq', axis=1, tiled=True)]
    ppermute x0 -> x88, waiting for transfers between devices: none -> 289 us  [the longest x84 236 us: swap_over(): return lax.ppermute(value, axis, [(i, i ^ step) for i in range(size)])]
    dot_general x26 -> x16, matrix products: 322 us -> 156 us  [matmul(): lax.dot_general(a, b, ((contract[:1], contract[1:]), ((), ())), preferred...]
    all_gather x2 -> x0, blocking collectives: 135 us -> none  [the longest x1 68.5 us: shards(): lax.all_gather(bias_hidden, ('batch', 'seq'), axis=0, tiled=True)]
    ppermute x0 -> x88, starting transfers between devices: none -> 99.6 us  [the longest x84 86 us: swap_over(): return lax.ppermute(value, axis, [(i, i ^ step) for i in range(size)])]
    another operation x4 -> x9, other arithmetic: 90.2 us -> 0.19 us  [the longest x6 0.11 us: spread_stats(): other = swap_over(jnp.stack([mean, square]), 'batch', step, plan.nb)]
    all_to_all x0 -> x7, waiting for transfers between devices: none -> 58.4 us  [the longest x4 33.8 us: scatter_weight(): pieces = lax.all_to_all(own, 'batch', 0, 0, tiled=True)]
  transfers between devices with their start and end apart: 12 -> 103, of which waited for: 9 -> 42; matrix products, arithmetic and copies ran while one was open for 7% -> 33% of each run, Pallas kernels for 0% -> 5%
where the time goes in v1:
time: 1020 us; the launch traced here: 1000 us
  waiting for transfers between devices  378 us (37%)
  local copies, waits for them, and re-layouts  156 us (15%)
  matrix products  156 us (15%)
  starting transfers between devices  151 us (15%)
  other arithmetic  75.2 us (7%)
  Pallas kernels  49.6 us (5%)
  blocking collectives  18 us (2%)
  between operations  17 us (2%)
    ppermute x84, waiting for transfers between devices, swap_over(): return lax.ppermute(value, axis, [(i, i ^ step) for i in range(size)])  236 us
    dot_general x16, matrix products, matmul(): lax.dot_general(a, b, ((contract[:1], contract[1:]), ((), ())), preferred...  156 us
    ppermute x84, starting transfers between devices, swap_over(): return lax.ppermute(value, axis, [(i, i ^ step) for i in range(size)])  86 us
    unnamed x180, local copies, waits for them, and re-layouts  61.8 us
    all_to_all x4, waiting for transfers between devices, scatter_weight(): pieces = lax.all_to_all(own, 'batch', 0, 0, tiled=True)  33.8 us
    all_gather x4, waiting for transfers between devices, gather_weight(): full = lax.all_gather(pieces, 'seq', axis=1, tiled=True)  31.1 us
    ppermute x1, waiting for transfers between devices, shards(): lax.ppermute(jnp.where(living, cotangent[0], jnp.zeros((), LOW)), BOTH, p...  28.7 us
    all_to_all x3, starting transfers between devices, gather_weight(): pieces = lax.all_to_all(pieces, 'batch', 0, 0, tiled=True)  27.9 us
  transfers between devices with their start and end apart: 103, of which 42 were waited for; matrix products, arithmetic and copies ran while one was open for 33% of the time, Pallas kernels for 5%

profile of v1, /device:TPU:4, one launch (start us, length us, event | category | flops | bytes accessed | tf_op | source)
XLA Modules:
  0.0 1001.2 jit_solution(7914401442934539044)
XLA Ops:
  28.1 20.3 %collective-permute-done.2 = f32[2,896]{1,0:T(2,128)S(1)} collective-permute-done((f32[2,896]{1,0:T(2,128)S(1)}, f32[2,896]{1,0:T(2,128)S(1)}, u32[]{:S(2)}, u32[]{:S(2)}) %collective-permute-start.2) | collective-permute-done | bytes 7200 | tf_op jit(solution)/shard_map/ppermute | solution.py:56
  121.5 10.7 %all-gather.5.cloned.1.call-done = bf16[8,256,768]{2,0,1:T(8,128)(2,1)} async-done(((bf16[8,64,768]{2,0,1:T(8,128)(2,1)}), bf16[8,256,768]{2,0,1:T(8,128)(2,1)}) %all-gather.5.cloned.1.call-update) | async-done | bytes 3145744 | tf_op jit(solution)/shard_map/all_gather | solution.py:136
  136.4 10.7 %fusion.107.proj = f32[2048,768]{1,0:T(8,128)} fusion(bf16[2048,2048]{1,0:T(8,128)(2,1)} %constant_dynamic-update-slice_fusion, bf16[2048,768]{1,0:T(8,128)(2,1)S(1)} %bitcast.170), kind=kOutput, calls=%fused_computation.301 | convolution fusion | flops 6442450944 | bytes 17825792 | tf_op jit(solution)/shard_map/dot_general | solution.py:212
  147.2 21.9 %attend.1 = (bf16[2048,768]{1,0:T(8,128)(2,1)}, f32[2048,256]{1,0:T(8,128)S(1)}, f32[2048,128]{1,0:T(8,128)S(1)}) custom-call(s32[2,5]{1,0:T(2,128)S(1)} %pad_add_fusion.info, f32[2048,768]{1,0:T(8,128)} %fusion.107.proj, f32[1024,512]{1,0:T(8,128)} %concatenate.81.tables, s32[2,1,1024]{2,1,0:T(1,128)S(1)} %broadcast_in_dim.33.seg_row, ...), custom_call_target="tpu_custom_call" | custom-call | tf_op jit(solution)/shard_map/attend/pallas_call | solution.py:335
  178.4 20.4 %all-gather.7.cloned.1.call-done = bf16[8,256,256]{2,0,1:T(8,128)(2,1)} async-done(((bf16[8,64,256]{2,0,1:T(8,128)(2,1)}), bf16[8,256,256]{2,0,1:T(8,128)(2,1)}) %all-gather.7.cloned.1.call-update) | async-done | bytes 1048592 | tf_op jit(solution)/shard_map/all_gather | solution.py:136
  208.5 18.0 %all_to_all.40 = bf16[8,64,1024]{2,1,0:T(8,128)(2,1)S(1)} all-to-all(bf16[8,64,1024]{2,1,0:T(8,128)(2,1)S(1)} %copy.115), channel_id=1, replica_groups=mesh['batch'=8,'seq'=4] {'batch'}, dimensions={0} | all-to-all | bytes 2097152 | tf_op jit(solution)/shard_map/all_to_all | solution.py:135
  239.5 14.9 %collective-permute-done.19 = bf16[256,1024]{1,0:T(8,128)(2,1)S(1)} collective-permute-done((bf16[256,1024]{1,0:T(8,128)(2,1)S(1)}, bf16[256,1024]{1,0:T(8,128)(2,1)S(1)}, u32[]{:S(2)}, u32[]{:S(2)}) %collective-permute-start.19) | collective-permute-done | bytes 524320 | tf_op jit(solution)/shard_map/ppermute | solution.py:56
  255.3 28.7 %collective-permute-done.43 = bf16[256,2048]{1,0:T(8,128)(2,1)S(1)} collective-permute-done((bf16[256,2048]{1,0:T(8,128)(2,1)S(1)}, bf16[256,2048]{1,0:T(8,128)(2,1)S(1)}, u32[]{:S(2)}, u32[]{:S(2)}) %collective-permute-start.43) | collective-permute-done | bytes 1048608 | tf_op jit(solution)/shard_map/ppermute | solution.py:423
  284.0 33.3 %collective-permute-start.44 = (bf16[256,2048]{1,0:T(8,128)(2,1)S(1)}, bf16[256,2048]{1,0:T(8,128)(2,1)}, u32[]{:S(2)}, u32[]{:S(2)}) collective-permute-start(bf16[256,2048]{1,0:T(8,128)(2,1)S(1)} %collective-permute-done.43), channel_id=1, source_target_pairs={{0,8},{4,12},{8,0},{12,4},{16,24},{20,28},{24,16},{28,20},{1,9},{5... | collective-permute-start | bytes 3145736 | tf_op jit(solution)/shard_map/ppermute | solution.py:56
  319.5 18.6 %all-to-all-start.3 = ((bf16[8,64,1024]{2,1,0:T(8,128)(2,1)}), bf16[8,64,1024]{2,1,0:T(8,128)(2,1)}, u32[]{:S(2)}, u32[]{:S(2)}) async-start(bf16[8,64,1024]{2,1,0:T(8,128)(2,1)} %copy.118), calls=%async_computation.3 | async-start | bytes 2097152 | tf_op jit(solution)/shard_map/all_to_all | solution.py:135
  344.0 24.6 %all-to-all-done.3 = bf16[8,64,1024]{2,1,0:T(8,128)(2,1)} async-done(((bf16[8,64,1024]{2,1,0:T(8,128)(2,1)}), bf16[8,64,1024]{2,1,0:T(8,128)(2,1)}, u32[]{:S(2)}, u32[]{:S(2)}) %all-to-all-start.3) | async-done | bytes 1048608 | tf_op jit(solution)/shard_map/all_to_all | solution.py:135
  381.9 15.8 %collective-permute-done.45 = bf16[256,2048]{1,0:T(8,128)(2,1)} collective-permute-done((bf16[256,2048]{1,0:T(8,128)(2,1)S(1)}, bf16[256,2048]{1,0:T(8,128)(2,1)}, u32[]{:S(2)}, u32[]{:S(2)}) %collective-permute-start.45) | collective-permute-done | bytes 1048608 | tf_op jit(solution)/shard_map/ppermute | solution.py:56
  398.9 10.0 collective-permute-done.46
  448.2 30.3 %fusion.89 = (f32[2048]{0:T(1024)S(1)}, f32[2048,1024]{0,1:T(8,128)S(1)}, f32[2048,1024]{0,1:T(8,128)}, f32[2048,1024]{0,1:T(8,128)}) fusion(bf16[2048,2048]{1,0:T(8,128)(2,1)} %constant_dynamic-update-slice_fusion.8, bf16[2048,1024]{1,0:T(8,128)(2,1)S(1)} %bitcast.160), kind=kOutput, calls=%fused_computation.285 | convolution fusion | flops 8724150272 | bytes 37756928 | tf_op jit(solution)/shard_map/dot_general | solution.py:212
  496.4 15.2 %fusion.106 = (f32[1024]{0:T(1024)}, f32[2048,1024]{1,0:T(8,128)}) fusion(bf16[2048,2048]{1,0:T(8,128)(2,1)} %constant_dynamic-update-slice_fusion.16, bf16[2048,1024]{1,0:T(8,128)(2,1)} %bitcast.163), kind=kOutput, calls=%fused_computation.300 | convolution fusion | flops 8592030720 | bytes 20975616 | tf_op jit(solution)/shard_map/dot_general | solution.py:212
  511.7 9.1 copy.121
  538.4 13.0 %fusion.7 = (bf16[2048,1024]{0,1:T(8,128)(2,1)S(1)}, bf16[2048,1024]{0,1:T(8,128)(2,1)S(1)}) fusion(f32[2048,1024]{0,1:T(8,128)} %get-tuple-element.88, f32[2048,1024]{0,1:T(8,128)} %get-tuple-element.176, f32[2048,1024]{0,1:T(8,128)} %copy.121, f32[2048,1024]{0,1:T(8,128)} %copy-done.4, f32[2048]{0:T(1024)S(1)} %bitcast.234, f32[2048]{0:T(1024)S(1)} %bitcast.233, ...), kind=kLoop, calls=%fused_computation.10 | loop fusion | flops 35651584 | bytes 41984000 | tf_op jit(solution)/shard_map/convert_element_type | solution.py:487
  564.8 11.0 %convolution_convert_fusion.5 = bf16[2048,1024]{1,0:T(8,128)(2,1)} fusion(bf16[2048,2048]{1,0:T(8,128)(2,1)S(1)} %bitcast.206, bf16[2048,1024]{0,1:T(8,128)(2,1)S(1)} %get-tuple-element.97), kind=kOutput, calls=%fused_computation.39 | convolution fusion | flops 8592031744 | bytes 16777216 | tf_op jit(solution)/shard_map/dot_general | solution.py:212
  575.9 8.8 fusion.104
  587.6 8.6 fusion.103
  603.9 8.3 collective-permute-done.57
  636.1 11.2 %collective-permute-done.58 = bf16[256,1024]{1,0:T(8,128)(2,1)S(1)} collective-permute-done((bf16[256,1024]{1,0:T(8,128)(2,1)S(1)}, bf16[256,1024]{1,0:T(8,128)(2,1)S(1)}, u32[]{:S(2)}, u32[]{:S(2)}) %collective-permute-start.58) | collective-permute-done | bytes 524320 | tf_op jit(solution)/shard_map/ppermute | solution.py:56
  650.2 8.4 collective-permute-done.41
  658.8 9.2 collective-permute-done.61
  676.9 21.1 %collective-permute-done.62 = bf16[256,2048]{1,0:T(8,128)(2,1)} collective-permute-done((bf16[256,2048]{1,0:T(8,128)(2,1)}, bf16[256,2048]{1,0:T(8,128)(2,1)}, u32[]{:S(2)}, u32[]{:S(2)}) %collective-permute-start.62) | collective-permute-done | bytes 1048608 | tf_op jit(solution)/shard_map/ppermute | solution.py:56
  704.0 12.7 %convolution_convert_fusion.4 = bf16[2048,1024]{1,0:T(8,128)(2,1)} fusion(bf16[2048,2048]{1,0:T(8,128)(2,1)} %constant_dynamic-update-slice_fusion.16, bf16[2048,1024]{0,1:T(8,128)(2,1)S(1)} %copy-done.16), kind=kOutput, calls=%fused_computation.38 | convolution fusion | flops 8592031744 | bytes 16777216 | tf_op jit(solution)/shard_map/dot_general | solution.py:212
  756.8 27.7 %attend_back.1 = bf16[2048,768]{1,0:T(8,128)(2,1)} custom-call(s32[2,5]{1,0:T(2,128)S(1)} %pad_add_fusion.info, bf16[2048,768]{1,0:T(8,128)(2,1)} %get-tuple-element.18.qkv, f32[2048,256]{1,0:T(8,128)S(1)} %copy-done.1, f32[2048,256]{1,0:T(8,128)} %subtract_multiply_fusion.1.grad, f32[2048,128]{1,0:T(8,128)S(1)} %copy-done.3, ...), custom_call_target="tpu_custom_call" | custom-call | tf_op jit(solution)/shard_map/attend_back/pallas_call | solution.py:363
  794.9 11.6 %convolution_convert_fusion.6 = bf16[2048,768]{1,0:T(8,128)(2,1)} fusion(bf16[2048,2048]{1,0:T(8,128)(2,1)} %constant_dynamic-update-slice_fusion, bf16[2048,768]{1,0:T(8,128)(2,1)} %attend_back.1), kind=kOutput, calls=%fused_computation.40 | convolution fusion | flops 6444023808 | bytes 14680064 | tf_op jit(solution)/shard_map/dot_general | solution.py:212
  817.4 12.1 %collective-permute-done.75 = bf16[256,1024]{1,0:T(8,128)(2,1)S(1)} collective-permute-done((bf16[256,1024]{1,0:T(8,128)(2,1)S(1)}, bf16[256,1024]{1,0:T(8,128)(2,1)S(1)}, u32[]{:S(2)}, u32[]{:S(2)}) %collective-permute-start.75) | collective-permute-done | bytes 524320 | tf_op jit(solution)/shard_map/ppermute | solution.py:56
  848.3 30.5 %collective-permute-done.86 = f32[2560]{0:T(1024)S(1)} collective-permute-done((f32[2560]{0:T(1024)S(1)}, f32[2560]{0:T(1024)S(1)}, u32[]{:S(2)}, u32[]{:S(2)}) %collective-permute-start.86) | collective-permute-done | bytes 10272 | tf_op jit(solution)/shard_map/ppermute | solution.py:56
  878.8 24.5 %collective-permute-done.42 = bf16[256,2048]{1,0:T(8,128)(2,1)S(1)} collective-permute-done((bf16[256,2048]{1,0:T(8,128)(2,1)}, bf16[256,2048]{1,0:T(8,128)(2,1)S(1)}, u32[]{:S(2)}, u32[]{:S(2)}) %collective-permute-start.42) | collective-permute-done | bytes 1048608 | tf_op jit(solution)/shard_map/ppermute | solution.py:479
  939.1 14.8 %all-to-all-done.7 = bf16[8,64,1024]{2,1,0:T(8,128)(2,1)} async-done(((bf16[8,64,1024]{2,1,0:T(8,128)(2,1)}), bf16[8,64,1024]{2,1,0:T(8,128)(2,1)}, u32[]{:S(2)}, u32[]{:S(2)}) %all-to-all-start.7) | async-done | bytes 1048608 | tf_op jit(solution)/shard_map/all_to_all | solution.py:149
  (618 shorter events, 454.9 us)
Async XLA Ops:
  14.2 53.3 %collective-permute-start = (bf16[256,2048]{1,0:T(8,128)(2,1)}, bf16[256,2048]{1,0:T(8,128)(2,1)S(1)}, u32[]{:S(2)}, u32[]{:S(2)}) collective-permute-start(bf16[256,2048]{1,0:T(8,128)(2,1)} %bitcast.257), channel_id=1, source_target_pairs={{0,22},{1,30},{2,6},{3,14},{4,12},{5,4},{6,28},{7,20},{8,21},{9,29... | collective-permute-start | bytes 3145736 | tf_op jit(solution)/shard_map/ppermute | solution.py:420
  21.3 40.1 %all-to-all-start = ((bf16[8,64,768]{2,1,0:T(8,128)(2,1)}), bf16[8,64,768]{2,1,0:T(8,128)(2,1)}, u32[]{:S(2)}, u32[]{:S(2)}) async-start(bf16[8,64,768]{2,1,0:T(8,128)(2,1)} %copy.104), calls=%async_computation | async-start | bytes 1572864 | tf_op jit(solution)/shard_map/all_to_all | solution.py:135
  61.4 109.7 %all-to-all-start.1 = ((bf16[8,64,256]{2,1,0:T(8,128)(2,1)}), bf16[8,64,256]{2,1,0:T(8,128)(2,1)S(1)}, u32[]{:S(2)}, u32[]{:S(2)}) async-start(bf16[8,64,256]{2,1,0:T(8,128)(2,1)} %copy.110), calls=%async_computation.1 | async-start | bytes 524288 | tf_op jit(solution)/shard_map/all_to_all | solution.py:135
  64.8 67.4 %all-gather.5.cloned.1.call-start = ((), (), s32[]{:S(2)}) async-start(), calls=%async_computation.12 | async-start | bytes 3932160 | tf_op jit(solution)/shard_map/all_gather | solution.py:136
  67.3 131.6 %all-gather.7.cloned.1.call-start = ((), (), s32[]{:S(2)}) async-start(), calls=%async_computation.13 | async-start | bytes 1310720 | tf_op jit(solution)/shard_map/all_gather | solution.py:136
  172.0 256.6 %all-gather.9.cloned.1.call-start = ((), (), s32[]{:S(2)}) async-start(), calls=%async_computation.14 | async-start | bytes 5242880 | tf_op jit(solution)/shard_map/all_gather | solution.py:136
  234.0 50.0 %collective-permute-start.43 = (bf16[256,2048]{1,0:T(8,128)(2,1)S(1)}, bf16[256,2048]{1,0:T(8,128)(2,1)S(1)}, u32[]{:S(2)}, u32[]{:S(2)}) collective-permute-start(bf16[256,2048]{1,0:T(8,128)(2,1)S(1)} %bitcast_select_fusion), channel_id=1, source_target_pairs={{0,22},{1,30},{2,6},{3,14},{4,12},{5,4},{6,28},{7,20},{8,21},{9,29... | collective-permute-start | bytes 3145736 | tf_op jit(solution)/shard_map/ppermute | solution.py:423
  238.3 100.0 %collective-permute-start.18 = (bf16[256,1024]{1,0:T(8,128)(2,1)}, bf16[256,1024]{1,0:T(8,128)(2,1)}, u32[]{:S(2)}, u32[]{:S(2)}) collective-permute-start(bf16[256,1024]{1,0:T(8,128)(2,1)} %get-tuple-element.119), channel_id=1, source_target_pairs={{0,8},{4,12},{8,0},{12,4},{16,24},{20,28},{24,16},{28,20},{1,9},{5... | collective-permute-start | bytes 1572872 | tf_op jit(solution)/shard_map/ppermute | solution.py:56
  239.3 98.9 %collective-permute-start.21 = (bf16[256,1024]{1,0:T(8,128)(2,1)}, bf16[256,1024]{1,0:T(8,128)(2,1)}, u32[]{:S(2)}, u32[]{:S(2)}) collective-permute-start(bf16[256,1024]{1,0:T(8,128)(2,1)} %get-tuple-element.121), channel_id=1, source_target_pairs={{0,16},{4,20},{8,24},{12,28},{16,0},{20,4},{24,8},{28,12},{1,17},{... | collective-permute-start | bytes 1572872 | tf_op jit(solution)/shard_map/ppermute | solution.py:56
  255.3 82.9 %collective-permute-start.20 = (bf16[256,1024]{1,0:T(8,128)(2,1)}, bf16[256,1024]{1,0:T(8,128)(2,1)}, u32[]{:S(2)}, u32[]{:S(2)}) collective-permute-start(bf16[256,1024]{1,0:T(8,128)(2,1)} %fusion.59), channel_id=1, source_target_pairs={{0,16},{4,20},{8,24},{12,28},{16,0},{20,4},{24,8},{28,12},{1,17},{... | collective-permute-start | bytes 1572872 | tf_op jit(solution)/shard_map/ppermute | solution.py:56
  284.0 87.6 %collective-permute-start.44 = (bf16[256,2048]{1,0:T(8,128)(2,1)S(1)}, bf16[256,2048]{1,0:T(8,128)(2,1)}, u32[]{:S(2)}, u32[]{:S(2)}) collective-permute-start(bf16[256,2048]{1,0:T(8,128)(2,1)S(1)} %collective-permute-done.43), channel_id=1, source_target_pairs={{0,8},{4,12},{8,0},{12,4},{16,24},{20,28},{24,16},{28,20},{1,9},{5... | collective-permute-start | bytes 3145736 | tf_op jit(solution)/shard_map/ppermute | solution.py:56
  319.5 49.1 %all-to-all-start.3 = ((bf16[8,64,1024]{2,1,0:T(8,128)(2,1)}), bf16[8,64,1024]{2,1,0:T(8,128)(2,1)}, u32[]{:S(2)}, u32[]{:S(2)}) async-start(bf16[8,64,1024]{2,1,0:T(8,128)(2,1)} %copy.118), calls=%async_computation.3 | async-start | bytes 2097152 | tf_op jit(solution)/shard_map/all_to_all | solution.py:135
  338.0 151.4 %all-gather.11.cloned.1.call-start = ((), (), s32[]{:S(2)}) async-start(), calls=%async_computation.15 | async-start | bytes 5242880 | tf_op jit(solution)/shard_map/all_gather | solution.py:136
  338.0 36.7 %collective-permute-start.23 = (bf16[256,1024]{1,0:T(8,128)(2,1)}, bf16[256,1024]{1,0:T(8,128)(2,1)}, u32[]{:S(2)}, u32[]{:S(2)}) collective-permute-start(bf16[256,1024]{1,0:T(8,128)(2,1)} %get-tuple-element.120), channel_id=1, source_target_pairs={{0,16},{4,20},{8,24},{12,28},{16,0},{20,4},{24,8},{28,12},{1,17},{... | collective-permute-start | bytes 1572872 | tf_op jit(solution)/shard_map/ppermute | solution.py:56
  341.8 32.9 %collective-permute-start.22 = (bf16[256,1024]{1,0:T(8,128)(2,1)}, bf16[256,1024]{1,0:T(8,128)(2,1)}, u32[]{:S(2)}, u32[]{:S(2)}) collective-permute-start(bf16[256,1024]{1,0:T(8,128)(2,1)} %get-tuple-element.106), channel_id=1, source_target_pairs={{0,8},{4,12},{8,0},{12,4},{16,24},{20,28},{24,16},{28,20},{1,9},{5... | collective-permute-start | bytes 1572872 | tf_op jit(solution)/shard_map/ppermute | solution.py:56
  371.4 531.8 %reduce-scatter.9.cloned.1.call-start = ((), (), s32[]{:S(2)}) async-start(), calls=%async_computation.18 | async-start | bytes 5242880 | tf_op jit(solution)/shard_map/reduce_scatter | solution.py:143
  371.5 54.9 %collective-permute-start.48 = (bf16[256,2048]{1,0:T(8,128)(2,1)S(1)}, bf16[256,2048]{1,0:T(8,128)(2,1)S(1)}, u32[]{:S(2)}, u32[]{:S(2)}) collective-permute-start(bf16[256,2048]{1,0:T(8,128)(2,1)S(1)} %collective-permute-done.43), channel_id=1, source_target_pairs={{0,4},{4,0},{8,12},{12,8},{16,20},{20,16},{24,28},{28,24},{1,5},{5... | collective-permute-start | bytes 3145736 | tf_op jit(solution)/shard_map/ppermute | solution.py:56
  372.7 36.1 %collective-permute-start.46 = (bf16[256,1024]{1,0:T(8,128)(2,1)S(1)}, bf16[256,1024]{1,0:T(8,128)(2,1)S(1)}, u32[]{:S(2)}, u32[]{:S(2)}) collective-permute-start(bf16[256,1024]{1,0:T(8,128)(2,1)S(1)} %slice.624), channel_id=1, source_target_pairs={{0,16},{4,20},{8,24},{12,28},{16,0},{20,4},{24,8},{28,12},{1,17},{... | collective-permute-start | bytes 1572872 | tf_op jit(solution)/shard_map/ppermute | solution.py:56
  380.5 38.7 %collective-permute-start.24 = (bf16[256,2048]{1,0:T(8,128)(2,1)}, bf16[256,2048]{1,0:T(8,128)(2,1)S(1)}, u32[]{:S(2)}, u32[]{:S(2)}) collective-permute-start(bf16[256,2048]{1,0:T(8,128)(2,1)} %get-tuple-element.90), channel_id=1, source_target_pairs={{0,8},{4,12},{8,0},{12,4},{16,24},{20,28},{24,16},{28,20},{1,9},{5... | collective-permute-start | bytes 3145736 | tf_op jit(solution)/shard_map/ppermute | solution.py:56
  380.5 45.1 %collective-permute-start.25 = (bf16[256,2048]{1,0:T(8,128)(2,1)}, bf16[256,2048]{1,0:T(8,128)(2,1)S(1)}, u32[]{:S(2)}, u32[]{:S(2)}) collective-permute-start(bf16[256,2048]{1,0:T(8,128)(2,1)} %get-tuple-element.90), channel_id=1, source_target_pairs={{0,16},{4,20},{8,24},{12,28},{16,0},{20,4},{24,8},{28,12},{1,17},{... | collective-permute-start | bytes 3145736 | tf_op jit(solution)/shard_map/ppermute | solution.py:56
  417.3 65.9 %collective-permute-start.50 = (bf16[256,2048]{1,0:T(8,128)(2,1)}, bf16[256,2048]{1,0:T(8,128)(2,1)}, u32[]{:S(2)}, u32[]{:S(2)}) collective-permute-start(bf16[256,2048]{1,0:T(8,128)(2,1)} %collective-permute-done.45), channel_id=1, source_target_pairs={{0,4},{4,0},{8,12},{12,8},{16,20},{20,16},{24,28},{28,24},{1,5},{5... | collective-permute-start | bytes 3145736 | tf_op jit(solution)/shard_map/ppermute | solution.py:56
  442.6 44.4 %collective-permute-start.51 = (bf16[256,2048]{1,0:T(8,128)(2,1)}, bf16[256,2048]{1,0:T(8,128)(2,1)}, u32[]{:S(2)}, u32[]{:S(2)}) collective-permute-start(bf16[256,2048]{1,0:T(8,128)(2,1)} %pad_maximum_fusion.4), channel_id=1, source_target_pairs={{0,4},{4,0},{8,12},{12,8},{16,20},{20,16},{24,28},{28,24},{1,5},{5... | collective-permute-start | bytes 3145736 | tf_op jit(solution)/shard_map/ppermute | solution.py:56
  575.8 342.9 %reduce-scatter.11.cloned.1.call-start = ((), (), s32[]{:S(2)}) async-start(), calls=%async_computation.19 | async-start | bytes 5242880 | tf_op jit(solution)/shard_map/reduce_scatter | solution.py:143
  626.0 32.6 %collective-permute-start.41 = (bf16[256,1024]{1,0:T(8,128)(2,1)S(1)}, bf16[256,1024]{1,0:T(8,128)(2,1)S(1)}, u32[]{:S(2)}, u32[]{:S(2)}) collective-permute-start(bf16[256,1024]{1,0:T(8,128)(2,1)S(1)} %copy-done.37), channel_id=1, source_target_pairs={{0,16},{4,20},{8,24},{12,28},{16,0},{20,4},{24,8},{28,12},{1,17},{... | collective-permute-start | bytes 1572872 | tf_op jit(solution)/shard_map/ppermute | solution.py:56
  626.1 41.9 %collective-permute-start.61 = (bf16[256,1024]{1,0:T(8,128)(2,1)S(1)}, bf16[256,1024]{1,0:T(8,128)(2,1)S(1)}, u32[]{:S(2)}, u32[]{:S(2)}) collective-permute-start(bf16[256,1024]{1,0:T(8,128)(2,1)S(1)} %get-tuple-element.112), channel_id=1, source_target_pairs={{0,16},{4,20},{8,24},{12,28},{16,0},{20,4},{24,8},{28,12},{1,17},{... | collective-permute-start | bytes 1572872 | tf_op jit(solution)/shard_map/ppermute | solution.py:56
  676.9 51.2 %collective-permute-start.66 = (bf16[256,2048]{1,0:T(8,128)(2,1)}, bf16[256,2048]{1,0:T(8,128)(2,1)}, u32[]{:S(2)}, u32[]{:S(2)}) collective-permute-start(bf16[256,2048]{1,0:T(8,128)(2,1)} %get-tuple-element.84), channel_id=1, source_target_pairs={{0,4},{4,0},{8,12},{12,8},{16,20},{20,16},{24,28},{28,24},{1,5},{5... | collective-permute-start | bytes 3145736 | tf_op jit(solution)/shard_map/ppermute | solution.py:56
  716.8 237.1 %reduce-scatter.7.cloned.1.call-start = ((), (), s32[]{:S(2)}) async-start(), calls=%async_computation.17 | async-start | bytes 1310720 | tf_op jit(solution)/shard_map/reduce_scatter | solution.py:143
  794.9 175.2 %reduce-scatter.5.cloned.1.call-start = ((), (), s32[]{:S(2)}) async-start(), calls=%async_computation.16 | async-start | bytes 3932160 | tf_op jit(solution)/shard_map/reduce_scatter | solution.py:143
  830.3 73.0 %collective-permute-start.42 = (bf16[256,2048]{1,0:T(8,128)(2,1)}, bf16[256,2048]{1,0:T(8,128)(2,1)S(1)}, u32[]{:S(2)}, u32[]{:S(2)}) collective-permute-start(bf16[256,2048]{1,0:T(8,128)(2,1)} %get-tuple-element.123), channel_id=1, source_target_pairs={{22,0},{30,1},{6,2},{14,3},{12,4},{4,5},{28,6},{20,7},{21,8},{29,9... | collective-permute-start | bytes 3145736 | tf_op jit(solution)/shard_map/ppermute | solution.py:479
  832.6 79.1 %collective-permute-start.79 = (bf16[256,1024]{1,0:T(8,128)(2,1)}, bf16[256,1024]{1,0:T(8,128)(2,1)}, u32[]{:S(2)}, u32[]{:S(2)}) collective-permute-start(bf16[256,1024]{1,0:T(8,128)(2,1)} %get-tuple-element.108), channel_id=1, source_target_pairs={{0,16},{4,20},{8,24},{12,28},{16,0},{20,4},{24,8},{28,12},{1,17},{... | collective-permute-start | bytes 1572872 | tf_op jit(solution)/shard_map/ppermute | solution.py:56
  848.1 63.6 %collective-permute-start.78 = (bf16[256,1024]{1,0:T(8,128)(2,1)}, bf16[256,1024]{1,0:T(8,128)(2,1)}, u32[]{:S(2)}, u32[]{:S(2)}) collective-permute-start(bf16[256,1024]{1,0:T(8,128)(2,1)} %get-tuple-element.100), channel_id=1, source_target_pairs={{0,8},{4,12},{8,0},{12,4},{16,24},{20,28},{24,16},{28,20},{1,9},{5... | collective-permute-start | bytes 1572872 | tf_op jit(solution)/shard_map/ppermute | solution.py:56
  933.5 42.0 %collective-permute-start.80 = (bf16[256,2048]{1,0:T(8,128)(2,1)}, bf16[256,2048]{1,0:T(8,128)(2,1)}, u32[]{:S(2)}, u32[]{:S(2)}) collective-permute-start(bf16[256,2048]{1,0:T(8,128)(2,1)} %fusion.26), channel_id=1, source_target_pairs={{22,0},{30,1},{6,2},{14,3},{12,4},{4,5},{28,6},{20,7},{21,8},{29,9... | collective-permute-start | bytes 3145736 | tf_op jit(solution)/shard_map/ppermute | solution.py:504
  (135 other events, 3065.6 us)
Sparse Core Ops, SparseCore 0:
  67.8 64.3 all-gather.4
  172.1 26.6 all-gather.6
  228.2 98.5 all-gather.8
  371.5 78.0 all-gather.10
  575.9 75.8 reduce-scatter.8
  716.9 74.7 reduce-scatter.10
  795.0 27.1 reduce-scatter.6
  824.6 81.2 reduce-scatter.4

commit v2 on v1

--- a/solution.py
+++ b/solution.py
@@ -11,6 +11,7 @@
 EPSILON = 1e-05
 HEAD = 64
 STRIPE = 256
+ROWS_AT_ONCE = 256
 LOW = jnp.bfloat16
 WIDE = jnp.float32
 BOTH = ("batch", "seq")
@@ -44,7 +45,7 @@
             for k in range(ns):
                 c, t = b % self.rows, b // self.rows
                 order = [c, 1 - c] if self.fast else list(range(self.rows))
-                entry = [t ^ turn[k][c]] + [row_of[k, p] for p in order]
+                entry = [row_of[k, p] for p in order]
                 for p in order:
                     for q in range(ns):
                         entry.append(q ^ t ^ turn[k][p] if self.fast else q ^ turn[k][p])
@@ -86,68 +87,95 @@
     return value
 
 
-def gather_blocks(plan, block):
+def sync(*values):
+    return lax.optimization_barrier(values)
+
+
+def gather_near(plan, block):
     if not plan.fast:
         slots, width = block.shape
         full = lax.all_gather(block, "batch", axis=0, tiled=False)
         full = full.reshape(plan.nb // plan.rows, plan.rows, slots, width)
-        return full.transpose(1, 0, 2, 3).reshape(plan.nb * slots, width)
-    half = block.shape[1] // 2
-    from_x = swap_over(block, "batch", 2, 8)
-    from_y = swap_over(block, "batch", 4, 8)
-    far_a = swap_over(from_x[:, :half], "batch", 4, 8)
-    far_b = swap_over(from_y[:, half:], "batch", 2, 8)
-    far = jnp.concatenate([far_a, far_b], axis=1)
-    own = [block, from_x, from_y, far]
-    other = [swap_over(piece, "batch", 1, 8) for piece in own]
-    return jnp.concatenate(own + other, axis=0)
-
-
-def reduce_blocks(plan, product, left):
-    count = left.shape[0]
+        return [full.transpose(1, 0, 2, 3).reshape(plan.nb * slots, width)]
+    return [block, swap_over(block, "batch", 2, 8), swap_over(block, "batch", 4, 8)]
+
+
+def gather_far(plan, near):
     if not plan.fast:
-        part = product(left).astype(LOW)
-        width = part.shape[1]
+        return near
+    block, from_x, from_y = near
+    half = block.shape[0] // 2
+    far = swap_over(from_x[:half], "batch", 4, 8), swap_over(from_y[half:], "batch", 2, 8)
+    other = [swap_over(piece, "batch", 1, 8) for piece in near]
+    *other, far_a, far_b = sync(*other, *far)
+    return [*near, far_a, far_b, *other, swap_over(far_a, "batch", 1, 8), swap_over(far_b, "batch", 1, 8)]
+
+
+def reduce_first(plan, kept, *others):
+    if not plan.fast:
+        count, width = kept.shape
         slots = count // plan.nb
-        part = part.reshape(plan.rows, plan.nb // plan.rows, slots, width).transpose(1, 0, 2, 3)
-        return lax.psum_scatter(
+        part = kept.reshape(plan.rows, plan.nb // plan.rows, slots, width).transpose(1, 0, 2, 3)
+        total = lax.psum_scatter(
             part.reshape(count, width), "batch", scatter_dimension=0, tiled=True
-        ).astype(WIDE)
-    other = swap_over(product(left[count // 2 :]).astype(LOW), "batch", 1, 8)
-    mine = product(left[: count // 2]) + other.astype(WIDE)
-    slots, width = count // 8, mine.shape[1]
-    half = width // 2
-    mine = mine.reshape(4, slots, width)
-    near, at_x, at_y, far = mine[0], mine[1], mine[2], mine[3]
-    to_y = swap_over(far[:, :half].astype(LOW), "batch", 2, 8).astype(WIDE)
-    to_x = swap_over(far[:, half:].astype(LOW), "batch", 4, 8).astype(WIDE)
-    x_a = swap_over(at_x[:, :half].astype(LOW), "batch", 2, 8).astype(WIDE)
-    y_b = swap_over(at_y[:, half:].astype(LOW), "batch", 4, 8).astype(WIDE)
-    x_b = swap_over((at_x[:, half:] + to_x).astype(LOW), "batch", 2, 8).astype(WIDE)
-    y_a = swap_over((at_y[:, :half] + to_y).astype(LOW), "batch", 4, 8).astype(WIDE)
-    return jnp.concatenate([near[:, :half] + x_a + y_a, near[:, half:] + x_b + y_b], axis=1)
-
-
-def gather_weight(plan, shard):
+        )
+        total, *others = sync(total, *others)
+        return total.astype(WIDE), others
+    over_x, over_y, near, at_x, at_y = kept
+    slots, half = at_x.shape
+    over_x, over_y = swap_over(over_x, "batch", 2, 8), swap_over(over_y, "batch", 4, 8)
+    over_x, over_y, *others = sync(over_x, over_y, *others)
+    to_x = (at_x + over_y[:slots].astype(WIDE)).astype(LOW)
+    to_y = (at_y + over_x[:slots].astype(WIDE)).astype(LOW)
+    first = near[:, :half] + over_x[slots:].astype(WIDE)
+    second = near[:, half:] + over_y[slots:].astype(WIDE)
+    return (first, second, to_x, to_y), others
+
+
+def reduce_last(plan, state):
+    if not plan.fast:
+        return state
+    first, second, to_x, to_y = state
+    from_x, from_y = swap_over(to_x, "batch", 2, 8), swap_over(to_y, "batch", 4, 8)
+    from_x, from_y = sync(from_x, from_y)
+    return jnp.concatenate([first + from_y.astype(WIDE), second + from_x.astype(WIDE)], axis=1)
+
+
+def split_columns(plan, shard):
     rows, width = shard.shape
-    part = width // plan.nb
-    pieces = shard.reshape(rows, plan.nb, part).transpose(1, 0, 2)
-    pieces = lax.all_to_all(pieces, "batch", 0, 0, tiled=True)
-    full = lax.all_gather(pieces, "seq", axis=1, tiled=True)
-    return full.reshape(plan.nb * plan.ns * rows, part)
-
-
-def scatter_weight(plan, part):
-    total, width = part.shape
-    rows = total // (plan.nb * plan.ns)
-    own = lax.psum_scatter(
-        part.astype(LOW).reshape(plan.nb, plan.ns * rows, width),
-        "seq",
-        scatter_dimension=1,
-        tiled=True,
-    )
-    pieces = lax.all_to_all(own, "batch", 0, 0, tiled=True)
-    return pieces.transpose(1, 0, 2).reshape(rows, plan.nb * width)
+    return shard.reshape(rows, plan.nb, width // plan.nb).transpose(1, 0, 2)
+
+
+def join_columns(plan, pieces):
+    nb, rows, part = pieces.shape
+    return pieces.transpose(1, 0, 2).reshape(rows, nb * part)
+
+
+def exchange(pieces):
+    return lax.all_to_all(pieces, "batch", 0, 0, tiled=True)
+
+
+def gather_layers(pieces):
+    nb, rows, part = pieces.shape
+    return lax.all_gather(pieces.reshape(nb * rows, part), "seq", axis=0, tiled=True)
+
+
+def scatter_layers(plan, part):
+    own = lax.psum_scatter(part, "seq", scatter_dimension=0, tiled=True)
+    rows, width = own.shape
+    return own.reshape(plan.nb, rows // plan.nb, width)
+
+
+def to_inner(plan, values):
+    count, width = values.shape
+    values = values.reshape(count, plan.nb, plan.ns, width // (plan.nb * plan.ns))
+    return values.transpose(0, 2, 1, 3).reshape(count, width)
+
+
+def to_outer(plan, values):
+    count, width = values.shape
+    values = values.reshape(count, plan.ns, plan.nb, width // (plan.nb * plan.ns))
+    return values.transpose(0, 2, 1, 3).reshape(count, width)
 
 
 def norm_stats(values):
@@ -156,11 +184,8 @@
     return mean, lax.rsqrt(jnp.mean(center * center, axis=-1, keepdims=True) + EPSILON)
 
 
-def spread_stats(plan, values):
-    count = values.shape[1]
-    mean = jnp.mean(values, axis=-1)
-    center = values - mean[:, None]
-    square = jnp.sum(center * center, axis=-1)
+def spread_stats(plan, stats, count):
+    mean, square = stats[0], stats[1]
     for step in bits(plan.nb):
         other = swap_over(jnp.stack([mean, square]), "batch", step, plan.nb)
         other = aligned(plan, other, step)
@@ -168,7 +193,13 @@
         mean = 0.5 * (mean + other[0])
         square = square + other[1] + gap * gap * (0.5 * count)
         count = 2 * count
-    return mean[:, None], lax.rsqrt(square / count + EPSILON)[:, None]
+    return jnp.stack([mean, lax.rsqrt(square / count + EPSILON)])
+
+
+def spread_sums(plan, sums, count):
+    for step in bits(plan.nb):
+        sums = sums + aligned(plan, swap_over(sums, "batch", step, plan.nb), step)
+    return sums / (count * plan.nb)
 
 
 def norm_back(upstream, gain, unit, scale):
@@ -176,16 +207,6 @@
     first = jnp.mean(scaled, axis=-1, keepdims=True)
     second = jnp.mean(scaled * unit, axis=-1, keepdims=True)
     grad = scale * (scaled - first - unit * second)
-    return grad, jnp.sum(upstream * unit, axis=0), jnp.sum(upstream, axis=0)
-
-
-def spread_norm_back(plan, upstream, gain, unit, scale):
-    scaled = upstream * gain
-    sums = jnp.stack([jnp.sum(scaled, axis=-1), jnp.sum(scaled * unit, axis=-1)])
-    for step in bits(plan.nb):
-        sums = sums + aligned(plan, swap_over(sums, "batch", step, plan.nb), step)
-    sums = sums / (upstream.shape[1] * plan.nb)
-    grad = scale * (scaled - sums[0][:, None] - unit * sums[1][:, None])
     return grad, jnp.sum(upstream * unit, axis=0), jnp.sum(upstream, axis=0)
 
 
@@ -212,6 +233,287 @@
     return lax.dot_general(a, b, ((contract[:1], contract[1:]), ((), ())), preferred_element_type=WIDE)
 
 
+def as_column(row):
+    return jnp.broadcast_to(row, (128, row.shape[1])).T[:, :1]
+
+
+def as_row(column):
+    return jnp.broadcast_to(column, (column.shape[0], 128)).T[:1]
+
+
+def stat_rows(values):
+    mean = jnp.mean(values, axis=-1, keepdims=True)
+    center = values - mean
+    square = jnp.sum(center * center, axis=-1, keepdims=True)
+    return jnp.concatenate([as_row(mean), as_row(square)], axis=0)
+
+
+def plain_end(acc, block, out):
+    out[...] = acc
+
+
+def gelu_end(acc, block, active_out, slope_out, stats_out):
+    phi = 0.5 + 0.5 * lax.erf(acc * (0.5**0.5))
+    active = acc * phi
+    active_out[...] = active
+    slope_out[...] = phi + acc * (jnp.exp(-0.5 * acc * acc) * ((2.0 * np.pi) ** -0.5))
+    stats_out[...] = stat_rows(active)
+
+
+def norm_back_end(acc, block, normal, stats, gain, bias, out, sums_out, vectors_out, low_out=None):
+    out[...] = acc
+    unit = (normal[...] - as_column(stats[0:1])) * as_column(stats[1:2])
+    if low_out is not None:
+        low_out[...] = (unit * gain[...] + bias[...]).astype(LOW)
+    scaled = acc * gain[...]
+    sums = [jnp.sum(scaled, axis=-1, keepdims=True), jnp.sum(scaled * unit, axis=-1, keepdims=True)]
+    sums_out[...] = jnp.concatenate([as_row(sums[0]), as_row(sums[1])], axis=0)
+    vectors = jnp.concatenate(
+        [jnp.sum(acc * unit, axis=0, keepdims=True), jnp.sum(acc, axis=0, keepdims=True)], axis=0
+    )
+
+    @pl.when(block == 0)
+    def _():
+        vectors_out[...] = vectors
+
+    @pl.when(block != 0)
+    def _():
+        vectors_out[...] += vectors
+
+
+def pieces_kernel(*refs, moves, loads, step, n_arrays, n_weights, n_extra, keep, columns, end):
+    arrays, weights = refs[:n_arrays], refs[n_arrays : n_arrays + n_weights]
+    at = n_arrays + n_weights + n_extra
+    extra = refs[n_arrays + n_weights : at]
+    full, kept = refs[at], refs[at + 1] if keep else None
+    outs = refs[at + 1 + keep : -6]
+    rows, weight, arrived, left, loaded, stored = refs[-6:]
+    block, count = pl.program_id(0), pl.num_programs(0)
+
+    @pl.when(block == 0)
+    def _():
+        for index, column, row, n in loads:
+            pltpu.make_async_copy(
+                weights[index].at[:, pl.ds(column, weight.shape[1])],
+                weight.at[pl.ds(row, n), :],
+                loaded.at[0],
+            ).start()
+        for index, first, row, n in moves:
+            pltpu.make_async_copy(
+                arrays[index].at[pl.ds(first, n), :], rows.at[pl.ds(row, n), :], arrived.at[row // step]
+            ).start()
+        pltpu.make_async_copy(weight, weight, loaded.at[0]).wait()
+        if keep:
+            pltpu.make_async_copy(weight, kept, stored.at[0]).start()
+
+    here = pl.ds(pl.multiple_of(block * step, step), step)
+    pltpu.make_async_copy(rows.at[here], rows.at[here], arrived.at[block]).wait()
+    pltpu.make_async_copy(rows.at[here], full.at[here], left.at[block]).start()
+    acc = matmul(rows[here, :], weight[:, :columns], (1, 0))
+    end(acc, block, *extra, *outs)
+
+    @pl.when(block == count - 1)
+    def _():
+        for i in range(rows.shape[0] // step):
+            part = pl.ds(i * step, step)
+            pltpu.make_async_copy(rows.at[part], full.at[part], left.at[i]).wait()
+        if keep:
+            pltpu.make_async_copy(weight, kept, stored.at[0]).wait()
+
+
+def pieces_matmul(arrays, weights, columns, end, extra, outs, name):
+    step = ROWS_AT_ONCE
+    moves, total = [], 0
+    for index, array in enumerate(arrays):
+        for first in range(0, array.shape[0], step):
+            n = min(step, array.shape[0] - first)
+            moves.append((index, first, total, n))
+            total += n
+    loads, inner = [], 0
+    for index, weight in enumerate(weights):
+        loads.append((index, columns[0], inner, weight.shape[0]))
+        inner += weight.shape[0]
+    keep = len(weights) > 1
+
+    def spec(shape, kind):
+        if kind == "rows":
+            return pl.BlockSpec((step, shape[1]), lambda i: (i, 0))
+        if kind == "lanes":
+            return pl.BlockSpec((shape[0], step), lambda i: (0, i))
+        return pl.BlockSpec(shape, lambda i: (0, 0))
+
+    anywhere = pl.BlockSpec(memory_space=pl.ANY)
+    kept = [jax.ShapeDtypeStruct((inner, columns[1]), LOW)] if keep else []
+    return pl.pallas_call(
+        functools.partial(
+            pieces_kernel,
+            moves=moves,
+            loads=loads,
+            step=step,
+            n_arrays=len(arrays),
+            n_weights=len(weights),
+            n_extra=len(extra),
+            keep=int(keep),
+            columns=columns[2],
+            end=end,
+        ),
+        grid=(total // step,),
+        in_specs=[anywhere] * (len(arrays) + len(weights))
+        + [spec(array.shape, kind) for array, kind in extra],
+        out_specs=[anywhere] * (1 + keep) + [spec(*out[:2]) for out in outs],
+        out_shape=[jax.ShapeDtypeStruct((total, inner), LOW)]
+        + kept
+        + [jax.ShapeDtypeStruct(out[0], out[2] if len(out) > 2 else WIDE) for out in outs],
+        scratch_shapes=[
+            pltpu.VMEM((total, inner), LOW),
+            pltpu.VMEM((inner, columns[1]), LOW),
+            pltpu.SemaphoreType.DMA((total // step,)),
+            pltpu.SemaphoreType.DMA((total // step,)),
+            pltpu.SemaphoreType.DMA((1,)),
+            pltpu.SemaphoreType.DMA((1,)),
+        ],
+        compiler_params=pltpu.CompilerParams(vmem_limit_bytes=56 << 20),
+        name=name,
+    )(*arrays, *weights, *[array for array, _ in extra])
+
+
+def mixed_left(values, stats, gain, bias):
+    unit = (values[...] - as_column(stats[0:1])) * as_column(stats[1:2])
+    return (unit * gain[...] + bias[...]).astype(LOW)
+
+
+def hidden_left(grad, active, slope, stats, sums, gain):
+    scale = as_column(stats[1:2])
+    unit = (active[...] - as_column(stats[0:1])) * scale
+    back = grad[...] * gain[...] - as_column(sums[0:1]) - unit * as_column(sums[1:2])
+    return (scale * back * slope[...]).astype(LOW)
+
+
+def plain_left(values):
+    return values[...]
+
+
+def part_kernel(*refs, n_in, make_left, keeps, own, split):
+    weight = refs[n_in]
+    left = make_left(*refs[:n_in])
+    acc = matmul(left, weight[...], (1, 1))
+    outs = refs[n_in + 1 :]
+    others = outs[:4]
+    if own:
+        outs = outs[5:] if keeps else outs[4:]
+    if keeps:
+        outs[0][...] = left
+        outs = outs[1:]
+    block = pl.program_id(0)
+    if not own:
+        if not split:
+            outs[0][...] = acc.astype(LOW)
+            return
+        for i, out in enumerate(outs):
+
+            @pl.when(block == i)
+            def _(out=out):
+                out[...] = acc.astype(LOW)
+
+        return
+    over_x, over_y, near, at_x, at_y = outs
+    slots, half = at_x.shape
+
+    @pl.when(block == 0)
+    def _():
+        near[...] = acc + others[0][...].astype(WIDE)
+
+    @pl.when(block == 1)
+    def _():
+        total = acc + others[1][...].astype(WIDE)
+        over_x[slots:] = total[:, :half].astype(LOW)
+        at_x[...] = total[:, half:]
+
+    @pl.when(block == 2)
+    def _():
+        total = acc + others[2][...].astype(WIDE)
+        over_y[slots:] = total[:, half:].astype(LOW)
+        at_y[...] = total[:, :half]
+
+    @pl.when(block == 3)
+    def _():
+        total = acc + others[3][...].astype(WIDE)
+        over_x[:slots] = total[:, :half].astype(LOW)
+        over_y[:slots] = total[:, half:].astype(LOW)
+
+
+def part_call(plan, ins, weight, columns, make_left, keeps, first, blocks, name, others=(), kept=()):
+    step = ROWS_AT_ONCE
+    total = next(array.shape[0] for array, kind in ins if kind == "rows")
+    rows, own = weight.shape[0], len(others) > 0
+
+    def spec(array, kind):
+        if kind == "rows":
+            return pl.BlockSpec((step, array.shape[1]), lambda i: (first + i, 0))
+        if kind == "lanes":
+            return pl.BlockSpec((array.shape[0], step), lambda i: (0, first + i))
+        return pl.BlockSpec(array.shape, lambda i: (0, 0))
+
+    in_specs = [spec(*item) for item in ins]
+    in_specs.append(
+        pl.BlockSpec(
+            (rows, columns[0]), lambda i: (0, columns[1]), pipeline_mode=pl.Buffered(1)
+        )
+    )
+    operands = [array for array, _ in ins] + [weight, *others]
+    in_specs += [
+        pl.BlockSpec((step, rows), lambda i: (0, 0), pipeline_mode=pl.Buffered(1)) for _ in others
+    ]
+    out_specs, out_shape, aliases = [], [], {}
+    if keeps:
+        if own:
+            aliases[len(operands)] = 0
+            in_specs.append(pl.BlockSpec(memory_space=pl.ANY))
+            operands += kept
+        out_specs.append(pl.BlockSpec((step, columns[0]), lambda i: (first + i, 0)))
+        out_shape.append(jax.ShapeDtypeStruct((total, columns[0]), LOW))
+    whole = []
+    if own:
+        half = rows // 2
+        whole = [((2 * step, half), LOW)] * 2 + [((step, rows), WIDE)] + [((step, half), WIDE)] * 2
+    elif plan.fast:
+        whole = [((step, rows), LOW)] * blocks
+    else:
+        out_specs.append(pl.BlockSpec((step, rows), lambda i: (i, 0)))
+        out_shape.append(jax.ShapeDtypeStruct((blocks * step, rows), LOW))
+    for shape, kind in whole:
+        out_specs.append(pl.BlockSpec(shape, lambda i: (0, 0)))
+        out_shape.append(jax.ShapeDtypeStruct(shape, kind))
+    return pl.pallas_call(
+        functools.partial(
+            part_kernel, n_in=len(ins), make_left=make_left, keeps=keeps, own=own, split=plan.fast
+        ),
+        grid=(blocks,),
+        in_specs=in_specs,
+        out_specs=out_specs,
+        out_shape=out_shape,
+        input_output_aliases=aliases,
+        compiler_params=pltpu.CompilerParams(vmem_limit_bytes=56 << 20),
+        name=name,
+    )(*operands)
+
+
+def block_parts(plan, ins, weight, columns, make_left, keeps, name):
+    total = next(array.shape[0] for array, kind in ins if kind == "rows")
+    blocks = total // ROWS_AT_ONCE
+    if not plan.fast:
+        *left, part = part_call(plan, ins, weight, columns, make_left, keeps, 0, blocks, name)
+        return *left, part
+    half = blocks // 2
+    outs = part_call(plan, ins, weight, columns, make_left, keeps, half, half, name + "_other")
+    left, parts = outs[: int(keeps)], outs[int(keeps) :]
+    others = [swap_over(part, "batch", 1, 8) for part in parts]
+    outs = part_call(
+        plan, ins, weight, columns, make_left, keeps, 0, half, name + "_own", others, left
+    )
+    return *outs[: int(keeps)], outs[int(keeps) :]
+
+
 def fill_bias(bias, valid, seg_row, seg_col, length):
     for i in range(length // STRIPE):
         low, high = i * STRIPE, (i + 1) * STRIPE
@@ -223,7 +525,9 @@
         bias[low:high, :high] = jnp.where(allowed, 0.0, -1e30)
 
 
-def attend_kernel(info, proj, tables, seg_row, seg_col, qkv, attended, log_total, bias, *, ns, slots, hd):
+def attend_kernel(
+    info, proj, tables, seg_row, seg_col, qkv, attended, log_total, stats, bias, *, ns, slots, hd
+):
     row, head = pl.program_id(0), pl.program_id(1)
     length = ns * slots
 
@@ -264,9 +568,15 @@
                 mine[rows], summed[rows], attended[pl.ds(to, slots), :]
             )
 
+    @pl.when(head == pl.num_programs(1) - 1)
+    def _():
+        for q in range(ns):
+            here = slice(q * slots, (q + 1) * slots)
+            stats[:, here] = stat_rows(attended[here])
+
 
 def attend_back_kernel(
-    info, qkv, attended, grad, log_total, tables, seg_row, seg_col, out,
+    info, qkv, attended, grad, stats, sums, gain, log_total, tables, seg_row, seg_col, out,
     bias, grad_low, product, grad_q, grad_k, grad_v, *, ns, slots, hd
 ):
     row, head = pl.program_id(0), pl.program_id(1)
@@ -278,10 +588,14 @@
     @pl.when(head == 0)
     def _():
         for q in range(ns):
-            source, low, high = place(q), q * slots, (q + 1) * slots
-            values = grad[pl.ds(source, slots), :]
-            grad_low[low:high] = values.astype(LOW)
-            product[low:high] = values * attended[pl.ds(source, slots), :]
+            to, low, high = place(q), q * slots, (q + 1) * slots
+            values = attended[low:high]
+            scale = as_column(stats[1:2, low:high])
+            unit = (values - as_column(stats[0:1, low:high])) * scale
+            back = grad[low:high] * gain[...] - as_column(sums[0:1, low:high])
+            back = scale * (back - unit * as_column(sums[1:2, low:high]))
+            grad_low[pl.ds(to, slots), :] = back.astype(LOW)
+            product[pl.ds(to, slots), :] = back * values
         fill_bias(bias, info[row, ns], seg_row[...], seg_col[...], length)
         for total in (grad_q, grad_k, grad_v):
             total[...] = jnp.zeros_like(total)
@@ -343,20 +657,26 @@
                 pl.BlockSpec((None, 1, length), lambda r, h, info: (r, 0, 0)),
                 pl.BlockSpec((None, length, 1), lambda r, h, info: (r, 0, 0)),
             ],
-            out_specs=[row_block(length, width), row_block(length, hd), row_block(length, 128)],
+            out_specs=[
+                row_block(length, width),
+                row_block(length, hd),
+                row_block(length, 128),
+                pl.BlockSpec((2, length), lambda r, h, info: (0, r)),
+            ],
             scratch_shapes=[pltpu.VMEM((length, length), WIDE)],
         ),
         out_shape=[
             jax.ShapeDtypeStruct((count, width), LOW),
             jax.ShapeDtypeStruct((count, hd), WIDE),
             jax.ShapeDtypeStruct((count, 128), WIDE),
+            jax.ShapeDtypeStruct((2, count), WIDE),
         ],
         compiler_params=pltpu.CompilerParams(vmem_limit_bytes=48 << 20),
         name="attend",
     )(info, proj, tables, segments[:, None, :], segments[:, :, None])
 
 
-def attend_back(plan, info, qkv, attended, grad, log_total, tables, segments):
+def attend_back(plan, info, qkv, attended, grad, stats, sums, gain, log_total, tables, segments):
     count, width = qkv.shape
     length, hd = count // plan.rows, width // 3
     slots = length // plan.ns
@@ -369,6 +689,9 @@
                 row_block(length, width),
                 row_block(length, hd),
                 row_block(length, hd),
+                pl.BlockSpec((2, length), lambda r, h, info: (0, r)),
+                pl.BlockSpec((2, length), lambda r, h, info: (0, r)),
+                shared_block(1, hd),
                 row_block(length, 128),
                 shared_block(length, 512),
                 pl.BlockSpec((None, 1, length), lambda r, h, info: (r, 0, 0)),
@@ -387,7 +710,10 @@
         out_shape=jax.ShapeDtypeStruct((count, width), LOW),
         compiler_params=pltpu.CompilerParams(vmem_limit_bytes=48 << 20),
         name="attend_back",
-    )(info, qkv, attended, grad, log_total, tables, segments[:, None, :], segments[:, :, None])
+    )(
+        info, qkv, attended, grad, stats, sums, gain, log_total, tables,
+        segments[:, None, :], segments[:, :, None],
+    )
 
 
 def shards(
@@ -417,21 +743,23 @@
         jnp.asarray(plan.table), batch_index * ns + seq_index, 0, keepdims=False
     )
 
-    tokens_low = lax.ppermute(tokens[0], BOTH, plan.there)
     slot = seq_index * slots + jnp.arange(slots, dtype=jnp.int32)
     living = (slot < valid_count[0])[:, None]
-    grad_low = lax.ppermute(
-        jnp.where(living, cotangent[0], jnp.zeros((), LOW)), BOTH, plan.there
-    )
-
-    group = w_qkv.reshape(w_qkv.shape[0], 3, nb, hd).transpose(0, 2, 1, 3)
-    qkv_w = gather_weight(plan, group.reshape(w_qkv.shape))
-    out_wt = gather_weight(plan, w_out.T)
-    up_w = gather_weight(plan, w_up)
-    down_wt = gather_weight(plan, w_down.T)
+    grad_low = to_inner(plan, jnp.where(living, cotangent[0], jnp.zeros((), LOW)))
+    tokens_low = lax.ppermute(to_inner(plan, tokens[0]), BOTH, plan.there)
+    group = w_qkv.reshape(w_qkv.shape[0], 3, nb, hd).transpose(2, 0, 1, 3)
+    group = group.reshape(nb, -1, 3 * hd)
+    attn_own = exchange(jnp.concatenate([group, split_columns(plan, w_out.T)], axis=2))
+    ffn_own = jnp.concatenate([split_columns(plan, w) for w in (w_up, w_down.T)], axis=2)
 
     own_params = (gain_attn, bias_attn, gain_mix, bias_mix, gain_ffn, bias_ffn, gain_hidden, bias_hidden)
     params = gather_over(jnp.concatenate([p.astype(WIDE) for p in own_params]), "seq", ns)
+    tables = xpos_tables(length)
+    tokens_low, attn_own, ffn_own, grad_low, params, tables = sync(
+        tokens_low, attn_own, ffn_own, grad_low, params, tables
+    )
+    attn_w = gather_layers(attn_own)
+    ffn_own = exchange(ffn_own)
     packed = jnp.concatenate(
         [params.reshape(-1), segments[0].astype(WIDE), valid_count.astype(WIDE)]
     )
@@ -442,83 +770,170 @@
         piece = spread[:, :, at : at + p.shape[0]]
         at += p.shape[0]
         if index in (0, 1, 4, 5):
-            vectors.append(piece.reshape(-1))
+            vectors.append(piece.transpose(1, 0, 2).reshape(1, -1))
         else:
-            vectors.append(lax.dynamic_index_in_dim(piece, batch_index, 0, False).reshape(-1))
+            vectors.append(lax.dynamic_index_in_dim(piece, batch_index, 0, False).reshape(1, -1))
     ga, ba, gm, bm, gf, bf, gh, bh = vectors
-    layer_rows = packed[entry[1 : 1 + plan.rows], params.size :].astype(jnp.int32)
+    layer_rows = jnp.concatenate(
+        [
+            lax.dynamic_slice_in_dim(packed[:, params.size :], entry[r], 1, 0)
+            for r in range(plan.rows)
+        ]
+    ).astype(jnp.int32)
     seg_rows = layer_rows[:, :length]
     info = jnp.concatenate(
-        [entry[1 + plan.rows :].reshape(plan.rows, ns), layer_rows[:, length:]], axis=1
-    )
-    tables = xpos_tables(length)
-
+        [entry[plan.rows :].reshape(plan.rows, ns), layer_rows[:, length:]], axis=1
+    )
+    count = plan.rows * length
     resid = tokens_low.astype(WIDE)
     mean_attn, scale_attn = norm_stats(resid)
     unit_attn = (resid - mean_attn) * scale_attn
-    normed = gather_blocks(plan, (unit_attn * ga + ba).astype(LOW))
-    projected = matmul(normed, qkv_w, (1, 0))
-    qkv, attended, log_total = attend(plan, info, projected, tables, seg_rows)
-    mean_mix, scale_mix = spread_stats(plan, attended)
-    unit_mix = (attended - mean_mix) * scale_mix
-    mixed = (unit_mix * gm + bm).astype(LOW)
-    resid_mid = resid + reduce_blocks(plan, lambda left: matmul(left, out_wt, (1, 1)), mixed)
+    normed_low = (unit_attn * ga + ba).astype(LOW)
+    normed_low, ffn_own, gm, bm, gf, bf, gh, bh = sync(
+        normed_low, ffn_own, gm, bm, gf, bf, gh, bh
+    )
+    up_w = gather_layers(ffn_own[:, :, :hidden_part])
+    down_wt = gather_layers(ffn_own[:, :, hidden_part:])
+
+    near = sync(*gather_near(plan, normed_low))
+    grad_low, *arrays = sync(grad_low, *gather_far(plan, near))
+    grad_low = lax.ppermute(grad_low, BOTH, plan.there)
+    normed, projected = pieces_matmul(
+        arrays,
+        [attn_w],
+        (0, 3 * hd, 3 * hd),
+        plain_end,
+        [],
+        [((count, 3 * hd), "rows")],
+        "project",
+    )
+    qkv, attended, log_total, stats_mix = attend(plan, info, projected, tables, seg_rows)
+    stats_mix, grad_low = sync(stats_mix, grad_low)
+    stats_mix = spread_stats(plan, stats_mix, hd)
+    mixed, kept = block_parts(
+        plan,
+        [(attended, "rows"), (stats_mix, "lanes"), (gm, "whole"), (bm, "whole")],
+        attn_w,
+        (hd, 3),
+        mixed_left,
+        True,
+        "out",
+    )
+    state, _ = reduce_first(plan, kept)
+    resid_mid = resid + reduce_last(plan, state)
+
     mean_ffn, scale_ffn = norm_stats(resid_mid)
     unit_ffn = (resid_mid - mean_ffn) * scale_ffn
-    ffn_in = gather_blocks(plan, (unit_ffn * gf + bf).astype(LOW))
-    hidden = matmul(ffn_in, up_w, (1, 0))
-    phi = 0.5 * lax.erfc(hidden * (-(0.5**0.5)))
-    active = hidden * phi
-    slope = phi + hidden * (jnp.exp(-0.5 * hidden * hidden) * ((2.0 * np.pi) ** -0.5))
-    mean_hid, scale_hid = spread_stats(plan, active)
-    unit_hid = (active - mean_hid) * scale_hid
-    hidden_low = (unit_hid * gh + bh).astype(LOW)
-    output = resid_mid + reduce_blocks(
-        plan, lambda left: matmul(left, down_wt, (1, 1)), hidden_low
-    )
-    output = lax.ppermute(output.astype(LOW), BOTH, plan.back)
-
-    grad_all = gather_blocks(plan, grad_low)
-    grad_hn = matmul(grad_all, down_wt, (1, 0))
-    grad_down = scatter_weight(plan, matmul(grad_all, hidden_low, (0, 0)))
-    grad_active, gain_hidden_part, bias_hidden_part = spread_norm_back(
-        plan, grad_hn, gh, unit_hid, scale_hid
-    )
-    grad_hidden = (grad_active * slope).astype(LOW)
-    grad_ffn_in = reduce_blocks(plan, lambda left: matmul(left, up_w, (1, 1)), grad_hidden)
-    grad_up = scatter_weight(plan, matmul(ffn_in, grad_hidden, (0, 0)))
+    near = sync(*gather_near(plan, (unit_ffn * gf + bf).astype(LOW)))
+    grad_later, *arrays = sync(grad_low, *gather_far(plan, near))
+    grad_near = gather_near(plan, grad_later)
+    ffn_in, active, slope, stats_hid = pieces_matmul(
+        arrays,
+        [up_w],
+        (0, hidden_part, hidden_part),
+        gelu_end,
+        [],
+        [((count, hidden_part), "rows"), ((count, hidden_part), "rows"), ((2, count), "lanes")],
+        "up",
+    )
+    stats_hid, *grad_near = sync(stats_hid, *grad_near)
+    grad_arrays = gather_far(plan, grad_near)
+    stats_hid = spread_stats(plan, stats_hid, hidden_part)
+
+    grad_all, grad_hn, sums_hid, vectors_hid, hidden_low = pieces_matmul(
+        grad_arrays,
+        [down_wt],
+        (0, hidden_part, hidden_part),
+        norm_back_end,
+        [(active, "rows"), (stats_hid, "lanes"), (gh, "whole"), (bh, "whole")],
+        [
+            ((count, hidden_part), "rows"),
+            ((2, count), "lanes"),
+            ((2, hidden_part), "whole"),
+            ((count, hidden_part), "rows", LOW),
+        ],
+        "down_back",
+    )
+    grad_down = matmul(grad_all, hidden_low, (0, 0)).astype(LOW)
+    sums_hid = spread_sums(plan, sums_hid, hidden_part)
+    sums_hid, grad_down = sync(sums_hid, grad_down)
+    grad_down = scatter_layers(plan, grad_down)
+    grad_hidden, kept = block_parts(
+        plan,
+        [
+            (grad_hn, "rows"), (active, "rows"), (slope, "rows"),
+            (stats_hid, "lanes"), (sums_hid, "lanes"), (gh, "whole"),
+        ],
+        up_w,
+        (hidden_part, 0),
+        hidden_left,
+        True,
+        "up_back",
+    )
+    grad_up = matmul(ffn_in, grad_hidden, (0, 0)).astype(LOW)
+    state, (grad_up, hidden_low) = reduce_first(plan, kept, grad_up, hidden_low)
+    grad_up = scatter_layers(plan, grad_up)
+    grad_ffn_in = reduce_last(plan, state)
     grad_mid, gain_ffn_part, bias_ffn_part = norm_back(grad_ffn_in, gf, unit_ffn, scale_ffn)
     grad_mid = grad_mid + grad_low.astype(WIDE)
-    mid_all = gather_blocks(plan, grad_mid.astype(LOW))
-    grad_mixed = matmul(mid_all, out_wt, (1, 0))
-    grad_out = scatter_weight(plan, matmul(mid_all, mixed, (0, 0)))
-    grad_attended, gain_mix_part, bias_mix_part = spread_norm_back(
-        plan, grad_mixed, gm, unit_mix, scale_mix
-    )
-    grad_proj = attend_back(plan, info, qkv, attended, grad_attended, log_total, tables, seg_rows)
-    grad_normed = reduce_blocks(plan, lambda left: matmul(left, qkv_w, (1, 1)), grad_proj)
-    grad_qkv = scatter_weight(plan, matmul(normed, grad_proj, (0, 0)))
+    (kept,) = block_parts(
+        plan, [(hidden_low, "rows")], down_wt, (hidden_part, 0), plain_left, False, "down"
+    )
+    kept, near, grad_down = sync(kept, gather_near(plan, grad_mid.astype(LOW)), grad_down)
+    arrays = sync(*gather_far(plan, near))
+    grad_down, arrays = sync(grad_down, arrays)
+    grad_down = exchange(grad_down)
+    mid_all, grad_mixed, sums_mix, vectors_mix = pieces_matmul(
+        arrays,
+        [attn_w],
+        (3 * hd, hd, hd),
+        norm_back_end,
+        [(attended, "rows"), (stats_mix, "lanes"), (gm, "whole"), (bm, "whole")],
+        [((count, hd), "rows"), ((2, count), "lanes"), ((2, hd), "whole")],
+        "out_back",
+    )
+    sums_mix, grad_down = sync(sums_mix, grad_down)
+    grad_out = matmul(mid_all, mixed, (0, 0)).astype(LOW)
+    sums_mix = spread_sums(plan, sums_mix, hd)
+    sums_mix, grad_out, kept = sync(sums_mix, grad_out, kept)
+    grad_out = scatter_layers(plan, grad_out)
+    grad_proj = attend_back(
+        plan, info, qkv, attended, grad_mixed, stats_mix, sums_mix, gm, log_total, tables, seg_rows
+    )
+    state, (grad_proj, grad_up) = reduce_first(plan, kept, grad_proj, grad_up)
+    grad_up = exchange(grad_up)
+    output = (resid_mid + reduce_last(plan, state)).astype(LOW)
+    grad_qkv = matmul(normed, grad_proj, (0, 0)).astype(LOW)
+    grad_proj, grad_qkv, output, grad_up = sync(grad_proj, grad_qkv, output, grad_up)
+    grad_qkv = scatter_layers(plan, grad_qkv)
+    output = lax.ppermute(output, BOTH, plan.back)
+    (kept,) = block_parts(
+        plan, [(grad_proj, "rows")], attn_w, (3 * hd, 0), plain_left, False, "project_back"
+    )
+    state, _ = reduce_first(plan, kept)
+    grad_normed = reduce_last(plan, state)
     grad_resid, gain_attn_part, bias_attn_part = norm_back(
         grad_normed, ga, unit_attn, scale_attn
     )
-    grad_tokens = lax.ppermute((grad_mid + grad_resid).astype(LOW), BOTH, plan.back)
-
-    whole = (gain_ffn_part, bias_ffn_part, gain_attn_part, bias_attn_part)
-    parts = (gain_mix_part, bias_mix_part, gain_hidden_part, bias_hidden_part)
-    whole_sum = sum_over(sum_over(jnp.stack(whole), "seq", ns), "batch", nb)
+    grad_tokens = (grad_mid + grad_resid).astype(LOW)
+    grad_tokens, grad_qkv, grad_out = sync(grad_tokens, grad_qkv, grad_out)
+    grad_tokens = lax.ppermute(grad_tokens, BOTH, plan.back)
+    grad_qkv, grad_out = exchange(grad_qkv), exchange(grad_out)
+
+    whole = jnp.stack([gain_ffn_part, bias_ffn_part, gain_attn_part, bias_attn_part])
+    whole_sum = sum_over(sum_over(whole, "seq", ns), "batch", nb)
     whole_sum = whole_sum.reshape(4, nb * ns, -1)
-    own = lax.dynamic_index_in_dim(whole_sum, batch_index * ns + seq_index, 1, False)
-    part_sum = sum_over(jnp.concatenate(parts), "seq", ns)
-    mixes = part_sum[: 2 * hd].reshape(2, ns, -1)
-    hiddens = part_sum[2 * hd :].reshape(2, ns, -1)
-    mixes = lax.dynamic_index_in_dim(mixes, seq_index, 1, False)
-    hiddens = lax.dynamic_index_in_dim(hiddens, seq_index, 1, False)
-
-    grad_qkv = grad_qkv.reshape(-1, nb, 3, hd).transpose(0, 2, 1, 3).reshape(w_qkv.shape)
+    own = lax.dynamic_index_in_dim(whole_sum, seq_index * nb + batch_index, 1, False)
+    part_sum = sum_over(jnp.concatenate([vectors_mix, vectors_hid], axis=1), "seq", ns)
+    mixes = lax.dynamic_index_in_dim(part_sum[:, :hd].reshape(2, ns, -1), seq_index, 1, False)
+    hiddens = lax.dynamic_index_in_dim(part_sum[:, hd:].reshape(2, ns, -1), seq_index, 1, False)
+
+    grad_qkv = grad_qkv.reshape(nb, -1, 3, hd).transpose(1, 2, 0, 3)
+    grad_out, grad_up, grad_down = [join_columns(plan, g) for g in (grad_out, grad_up, grad_down)]
     return (
-        output[None],
-        grad_tokens.astype(WIDE)[None],
-        grad_qkv.astype(WIDE),
+        to_outer(plan, output)[None],
+        to_outer(plan, grad_tokens).astype(WIDE)[None],
+        grad_qkv.reshape(w_qkv.shape).astype(WIDE),
         grad_out.astype(WIDE).T,
         grad_up.astype(WIDE),
         grad_down.astype(WIDE).T,

time: 1020 us -> 832 us (0.82)
  Pallas kernels: 49.6 us -> 208 us
  matrix products: 156 us -> 46 us
  local copies, waits for them, and re-layouts: 156 us -> 71.1 us
  waiting for transfers between devices: 378 us -> 302 us
  starting transfers between devices: 151 us -> 120 us
  other arithmetic: 75.2 us -> 49.4 us
  blocking collectives: 18 us -> 0 us
    pallas_call x0 -> x12, Pallas kernels: none -> 154 us  [the longest x8 86.5 us: part_call(): pl.pallas_call(functools.partial(part_kernel, n_in=len(ins), make_left=ma...]
    dot_general x16 -> x4, matrix products: 156 us -> 46 us  [matmul(): lax.dot_general(a, b, ((contract[:1], contract[1:]), ((), ())), preferred...]
    ppermute x4, waiting for transfers between devices: 53.1 us -> 0.01 us  [the longest x1 0.01 us: shards(): tokens_low = lax.ppermute(to_inner(plan, tokens[0]), BOTH, plan.there)]
    unnamed x180 -> x139, local copies, waits for them, and re-layouts: 61.8 us -> 22.3 us
    ppermute x84 -> x92, waiting for transfers between devices: 236 us -> 268 us  [swap_over(): return lax.ppermute(value, axis, [(i, i ^ step) for i in range(size)])]
    all_gather x4 -> x3, waiting for transfers between devices: 31.1 us -> 0.01 us  [gather_layers(): lax.all_gather(pieces.reshape(nb * rows, part), 'seq', axis=0, tiled=True)]
    all_to_all x7 -> x6, waiting for transfers between devices: 58.4 us -> 34.2 us  [exchange(): return lax.all_to_all(pieces, 'batch', 0, 0, tiled=True)]
    all_to_all x7 -> x6, starting transfers between devices: 49.9 us -> 28.8 us  [exchange(): return lax.all_to_all(pieces, 'batch', 0, 0, tiled=True)]
  transfers between devices with their start and end apart: 103 -> 109, of which waited for: 42 -> 67; matrix products, arithmetic and copies ran while one was open for 33% -> 17% of each run, Pallas kernels for 5% -> 23%
where the time goes in v2:
time: 832 us; the launch traced here: 817 us
  waiting for transfers between devices  302 us (36%)
  Pallas kernels  208 us (25%)
  starting transfers between devices  120 us (14%)
  local copies, waits for them, and re-layouts  71.1 us (9%)
  other arithmetic  49.4 us (6%)
  matrix products  46 us (6%)
  between operations  20.4 us (2%)
    ppermute x92, waiting for transfers between devices, swap_over(): return lax.ppermute(value, axis, [(i, i ^ step) for i in range(size)])  268 us
    pallas_call x8, Pallas kernels, part_call(): pl.pallas_call(functools.partial(part_kernel, n_in=len(ins), make_left=ma...  86.5 us
    ppermute x92, starting transfers between devices, swap_over(): return lax.ppermute(value, axis, [(i, i ^ step) for i in range(size)])  77.9 us
    pallas_call x4, Pallas kernels, pieces_matmul(): pl.pallas_call(functools.partial(pieces_kernel, moves=moves, loads=loads,...  68 us
    dot_general x4, matrix products, matmul(): lax.dot_general(a, b, ((contract[:1], contract[1:]), ((), ())), preferred...  46 us
    all_to_all x6, waiting for transfers between devices, exchange(): return lax.all_to_all(pieces, 'batch', 0, 0, tiled=True)  34.2 us
    pallas_call x1, Pallas kernels, attend_back(): pl.pallas_call(functools.partial(attend_back_kernel, ns=plan.ns, slots=sl...  29.7 us
    all_to_all x6, starting transfers between devices, exchange(): return lax.all_to_all(pieces, 'batch', 0, 0, tiled=True)  28.8 us
  transfers between devices with their start and end apart: 109, of which 67 were waited for; matrix products, arithmetic and copies ran while one was open for 17% of the time, Pallas kernels for 23%

profile of v2, /device:TPU:4, one launch (start us, length us, event | category | flops | bytes accessed | tf_op | source)
XLA Modules:
  0.0 817.0 jit_solution(13286347491920180576)
XLA Ops:
  80.7 20.6 %all-to-all-done.1 = bf16[8,64,2048]{2,1,0:T(8,128)(2,1)S(1)} async-done(((bf16[8,64,2048]{2,1,0:T(8,128)(2,1)}), bf16[8,64,2048]{2,1,0:T(8,128)(2,1)S(1)}, u32[]{:S(2)}, u32[]{:S(2)}) %all-to-all-start.1) | async-done | bytes 2097184 | tf_op jit(solution)/shard_map/all_to_all | solution.py:155
  103.3 21.2 %collective-permute-done.7.refs_2_ = bf16[256,2048]{1,0:T(8,128)(2,1)S(1)} collective-permute-done((bf16[256,2048]{1,0:T(8,128)(2,1)}, bf16[256,2048]{1,0:T(8,128)(2,1)S(1)}, u32[]{:S(2)}, u32[]{:S(2)}) %collective-permute-start.7) | collective-permute-done | bytes 1048608 | tf_op jit(solution)/shard_map/ppermute | solution.py:57
  129.9 12.0 %collective-permute-done.12.refs_4_ = bf16[128,2048]{1,0:T(8,128)(2,1)S(1)} collective-permute-done((bf16[128,2048]{1,0:T(8,128)(2,1)S(1)}, bf16[128,2048]{1,0:T(8,128)(2,1)S(1)}, u32[]{:S(2)}, u32[]{:S(2)}) %collective-permute-start.12) | collective-permute-done | bytes 524320 | tf_op jit(solution)/shard_map/ppermute | solution.py:57
  155.9 13.6 %project.1 = (bf16[2048,2048]{1,0:T(8,128)(2,1)}, f32[2048,768]{1,0:T(8,128)}) custom-call(bf16[256,2048]{1,0:T(8,128)(2,1)} %fusion.7.refs_0_, bf16[256,2048]{1,0:T(8,128)(2,1)} %copy-done.21, bf16[256,2048]{1,0:T(8,128)(2,1)} %copy-done.20, bf16[128,2048]{1,0:T(8,128)(2,1)} %copy-done.54, bf16[128,2048]{1,0:T(8,128)(2,1)} %copy-done.53, ...), custom_call_target="tpu_custom_call" | custom-call | tf_op jit(solution)/shard_map/project/pallas_call | solution.py:347
  169.5 23.5 %attend.1 = (bf16[2048,768]{1,0:T(8,128)(2,1)}, f32[2048,256]{1,0:T(8,128)S(1)}, f32[2048,128]{1,0:T(8,128)S(1)}, f32[2,2048]{1,0:T(2,128)S(1)}) custom-call(s32[2,5]{1,0:T(2,128)S(1)} %pad_add_fusion.info, f32[2048,768]{1,0:T(8,128)} %get-tuple-element.233.proj, f32[1024,512]{1,0:T(8,128)} %concatenate.57.tables, ...), custom_call_target="tpu_custom_call" | custom-call | tf_op jit(solution)/shard_map/attend/pallas_call | solution.py:649
  222.7 8.9 %out_own.1 = (bf16[2048,256]{1,0:T(8,128)(2,1)}, bf16[512,1024]{1,0:T(8,128)(2,1)}, bf16[512,1024]{1,0:T(8,128)(2,1)}, f32[256,2048]{1,0:T(8,128)}, f32[256,1024]{1,0:T(8,128)}, /*index=5*/f32[256,1024]{1,0:T(8,128)}) custom-call(f32[2048,256]{1,0:T(8,128)} %copy-done, ...), custom_call_target="tpu_custom_call", output_to_operand_aliasing={{0}: (9, {})} | custom-call | tf_op jit(solution)/shard_map/out_own/pallas_call | solution.py:487
  233.0 24.1 %collective-permute-done.23 = bf16[512,1024]{1,0:T(8,128)(2,1)S(1)} collective-permute-done((bf16[512,1024]{1,0:T(8,128)(2,1)}, bf16[512,1024]{1,0:T(8,128)(2,1)S(1)}, u32[]{:S(2)}, u32[]{:S(2)}) %collective-permute-start.23) | collective-permute-done | bytes 1048608 | tf_op jit(solution)/shard_map/ppermute | solution.py:57
  261.0 11.6 %collective-permute-done.26 = bf16[256,1024]{1,0:T(8,128)(2,1)S(1)} collective-permute-done((bf16[256,1024]{1,0:T(8,128)(2,1)S(1)}, bf16[256,1024]{1,0:T(8,128)(2,1)S(1)}, u32[]{:S(2)}, u32[]{:S(2)}) %collective-permute-start.26) | collective-permute-done | bytes 524320 | tf_op jit(solution)/shard_map/ppermute | solution.py:57
  279.1 21.0 %collective-permute-done.28.refs_2_ = bf16[256,2048]{1,0:T(8,128)(2,1)} collective-permute-done((bf16[256,2048]{1,0:T(8,128)(2,1)}, bf16[256,2048]{1,0:T(8,128)(2,1)}, u32[]{:S(2)}, u32[]{:S(2)}) %collective-permute-start.28) | collective-permute-done | bytes 1048608 | tf_op jit(solution)/shard_map/ppermute | solution.py:57
  305.4 12.7 %collective-permute-done.33.refs_4_ = bf16[128,2048]{1,0:T(8,128)(2,1)S(1)} collective-permute-done((bf16[128,2048]{1,0:T(8,128)(2,1)S(1)}, bf16[128,2048]{1,0:T(8,128)(2,1)S(1)}, u32[]{:S(2)}, u32[]{:S(2)}) %collective-permute-start.33) | collective-permute-done | bytes 524320 | tf_op jit(solution)/shard_map/ppermute | solution.py:57
  323.5 20.1 %up.1 = (bf16[2048,2048]{1,0:T(8,128)(2,1)}, f32[2048,1024]{1,0:T(8,128)}, f32[2048,1024]{1,0:T(8,128)}, f32[2,2048]{1,0:T(2,128)}) custom-call(bf16[256,2048]{1,0:T(8,128)(2,1)} %add_convert_fusion.refs_0_, bf16[256,2048]{1,0:T(8,128)(2,1)} %collective-permute-done.27.refs_1_, bf16[256,2048]{1,0:T(8,128)(2,1)} %collective-permute-done.28.refs_2_, ...), custom_call_target="tpu_custom_call" | custom-call | tf_op jit(solution)/shard_map/up/pallas_call | solution.py:347
  361.5 10.8 %collective-permute-done.42.refs_4_ = bf16[128,2048]{1,0:T(8,128)(2,1)} collective-permute-done((bf16[128,2048]{1,0:T(8,128)(2,1)}, bf16[128,2048]{1,0:T(8,128)(2,1)}, u32[]{:S(2)}, u32[]{:S(2)}) %collective-permute-start.42) | collective-permute-done | bytes 524320 | tf_op jit(solution)/shard_map/ppermute | solution.py:57
  376.3 21.4 %down_back.1 = (bf16[2048,2048]{1,0:T(8,128)(2,1)}, f32[2048,1024]{1,0:T(8,128)}, f32[2,2048]{1,0:T(2,128)}, f32[2,1024]{1,0:T(2,128)}, bf16[2048,1024]{1,0:T(8,128)(2,1)}) custom-call(bf16[256,2048]{1,0:T(8,128)(2,1)} %collective-permute-done.15.refs_0_, bf16[256,2048]{1,0:T(8,128)(2,1)} %collective-permute-done.36.refs_1_, ...), custom_call_target="tpu_custom_call" | custom-call | tf_op jit(solution)/shard_map/down_back/pallas_call | solution.py:347
  405.2 14.0 %convolution_convert_fusion.1 = bf16[2048,1024]{1,0:T(8,128)(2,1)} fusion(bf16[2048,2048]{1,0:T(8,128)(2,1)} %get-tuple-element.294, bf16[2048,1024]{1,0:T(8,128)(2,1)} %get-tuple-element.306.refs_0_), kind=kOutput, calls=%fused_computation.1 | convolution fusion | flops 8592031744 | bytes 16777216 | tf_op jit(solution)/shard_map/dot_general | solution.py:233
  420.1 13.3 %up_back_other.1 = (bf16[2048,1024]{1,0:T(8,128)(2,1)}, bf16[256,2048]{1,0:T(8,128)(2,1)}, bf16[256,2048]{1,0:T(8,128)(2,1)}, bf16[256,2048]{1,0:T(8,128)(2,1)}, bf16[256,2048]{1,0:T(8,128)(2,1)}) custom-call(f32[2048,1024]{1,0:T(8,128)} %get-tuple-element.291.refs_0_, f32[2048,1024]{1,0:T(8,128)} %get-tuple-element.287.refs_11_.refs_1_, ...), custom_call_target="tpu_custom_call" | custom-call | tf_op jit(solution)/shard_map/up_back_other/pallas_call | solution.py:487
  441.8 15.4 %up_back_own.1 = (bf16[2048,1024]{1,0:T(8,128)(2,1)}, bf16[512,1024]{1,0:T(8,128)(2,1)}, bf16[512,1024]{1,0:T(8,128)(2,1)}, f32[256,2048]{1,0:T(8,128)}, f32[256,1024]{1,0:T(8,128)}, /*index=5*/f32[256,1024]{1,0:T(8,128)}) custom-call(f32[2048,1024]{1,0:T(8,128)} %get-tuple-element.291.refs_0_, ...), custom_call_target="tpu_custom_call", output_to_operand_aliasing={{0}: (11, {})} | custom-call | tf_op jit(solution)/shard_map/up_back_own/pallas_call | solution.py:487
  458.9 14.1 %convolution_convert_fusion = bf16[2048,1024]{1,0:T(8,128)(2,1)} fusion(bf16[2048,2048]{1,0:T(8,128)(2,1)} %get-tuple-element.304, bf16[2048,1024]{1,0:T(8,128)(2,1)} %get-tuple-element.305), kind=kOutput, calls=%fused_computation | convolution fusion | flops 8592031744 | bytes 16777216 | tf_op jit(solution)/shard_map/dot_general | solution.py:233
  473.0 9.8 %collective-permute-done.55 = bf16[512,1024]{1,0:T(8,128)(2,1)} collective-permute-done((bf16[512,1024]{1,0:T(8,128)(2,1)}, bf16[512,1024]{1,0:T(8,128)(2,1)}, u32[]{:S(2)}, u32[]{:S(2)}) %collective-permute-start.55) | collective-permute-done | bytes 1048608 | tf_op jit(solution)/shard_map/ppermute | solution.py:57
  490.1 10.5 %down_other.1 = (bf16[256,2048]{1,0:T(8,128)(2,1)}, bf16[256,2048]{1,0:T(8,128)(2,1)}, bf16[256,2048]{1,0:T(8,128)(2,1)}, bf16[256,2048]{1,0:T(8,128)(2,1)}) custom-call(bf16[2048,1024]{1,0:T(8,128)(2,1)} %get-tuple-element.306.refs_0_, bf16[2048,1024]{1,0:T(8,128)(2,1)} %all-gather.8.cloned.1.call-done.refs_10_.refs_1_), custom_call_target="tpu_custom_call" | custom-call | tf_op jit(solution)/shard_map/down_other/pallas_call | solution.py:487
  511.3 12.4 %down_own.1 = (bf16[512,1024]{1,0:T(8,128)(2,1)}, bf16[512,1024]{1,0:T(8,128)(2,1)}, f32[256,2048]{1,0:T(8,128)}, f32[256,1024]{1,0:T(8,128)}, f32[256,1024]{1,0:T(8,128)}) custom-call(bf16[2048,1024]{1,0:T(8,128)(2,1)} %get-tuple-element.306.refs_0_, bf16[2048,1024]{1,0:T(8,128)(2,1)} %all-gather.8.cloned.1.call-done.refs_10_.refs_1_, ...), custom_call_target="tpu_custom_call" | custom-call | tf_op jit(solution)/shard_map/down_own/pallas_call | solution.py:487
  523.7 9.4 %collective-permute-done.64.refs_2_ = bf16[256,2048]{1,0:T(8,128)(2,1)S(1)} collective-permute-done((bf16[256,2048]{1,0:T(8,128)(2,1)S(1)}, bf16[256,2048]{1,0:T(8,128)(2,1)S(1)}, u32[]{:S(2)}, u32[]{:S(2)}) %collective-permute-start.64) | collective-permute-done | bytes 1048608 | tf_op jit(solution)/shard_map/ppermute | solution.py:57
  536.5 12.4 %collective-permute-done.69.refs_4_ = bf16[128,2048]{1,0:T(8,128)(2,1)S(1)} collective-permute-done((bf16[128,2048]{1,0:T(8,128)(2,1)S(1)}, bf16[128,2048]{1,0:T(8,128)(2,1)S(1)}, u32[]{:S(2)}, u32[]{:S(2)}) %collective-permute-start.69) | collective-permute-done | bytes 524320 | tf_op jit(solution)/shard_map/ppermute | solution.py:57
  557.9 12.8 %out_back.1 = (bf16[2048,2048]{1,0:T(8,128)(2,1)}, f32[2048,256]{1,0:T(8,128)}, f32[2,2048]{1,0:T(2,128)}, f32[2,256]{1,0:T(2,128)}) custom-call(bf16[256,2048]{1,0:T(8,128)(2,1)} %copy-done.15, bf16[256,2048]{1,0:T(8,128)(2,1)} %copy-done.23, bf16[256,2048]{1,0:T(8,128)(2,1)} %copy-done.22, bf16[128,2048]{1,0:T(8,128)(2,1)} %copy-done.59, ...), custom_call_target="tpu_custom_call" | custom-call | tf_op jit(solution)/shard_map/out_back/pallas_call | solution.py:347
  579.6 7.3 convolution_convert_fusion.3
  589.6 29.7 %attend_back.1.refs_0_ = bf16[2048,768]{1,0:T(8,128)(2,1)} custom-call(s32[2,5]{1,0:T(2,128)S(1)} %pad_add_fusion.info, bf16[2048,768]{1,0:T(8,128)(2,1)} %get-tuple-element.365.qkv, f32[2048,256]{1,0:T(8,128)S(1)} %copy-done.1, f32[2048,256]{1,0:T(8,128)} %get-tuple-element.366.grad, f32[2,2048]{1,0:T(2,128)S(1)} %copy-done.4, ...), custom_call_target="tpu_custom_call" | custom-call | tf_op jit(solution)/shard_map/attend_back/pallas_call | solution.py:683
  631.6 10.6 %convolution_convert_fusion.2 = bf16[2048,768]{1,0:T(8,128)(2,1)} fusion(bf16[2048,2048]{1,0:T(8,128)(2,1)} %get-tuple-element.371, bf16[2048,768]{1,0:T(8,128)(2,1)S(1)} %copy-done.11), kind=kOutput, calls=%fused_computation.2 | convolution fusion | flops 6444023808 | bytes 14680064 | tf_op jit(solution)/shard_map/dot_general | solution.py:233
  654.1 8.6 %project_back_other.1 = (bf16[256,2048]{1,0:T(8,128)(2,1)}, bf16[256,2048]{1,0:T(8,128)(2,1)}, bf16[256,2048]{1,0:T(8,128)(2,1)}, bf16[256,2048]{1,0:T(8,128)(2,1)}) custom-call(bf16[2048,768]{1,0:T(8,128)(2,1)} %attend_back.1.refs_0_, bf16[2048,1024]{1,0:T(8,128)(2,1)} %all-gather.4.cloned.1.call-done.refs_10_.refs_4_.refs_1_), custom_call_target="tpu_custom_call" | custom-call | tf_op jit(solution)/shard_map/project_back_other/pallas_call | solution.py:487
  671.1 10.8 %project_back_own.1 = (bf16[512,1024]{1,0:T(8,128)(2,1)}, bf16[512,1024]{1,0:T(8,128)(2,1)}, f32[256,2048]{1,0:T(8,128)}, f32[256,1024]{1,0:T(8,128)}, f32[256,1024]{1,0:T(8,128)}) custom-call(bf16[2048,768]{1,0:T(8,128)(2,1)} %attend_back.1.refs_0_, bf16[2048,1024]{1,0:T(8,128)(2,1)} %all-gather.4.cloned.1.call-done.refs_10_.refs_4_.refs_1_, ...), custom_call_target="tpu_custom_call" | custom-call | tf_op jit(solution)/shard_map/project_back_own/pallas_call | solution.py:487
  683.8 23.5 %collective-permute-done.84 = bf16[512,1024]{1,0:T(8,128)(2,1)S(1)} collective-permute-done((bf16[512,1024]{1,0:T(8,128)(2,1)}, bf16[512,1024]{1,0:T(8,128)(2,1)S(1)}, u32[]{:S(2)}, u32[]{:S(2)}) %collective-permute-start.84) | collective-permute-done | bytes 1048608 | tf_op jit(solution)/shard_map/ppermute | solution.py:57
  733.0 8.2 %collective-permute-start.89 = (f32[4,2048]{1,0:T(4,128)S(1)}, f32[4,2048]{1,0:T(4,128)S(1)}, u32[]{:S(2)}, u32[]{:S(2)}) collective-permute-start(f32[4,2048]{1,0:T(4,128)S(1)} %pad_maximum_fusion.7), channel_id=1, source_target_pairs={{0,1},{1,0},{2,3},{3,2},{4,5},{5,4},{6,7},{7,6},{8,9},{9,8},{10,11... | collective-permute-start | bytes 98312 | tf_op jit(solution)/shard_map/ppermute | solution.py:57
  741.2 12.7 %collective-permute-done.89 = f32[4,2048]{1,0:T(4,128)S(1)} collective-permute-done((f32[4,2048]{1,0:T(4,128)S(1)}, f32[4,2048]{1,0:T(4,128)S(1)}, u32[]{:S(2)}, u32[]{:S(2)}) %collective-permute-start.89) | collective-permute-done | bytes 32800 | tf_op jit(solution)/shard_map/ppermute | solution.py:57
  788.6 12.1 %all-to-all-done.4 = bf16[8,64,768]{2,1,0:T(8,128)(2,1)S(1)} async-done(((bf16[8,64,768]{2,1,0:T(8,128)(2,1)}), bf16[8,64,768]{2,1,0:T(8,128)(2,1)S(1)}, u32[]{:S(2)}, u32[]{:S(2)}) %all-to-all-start.4) | async-done | bytes 786464 | tf_op jit(solution)/shard_map/all_to_all | solution.py:155
  (552 shorter events, 327.4 us)
Async XLA Ops:
  12.6 25.0 %collective-permute-start.1 = (f32[1,896]{1,0:T(1,128)S(1)}, f32[1,896]{1,0:T(1,128)S(1)}, u32[]{:S(2)}, u32[]{:S(2)}) collective-permute-start(f32[1,896]{1,0:T(1,128)S(1)} %reshape.399), channel_id=1, source_target_pairs={{0,1},{1,0},{2,3},{3,2},{4,5},{5,4},{6,7},{7,6},{8,9},{9,8},{10,11... | collective-permute-start | bytes 10760 | tf_op jit(solution)/shard_map/ppermute | solution.py:57
  19.0 38.9 %all-to-all-start = ((bf16[8,64,1024]{2,1,0:T(8,128)(2,1)}), bf16[8,64,1024]{2,1,0:T(8,128)(2,1)}, u32[]{:S(2)}, u32[]{:S(2)}) async-start(bf16[8,64,1024]{2,1,0:T(8,128)(2,1)} %pad_maximum_fusion.3), calls=%async_computation | async-start | bytes 2097152 | tf_op jit(solution)/shard_map/all_to_all | solution.py:155
  23.6 132.3 %all-gather.4.cloned.1.call-start = ((), (), s32[]{:S(2)}) async-start(), calls=%async_computation.10 | async-start | bytes 5242880 | tf_op jit(solution)/shard_map/all_gather | solution.py:160
  25.7 32.2 %collective-permute-start = (bf16[256,2048]{1,0:T(8,128)(2,1)}, bf16[256,2048]{1,0:T(8,128)(2,1)S(1)}, u32[]{:S(2)}, u32[]{:S(2)}) collective-permute-start(bf16[256,2048]{1,0:T(8,128)(2,1)} %copy.91), channel_id=1, source_target_pairs={{0,22},{1,30},{2,6},{3,14},{4,12},{5,4},{6,28},{7,20},{8,21},{9,29... | collective-permute-start | bytes 3145736 | tf_op jit(solution)/shard_map/ppermute | solution.py:749
  72.6 28.7 %all-to-all-start.1 = ((bf16[8,64,2048]{2,1,0:T(8,128)(2,1)}), bf16[8,64,2048]{2,1,0:T(8,128)(2,1)S(1)}, u32[]{:S(2)}, u32[]{:S(2)}) async-start(bf16[8,64,2048]{2,1,0:T(8,128)(2,1)} %pad_maximum_fusion), calls=%async_computation.1 | async-start | bytes 4194304 | tf_op jit(solution)/shard_map/all_to_all | solution.py:155
  76.2 247.3 %all-gather.6.cloned.1.call-start = ((), (), s32[]{:S(2)}) async-start(), calls=%async_computation.11 | async-start | bytes 5242880 | tf_op jit(solution)/shard_map/all_gather | solution.py:160
  101.3 23.2 %collective-permute-start.7 = (bf16[256,2048]{1,0:T(8,128)(2,1)}, bf16[256,2048]{1,0:T(8,128)(2,1)S(1)}, u32[]{:S(2)}, u32[]{:S(2)}) collective-permute-start(bf16[256,2048]{1,0:T(8,128)(2,1)} %fusion.7.refs_0_), channel_id=1, source_target_pairs={{0,16},{4,20},{8,24},{12,28},{16,0},{20,4},{24,8},{28,12},{1,17},{... | collective-permute-start | bytes 3145736 | tf_op jit(solution)/shard_map/ppermute | solution.py:57
  102.9 23.9 %collective-permute-start.6 = (bf16[256,2048]{1,0:T(8,128)(2,1)}, bf16[256,2048]{1,0:T(8,128)(2,1)S(1)}, u32[]{:S(2)}, u32[]{:S(2)}) collective-permute-start(bf16[256,2048]{1,0:T(8,128)(2,1)} %fusion.7.refs_0_), channel_id=1, source_target_pairs={{0,8},{4,12},{8,0},{12,4},{16,24},{20,28},{24,16},{28,20},{1,9},{5... | collective-permute-start | bytes 3145736 | tf_op jit(solution)/shard_map/ppermute | solution.py:57
  147.8 47.5 %collective-permute-start.15 = (bf16[256,2048]{1,0:T(8,128)(2,1)}, bf16[256,2048]{1,0:T(8,128)(2,1)}, u32[]{:S(2)}, u32[]{:S(2)}) collective-permute-start(bf16[256,2048]{1,0:T(8,128)(2,1)} %copy.101), channel_id=1, source_target_pairs={{0,22},{1,30},{2,6},{3,14},{4,12},{5,4},{6,28},{7,20},{8,21},{9,29... | collective-permute-start | bytes 3145736 | tf_op jit(solution)/shard_map/ppermute | solution.py:800
  201.8 172.7 %all-gather.8.cloned.1.call-start = ((), (), s32[]{:S(2)}) async-start(), calls=%async_computation.12 | async-start | bytes 5242880 | tf_op jit(solution)/shard_map/all_gather | solution.py:160
  231.6 25.5 %collective-permute-start.23 = (bf16[512,1024]{1,0:T(8,128)(2,1)}, bf16[512,1024]{1,0:T(8,128)(2,1)S(1)}, u32[]{:S(2)}, u32[]{:S(2)}) collective-permute-start(bf16[512,1024]{1,0:T(8,128)(2,1)} %get-tuple-element.248), channel_id=1, source_target_pairs={{0,8},{4,12},{8,0},{12,4},{16,24},{20,28},{24,16},{28,20},{1,9},{5... | collective-permute-start | bytes 3145736 | tf_op jit(solution)/shard_map/ppermute | solution.py:57
  232.9 25.1 %collective-permute-start.24 = (bf16[512,1024]{1,0:T(8,128)(2,1)}, bf16[512,1024]{1,0:T(8,128)(2,1)S(1)}, u32[]{:S(2)}, u32[]{:S(2)}) collective-permute-start(bf16[512,1024]{1,0:T(8,128)(2,1)} %get-tuple-element.249), channel_id=1, source_target_pairs={{0,16},{4,20},{8,24},{12,28},{16,0},{20,4},{24,8},{28,12},{1,17},{... | collective-permute-start | bytes 3145736 | tf_op jit(solution)/shard_map/ppermute | solution.py:57
  276.5 23.7 %collective-permute-start.28 = (bf16[256,2048]{1,0:T(8,128)(2,1)}, bf16[256,2048]{1,0:T(8,128)(2,1)}, u32[]{:S(2)}, u32[]{:S(2)}) collective-permute-start(bf16[256,2048]{1,0:T(8,128)(2,1)} %add_convert_fusion.refs_0_), channel_id=1, source_target_pairs={{0,16},{4,20},{8,24},{12,28},{16,0},{20,4},{24,8},{28,12},{1,17},{... | collective-permute-start | bytes 3145736 | tf_op jit(solution)/shard_map/ppermute | solution.py:57
  277.9 23.1 %collective-permute-start.27 = (bf16[256,2048]{1,0:T(8,128)(2,1)}, bf16[256,2048]{1,0:T(8,128)(2,1)}, u32[]{:S(2)}, u32[]{:S(2)}) collective-permute-start(bf16[256,2048]{1,0:T(8,128)(2,1)} %add_convert_fusion.refs_0_), channel_id=1, source_target_pairs={{0,8},{4,12},{8,0},{12,4},{16,24},{20,28},{24,16},{28,20},{1,9},{5... | collective-permute-start | bytes 3145736 | tf_op jit(solution)/shard_map/ppermute | solution.py:57
  278.7 255.2 %reduce-scatter.5.cloned.1.call-start = ((), (), s32[]{:S(2)}) async-start(), calls=%async_computation.13 | async-start | bytes 5242880 | tf_op jit(solution)/shard_map/reduce_scatter | solution.py:164
  321.3 25.5 %collective-permute-start.37 = (bf16[256,2048]{1,0:T(8,128)(2,1)}, bf16[256,2048]{1,0:T(8,128)(2,1)}, u32[]{:S(2)}, u32[]{:S(2)}) collective-permute-start(bf16[256,2048]{1,0:T(8,128)(2,1)} %collective-permute-done.15.refs_0_), channel_id=1, source_target_pairs={{0,16},{4,20},{8,24},{12,28},{16,0},{20,4},{24,8},{28,12},{1,17},{... | collective-permute-start | bytes 3145736 | tf_op jit(solution)/shard_map/ppermute | solution.py:57
  322.2 25.4 %collective-permute-start.36 = (bf16[256,2048]{1,0:T(8,128)(2,1)}, bf16[256,2048]{1,0:T(8,128)(2,1)}, u32[]{:S(2)}, u32[]{:S(2)}) collective-permute-start(bf16[256,2048]{1,0:T(8,128)(2,1)} %collective-permute-done.15.refs_0_), channel_id=1, source_target_pairs={{0,8},{4,12},{8,0},{12,4},{16,24},{20,28},{24,16},{28,20},{1,9},{5... | collective-permute-start | bytes 3145736 | tf_op jit(solution)/shard_map/ppermute | solution.py:57
  419.9 199.5 %reduce-scatter.7.cloned.1.call-start = ((), (), s32[]{:S(2)}) async-start(), calls=%async_computation.14 | async-start | bytes 5242880 | tf_op jit(solution)/shard_map/reduce_scatter | solution.py:164
  457.2 25.6 %collective-permute-start.55 = (bf16[512,1024]{1,0:T(8,128)(2,1)}, bf16[512,1024]{1,0:T(8,128)(2,1)}, u32[]{:S(2)}, u32[]{:S(2)}) collective-permute-start(bf16[512,1024]{1,0:T(8,128)(2,1)} %get-tuple-element.302), channel_id=1, source_target_pairs={{0,8},{4,12},{8,0},{12,4},{16,24},{20,28},{24,16},{28,20},{1,9},{5... | collective-permute-start | bytes 3145736 | tf_op jit(solution)/shard_map/ppermute | solution.py:57
  458.1 25.3 %collective-permute-start.56 = (bf16[512,1024]{1,0:T(8,128)(2,1)}, bf16[512,1024]{1,0:T(8,128)(2,1)}, u32[]{:S(2)}, u32[]{:S(2)}) collective-permute-start(bf16[512,1024]{1,0:T(8,128)(2,1)} %get-tuple-element.303), channel_id=1, source_target_pairs={{0,16},{4,20},{8,24},{12,28},{16,0},{20,4},{24,8},{28,12},{1,17},{... | collective-permute-start | bytes 3145736 | tf_op jit(solution)/shard_map/ppermute | solution.py:57
  508.1 25.1 %collective-permute-start.64 = (bf16[256,2048]{1,0:T(8,128)(2,1)S(1)}, bf16[256,2048]{1,0:T(8,128)(2,1)S(1)}, u32[]{:S(2)}, u32[]{:S(2)}) collective-permute-start(bf16[256,2048]{1,0:T(8,128)(2,1)S(1)} %get-tuple-element.343.refs_0_), channel_id=1, source_target_pairs={{0,16},{4,20},{8,24},{12,28},{16,0},{20,4},{24,8},{28,12},{1,17},{... | collective-permute-start | bytes 3145736 | tf_op jit(solution)/shard_map/ppermute | solution.py:57
  509.2 24.6 %collective-permute-start.63 = (bf16[256,2048]{1,0:T(8,128)(2,1)S(1)}, bf16[256,2048]{1,0:T(8,128)(2,1)S(1)}, u32[]{:S(2)}, u32[]{:S(2)}) collective-permute-start(bf16[256,2048]{1,0:T(8,128)(2,1)S(1)} %get-tuple-element.343.refs_0_), channel_id=1, source_target_pairs={{0,8},{4,12},{8,0},{12,4},{16,24},{20,28},{24,16},{28,20},{1,9},{5... | collective-permute-start | bytes 3145736 | tf_op jit(solution)/shard_map/ppermute | solution.py:57
  557.9 199.8 %reduce-scatter.11.cloned.1.call-start = ((), (), s32[]{:S(2)}) async-start(), calls=%async_computation.16 | async-start | bytes 1310720 | tf_op jit(solution)/shard_map/reduce_scatter | solution.py:164
  587.1 32.3 %collective-permute-start.75 = (bf16[512,1024]{1,0:T(8,128)(2,1)}, bf16[512,1024]{1,0:T(8,128)(2,1)}, u32[]{:S(2)}, u32[]{:S(2)}) collective-permute-start(bf16[512,1024]{1,0:T(8,128)(2,1)} %get-tuple-element.363), channel_id=1, source_target_pairs={{0,8},{4,12},{8,0},{12,4},{16,24},{20,28},{24,16},{28,20},{1,9},{5... | collective-permute-start | bytes 3145736 | tf_op jit(solution)/shard_map/ppermute | solution.py:57
  587.6 31.7 %collective-permute-start.76 = (bf16[512,1024]{1,0:T(8,128)(2,1)}, bf16[512,1024]{1,0:T(8,128)(2,1)}, u32[]{:S(2)}, u32[]{:S(2)}) collective-permute-start(bf16[512,1024]{1,0:T(8,128)(2,1)} %get-tuple-element.364), channel_id=1, source_target_pairs={{0,16},{4,20},{8,24},{12,28},{16,0},{20,4},{24,8},{28,12},{1,17},{... | collective-permute-start | bytes 3145736 | tf_op jit(solution)/shard_map/ppermute | solution.py:57
  619.3 34.7 %all-to-all-start.3 = ((bf16[8,64,1024]{2,1,0:T(8,128)(2,1)}), bf16[8,64,1024]{2,1,0:T(8,128)(2,1)}, u32[]{:S(2)}, u32[]{:S(2)}) async-start(bf16[8,64,1024]{2,1,0:T(8,128)(2,1)} %bitcast.131), calls=%async_computation.5 | async-start | bytes 2097152 | tf_op jit(solution)/shard_map/all_to_all | solution.py:155
  624.9 132.9 %reduce-scatter.9.cloned.1.call-start = ((), (), s32[]{:S(2)}) async-start(), calls=%async_computation.15 | async-start | bytes 3932160 | tf_op jit(solution)/shard_map/reduce_scatter | solution.py:164
  681.9 25.4 %collective-permute-start.84 = (bf16[512,1024]{1,0:T(8,128)(2,1)}, bf16[512,1024]{1,0:T(8,128)(2,1)S(1)}, u32[]{:S(2)}, u32[]{:S(2)}) collective-permute-start(bf16[512,1024]{1,0:T(8,128)(2,1)} %get-tuple-element.387), channel_id=1, source_target_pairs={{0,8},{4,12},{8,0},{12,4},{16,24},{20,28},{24,16},{28,20},{1,9},{5... | collective-permute-start | bytes 3145736 | tf_op jit(solution)/shard_map/ppermute | solution.py:57
  682.4 25.2 %collective-permute-start.85 = (bf16[512,1024]{1,0:T(8,128)(2,1)}, bf16[512,1024]{1,0:T(8,128)(2,1)S(1)}, u32[]{:S(2)}, u32[]{:S(2)}) collective-permute-start(bf16[512,1024]{1,0:T(8,128)(2,1)} %get-tuple-element.388), channel_id=1, source_target_pairs={{0,16},{4,20},{8,24},{12,28},{16,0},{20,4},{24,8},{28,12},{1,17},{... | collective-permute-start | bytes 3145736 | tf_op jit(solution)/shard_map/ppermute | solution.py:57
  726.6 52.6 %collective-permute-start.79 = (bf16[256,2048]{1,0:T(8,128)(2,1)}, bf16[256,2048]{1,0:T(8,128)(2,1)}, u32[]{:S(2)}, u32[]{:S(2)}) collective-permute-start(bf16[256,2048]{1,0:T(8,128)(2,1)} %fusion.15), channel_id=1, source_target_pairs={{22,0},{30,1},{6,2},{14,3},{12,4},{4,5},{28,6},{20,7},{21,8},{29,9... | collective-permute-start | bytes 3145736 | tf_op jit(solution)/shard_map/ppermute | solution.py:909
  763.6 40.5 %collective-permute-start.88 = (bf16[256,2048]{1,0:T(8,128)(2,1)}, bf16[256,2048]{1,0:T(8,128)(2,1)}, u32[]{:S(2)}, u32[]{:S(2)}) collective-permute-start(bf16[256,2048]{1,0:T(8,128)(2,1)} %fusion.12), channel_id=1, source_target_pairs={{22,0},{30,1},{6,2},{14,3},{12,4},{4,5},{28,6},{20,7},{21,8},{29,9... | collective-permute-start | bytes 3145736 | tf_op jit(solution)/shard_map/ppermute | solution.py:920
  769.4 31.3 %all-to-all-start.4 = ((bf16[8,64,768]{2,1,0:T(8,128)(2,1)}), bf16[8,64,768]{2,1,0:T(8,128)(2,1)S(1)}, u32[]{:S(2)}, u32[]{:S(2)}) async-start(bf16[8,64,768]{2,1,0:T(8,128)(2,1)} %bitcast.137), calls=%async_computation.8 | async-start | bytes 1572864 | tf_op jit(solution)/shard_map/all_to_all | solution.py:155
  (143 other events, 1538.4 us)
Sparse Core Ops, SparseCore 0:
  58.0 88.1 all-gather.3
  201.9 85.7 all-gather.5
  289.3 79.2 all-gather.7
  420.0 81.8 reduce-scatter.4
  504.1 77.2 reduce-scatter.6
  588.4 33.4 reduce-scatter.10
  654.2 65.6 reduce-scatter.8

commit v3 on v2

--- a/solution.py
+++ b/solution.py
@@ -121,14 +121,15 @@
         )
         total, *others = sync(total, *others)
         return total.astype(WIDE), others
-    over_x, over_y, near, at_x, at_y = kept
+    over_x, far_y, over_y, near, at_x, at_y = kept
     slots, half = at_x.shape
-    over_x, over_y = swap_over(over_x, "batch", 2, 8), swap_over(over_y, "batch", 4, 8)
-    over_x, over_y, *others = sync(over_x, over_y, *others)
-    to_x = (at_x + over_y[:slots].astype(WIDE)).astype(LOW)
+    over_x, far_y = swap_over(over_x, "batch", 2, 8), swap_over(far_y, "batch", 4, 8)
+    over_y = swap_over(over_y, "batch", 4, 8)
+    over_x, far_y, over_y, *others = sync(over_x, far_y, over_y, *others)
+    to_x = (at_x + far_y.astype(WIDE)).astype(LOW)
     to_y = (at_y + over_x[:slots].astype(WIDE)).astype(LOW)
     first = near[:, :half] + over_x[slots:].astype(WIDE)
-    second = near[:, half:] + over_y[slots:].astype(WIDE)
+    second = near[:, half:] + over_y.astype(WIDE)
     return (first, second, to_x, to_y), others
 
 
@@ -166,16 +167,35 @@
     return own.reshape(plan.nb, rows // plan.nb, width)
 
 
-def to_inner(plan, values):
+def reorder_kernel(values, out, *, sources):
+    low = lax.broadcasted_iota(jnp.int32, (values.shape[0], 128), 1) < 64
+    for at, (first, second, half) in enumerate(sources):
+        a = values[:, first * 128 : first * 128 + 128].astype(WIDE)
+        b = values[:, second * 128 : second * 128 + 128].astype(WIDE)
+        if half:
+            a = pltpu.roll(a, 64, 1)
+        else:
+            b = pltpu.roll(b, 64, 1)
+        out[:, at * 128 : at * 128 + 128] = jnp.where(low, a, b).astype(out.dtype)
+
+
+def reorder(plan, values, outward, dtype):
     count, width = values.shape
-    values = values.reshape(count, plan.nb, plan.ns, width // (plan.nb * plan.ns))
-    return values.transpose(0, 2, 1, 3).reshape(count, width)
-
-
-def to_outer(plan, values):
-    count, width = values.shape
-    values = values.reshape(count, plan.ns, plan.nb, width // (plan.nb * plan.ns))
-    return values.transpose(0, 2, 1, 3).reshape(count, width)
+    sizes = (plan.ns, plan.nb) if outward else (plan.nb, plan.ns)
+    if width != plan.nb * plan.ns * 64 or sizes[0] % 2 or sizes[1] % 2:
+        values = values.reshape(count, *sizes, width // (plan.nb * plan.ns))
+        return values.transpose(0, 2, 1, 3).reshape(count, width).astype(dtype)
+    sources = []
+    for inner in range(sizes[1]):
+        for outer in range(0, sizes[0], 2):
+            at = outer * sizes[1] + inner
+            sources.append((at // 2, (at + sizes[1]) // 2, at % 2))
+    return pl.pallas_call(
+        functools.partial(reorder_kernel, sources=sources),
+        out_shape=jax.ShapeDtypeStruct(values.shape, dtype),
+        compiler_params=pltpu.CompilerParams(vmem_limit_bytes=48 << 20),
+        name="reorder",
+    )(values)
 
 
 def norm_stats(values):
@@ -212,16 +232,14 @@
 
 def xpos_tables(length):
     slot_pos = (jnp.arange(length, dtype=jnp.int32) - length // 2).astype(WIDE)
-    index = jnp.arange(32, dtype=jnp.int32).astype(WIDE)
+    lane = jnp.arange(128, dtype=jnp.int32)
+    index = (lane % 32).astype(WIDE)
     angle = slot_pos[:, None] * jnp.exp(index * (-jnp.log(10000.0) / 32.0))[None, :]
     zeta = (index / 32.0 + 0.4) / 1.4
     growth = jnp.exp(slot_pos[:, None] * jnp.log(zeta)[None, :] / 512.0)
     cosine, sine = jnp.cos(angle), jnp.sin(angle)
-    tables = []
-    for scale in (growth, 1.0 / growth):
-        tables += [cosine * scale] * 4
-        tables += [-sine * scale, sine * scale] * 2
-    return jnp.concatenate(tables, axis=1)
+    sine = jnp.where(lane % 64 < 32, -sine, sine)
+    return cosine * growth, sine * growth, cosine / growth, sine / growth
 
 
 def swap_halves(values):
@@ -321,14 +339,19 @@
             pltpu.make_async_copy(weight, kept, stored.at[0]).wait()
 
 
-def pieces_matmul(arrays, weights, columns, end, extra, outs, name):
-    step = ROWS_AT_ONCE
+def moves_of(arrays, step):
     moves, total = [], 0
     for index, array in enumerate(arrays):
         for first in range(0, array.shape[0], step):
             n = min(step, array.shape[0] - first)
             moves.append((index, first, total, n))
             total += n
+    return moves, total
+
+
+def pieces_matmul(arrays, weights, columns, end, extra, outs, name):
+    step = ROWS_AT_ONCE
+    moves, total = moves_of(arrays, step)
     loads, inner = [], 0
     for index, weight in enumerate(weights):
         loads.append((index, columns[0], inner, weight.shape[0]))
@@ -393,100 +416,95 @@
     return values[...]
 
 
-def part_kernel(*refs, n_in, make_left, keeps, own, split):
-    weight = refs[n_in]
+def part_kernel(*refs, n_in, make_left, keeps, ends):
+    n_more = len(ends[1])
     left = make_left(*refs[:n_in])
-    acc = matmul(left, weight[...], (1, 1))
-    outs = refs[n_in + 1 :]
-    others = outs[:4]
-    if own:
-        outs = outs[5:] if keeps else outs[4:]
+    acc = matmul(left, refs[n_in][...], (1, 1))
+    more, outs = refs[n_in + 1 : n_in + 1 + n_more], refs[n_in + 1 + n_more :]
     if keeps:
-        outs[0][...] = left
-        outs = outs[1:]
-    block = pl.program_id(0)
-    if not own:
-        if not split:
-            outs[0][...] = acc.astype(LOW)
-            return
-        for i, out in enumerate(outs):
-
-            @pl.when(block == i)
-            def _(out=out):
-                out[...] = acc.astype(LOW)
-
+        outs[0 if ends[2] else 1][...] = left
+        outs = outs[1:] if ends[2] else outs[2:]
+    ends[0](acc, pl.program_id(0), *more, *outs)
+
+
+def other_end(acc, block, *outs):
+    if len(outs) == 1:
+        outs[0][...] = acc.astype(LOW)
         return
-    over_x, over_y, near, at_x, at_y = outs
+    for i, out in enumerate(outs):
+
+        @pl.when(block == i)
+        def _(out=out):
+            out[...] = acc.astype(LOW)
+
+
+def own_x_end(acc, block, from_x, from_far, over_x, far_y, at_x):
     slots, half = at_x.shape
 
     @pl.when(block == 0)
     def _():
-        near[...] = acc + others[0][...].astype(WIDE)
-
-    @pl.when(block == 1)
-    def _():
-        total = acc + others[1][...].astype(WIDE)
+        total = acc + from_x[...].astype(WIDE)
         over_x[slots:] = total[:, :half].astype(LOW)
         at_x[...] = total[:, half:]
 
-    @pl.when(block == 2)
-    def _():
-        total = acc + others[2][...].astype(WIDE)
-        over_y[slots:] = total[:, half:].astype(LOW)
+    @pl.when(block == 1)
+    def _():
+        total = acc + from_far[...].astype(WIDE)
+        over_x[:slots] = total[:, :half].astype(LOW)
+        far_y[...] = total[:, half:].astype(LOW)
+
+
+def own_y_end(acc, block, from_near, from_y, over_y, near, at_y):
+    half = at_y.shape[1]
+
+    @pl.when(block == 0)
+    def _():
+        near[...] = acc + from_near[...].astype(WIDE)
+
+    @pl.when(block == 1)
+    def _():
+        total = acc + from_y[...].astype(WIDE)
+        over_y[...] = total[:, half:].astype(LOW)
         at_y[...] = total[:, :half]
 
-    @pl.when(block == 3)
-    def _():
-        total = acc + others[3][...].astype(WIDE)
-        over_x[:slots] = total[:, :half].astype(LOW)
-        over_y[:slots] = total[:, half:].astype(LOW)
-
-
-def part_call(plan, ins, weight, columns, make_left, keeps, first, blocks, name, others=(), kept=()):
+
+def part_call(ins, weight, columns, make_left, kept, at, blocks, end, more, outs, name):
     step = ROWS_AT_ONCE
     total = next(array.shape[0] for array, kind in ins if kind == "rows")
-    rows, own = weight.shape[0], len(others) > 0
+    rows = weight.shape[0]
 
     def spec(array, kind):
         if kind == "rows":
-            return pl.BlockSpec((step, array.shape[1]), lambda i: (first + i, 0))
+            return pl.BlockSpec((step, array.shape[1]), lambda i: (at(i), 0))
         if kind == "lanes":
-            return pl.BlockSpec((array.shape[0], step), lambda i: (0, first + i))
+            return pl.BlockSpec((array.shape[0], step), lambda i: (0, at(i)))
         return pl.BlockSpec(array.shape, lambda i: (0, 0))
 
+    once = pl.Buffered(1)
     in_specs = [spec(*item) for item in ins]
     in_specs.append(
-        pl.BlockSpec(
-            (rows, columns[0]), lambda i: (0, columns[1]), pipeline_mode=pl.Buffered(1)
-        )
-    )
-    operands = [array for array, _ in ins] + [weight, *others]
-    in_specs += [
-        pl.BlockSpec((step, rows), lambda i: (0, 0), pipeline_mode=pl.Buffered(1)) for _ in others
-    ]
+        pl.BlockSpec((rows, columns[0]), lambda i: (0, columns[1]), pipeline_mode=once)
+    )
+    in_specs += [pl.BlockSpec(m.shape, lambda i: (0, 0), pipeline_mode=once) for m in more]
+    operands = [array for array, _ in ins] + [weight, *more]
     out_specs, out_shape, aliases = [], [], {}
-    if keeps:
-        if own:
+    if kept is not None:
+        if kept:
             aliases[len(operands)] = 0
             in_specs.append(pl.BlockSpec(memory_space=pl.ANY))
             operands += kept
-        out_specs.append(pl.BlockSpec((step, columns[0]), lambda i: (first + i, 0)))
+        out_specs.append(pl.BlockSpec((step, columns[0]), lambda i: (at(i), 0)))
         out_shape.append(jax.ShapeDtypeStruct((total, columns[0]), LOW))
-    whole = []
-    if own:
-        half = rows // 2
-        whole = [((2 * step, half), LOW)] * 2 + [((step, rows), WIDE)] + [((step, half), WIDE)] * 2
-    elif plan.fast:
-        whole = [((step, rows), LOW)] * blocks
-    else:
-        out_specs.append(pl.BlockSpec((step, rows), lambda i: (i, 0)))
-        out_shape.append(jax.ShapeDtypeStruct((blocks * step, rows), LOW))
-    for shape, kind in whole:
-        out_specs.append(pl.BlockSpec(shape, lambda i: (0, 0)))
-        out_shape.append(jax.ShapeDtypeStruct(shape, kind))
+    for shape, dtype, moves in outs:
+        out_specs.append(pl.BlockSpec((step if moves else shape[0], shape[1]), lambda i, m=moves: (i if m else 0, 0)))
+        out_shape.append(jax.ShapeDtypeStruct(shape, dtype))
     return pl.pallas_call(
         functools.partial(
-            part_kernel, n_in=len(ins), make_left=make_left, keeps=keeps, own=own, split=plan.fast
+            part_kernel,
+            n_in=len(ins),
+            make_left=make_left,
+            keeps=kept is not None,
+            ends=(end, more, not kept),
         ),
         grid=(blocks,),
         in_specs=in_specs,
@@ -499,19 +517,34 @@
 
 
 def block_parts(plan, ins, weight, columns, make_left, keeps, name):
-    total = next(array.shape[0] for array, kind in ins if kind == "rows")
-    blocks = total // ROWS_AT_ONCE
+    step, rows = ROWS_AT_ONCE, weight.shape[0]
+    left = [] if keeps else None
+
+    def call(at, blocks, end, more, outs, name):
+        return part_call(ins, weight, columns, make_left, left, at, blocks, end, more, outs, name)
+
     if not plan.fast:
-        *left, part = part_call(plan, ins, weight, columns, make_left, keeps, 0, blocks, name)
-        return *left, part
-    half = blocks // 2
-    outs = part_call(plan, ins, weight, columns, make_left, keeps, half, half, name + "_other")
-    left, parts = outs[: int(keeps)], outs[int(keeps) :]
-    others = [swap_over(part, "batch", 1, 8) for part in parts]
-    outs = part_call(
-        plan, ins, weight, columns, make_left, keeps, 0, half, name + "_own", others, left
-    )
-    return *outs[: int(keeps)], outs[int(keeps) :]
+        total = next(array.shape[0] for array, kind in ins if kind == "rows")
+        outs = [((total, rows), LOW, True)]
+        return call(lambda i: i, total // step, other_end, [], outs, name)
+    half = rows // 2
+    outs = [((step, rows), LOW, False)] * 4
+    outs = call(lambda i: 4 + i, 4, other_end, [], outs, name + "_other")
+    if keeps:
+        left = [outs[0]]
+    near, at_x, at_y, far = outs[int(keeps) :]
+    others = [swap_over(part, "batch", 1, 8) for part in (at_x, far, near, at_y)]
+    outs = [((2 * step, half), LOW, False), ((step, half), LOW, False), ((step, half), WIDE, False)]
+    outs = call(lambda i: 1 + 2 * i, 2, own_x_end, others[:2], outs, name + "_own_x")
+    if keeps:
+        left = [outs[0]]
+    over_x, far_y, at_x = outs[int(keeps) :]
+    outs = [((step, half), LOW, False), ((step, rows), WIDE, False), ((step, half), WIDE, False)]
+    outs = call(lambda i: 2 * i, 2, own_y_end, others[2:], outs, name + "_own_y")
+    if keeps:
+        left = [outs[0]]
+    over_y, near, at_y = outs[int(keeps) :]
+    return *(left or []), (over_x, far_y, over_y, near, at_x, at_y)
 
 
 def fill_bias(bias, valid, seg_row, seg_col, length):
@@ -526,7 +559,8 @@
 
 
 def attend_kernel(
-    info, proj, tables, seg_row, seg_col, qkv, attended, log_total, stats, bias, *, ns, slots, hd
+    info, proj, cos_q, sin_q, cos_k, sin_k, seg_row, seg_col, qkv, attended, log_total, stats, bias,
+    *, ns, slots, hd
 ):
     row, head = pl.program_id(0), pl.program_id(1)
     length = ns * slots
@@ -538,9 +572,8 @@
     def _():
         for q in range(ns):
             source, low, high = place(q), q * slots, (q + 1) * slots
-            for part in range(2):
-                cosine = tables[low:high, 256 * part : 256 * part + 128]
-                sine = tables[low:high, 256 * part + 128 : 256 * part + 256]
+            for part, (cosine, sine) in enumerate(((cos_q, sin_q), (cos_k, sin_k))):
+                cosine, sine = cosine[low:high], sine[low:high]
                 for pair in range(hd // 128):
                     at = part * hd + pair * 128
                     values = proj[pl.ds(source, slots), at : at + 128]
@@ -576,7 +609,7 @@
 
 
 def attend_back_kernel(
-    info, qkv, attended, grad, stats, sums, gain, log_total, tables, seg_row, seg_col, out,
+    info, qkv, attended, grad, stats, sums, gain, log_total, cos_q, sin_q, cos_k, sin_k, seg_row, seg_col, out,
     bias, grad_low, product, grad_q, grad_k, grad_v, *, ns, slots, hd
 ):
     row, head = pl.program_id(0), pl.program_id(1)
@@ -623,9 +656,9 @@
     def _():
         for q in range(ns):
             target, low, high = place(q), q * slots, (q + 1) * slots
-            for part, total in enumerate((grad_q, grad_k)):
-                cosine = tables[low:high, 256 * part : 256 * part + 128]
-                sine = tables[low:high, 256 * part + 128 : 256 * part + 256]
+            tables = (cos_q, sin_q, grad_q), (cos_k, sin_k, grad_k)
+            for part, (cosine, sine, total) in enumerate(tables):
+                cosine, sine = cosine[low:high], sine[low:high]
                 for pair in range(hd // 128):
                     values = total[low:high, pair * 128 : pair * 128 + 128]
                     turned = values * cosine - swap_halves(values) * sine
@@ -653,7 +686,7 @@
             grid=(plan.rows, hd // HEAD),
             in_specs=[
                 row_block(length, width),
-                shared_block(length, 512),
+                *[shared_block(length, 128)] * 4,
                 pl.BlockSpec((None, 1, length), lambda r, h, info: (r, 0, 0)),
                 pl.BlockSpec((None, length, 1), lambda r, h, info: (r, 0, 0)),
             ],
@@ -673,7 +706,7 @@
         ],
         compiler_params=pltpu.CompilerParams(vmem_limit_bytes=48 << 20),
         name="attend",
-    )(info, proj, tables, segments[:, None, :], segments[:, :, None])
+    )(info, proj, *tables, segments[:, None, :], segments[:, :, None])
 
 
 def attend_back(plan, info, qkv, attended, grad, stats, sums, gain, log_total, tables, segments):
@@ -693,7 +726,7 @@
                 pl.BlockSpec((2, length), lambda r, h, info: (0, r)),
                 shared_block(1, hd),
                 row_block(length, 128),
-                shared_block(length, 512),
+                *[shared_block(length, 128)] * 4,
                 pl.BlockSpec((None, 1, length), lambda r, h, info: (r, 0, 0)),
                 pl.BlockSpec((None, length, 1), lambda r, h, info: (r, 0, 0)),
             ],
@@ -711,7 +744,7 @@
         compiler_params=pltpu.CompilerParams(vmem_limit_bytes=48 << 20),
         name="attend_back",
     )(
-        info, qkv, attended, grad, stats, sums, gain, log_total, tables,
+        info, qkv, attended, grad, stats, sums, gain, log_total, *tables,
         segments[:, None, :], segments[:, :, None],
     )
 
@@ -743,23 +776,18 @@
         jnp.asarray(plan.table), batch_index * ns + seq_index, 0, keepdims=False
     )
 
-    slot = seq_index * slots + jnp.arange(slots, dtype=jnp.int32)
-    living = (slot < valid_count[0])[:, None]
-    grad_low = to_inner(plan, jnp.where(living, cotangent[0], jnp.zeros((), LOW)))
-    tokens_low = lax.ppermute(to_inner(plan, tokens[0]), BOTH, plan.there)
+    tokens_low = reorder(plan, tokens[0], False, LOW)
     group = w_qkv.reshape(w_qkv.shape[0], 3, nb, hd).transpose(2, 0, 1, 3)
     group = group.reshape(nb, -1, 3 * hd)
-    attn_own = exchange(jnp.concatenate([group, split_columns(plan, w_out.T)], axis=2))
-    ffn_own = jnp.concatenate([split_columns(plan, w) for w in (w_up, w_down.T)], axis=2)
+    attn_own = jnp.concatenate([group, split_columns(plan, w_out.T)], axis=2)
+    tokens_low, attn_own = sync(tokens_low, attn_own)
+    attn_own = exchange(attn_own)
+    qkv_w = gather_layers(attn_own[:, :, : 3 * hd])
+    tokens_low = lax.ppermute(tokens_low, BOTH, plan.there)
 
     own_params = (gain_attn, bias_attn, gain_mix, bias_mix, gain_ffn, bias_ffn, gain_hidden, bias_hidden)
+    tokens_low, cotangent, attn_own, *own_params = sync(tokens_low, cotangent, attn_own, *own_params)
     params = gather_over(jnp.concatenate([p.astype(WIDE) for p in own_params]), "seq", ns)
-    tables = xpos_tables(length)
-    tokens_low, attn_own, ffn_own, grad_low, params, tables = sync(
-        tokens_low, attn_own, ffn_own, grad_low, params, tables
-    )
-    attn_w = gather_layers(attn_own)
-    ffn_own = exchange(ffn_own)
     packed = jnp.concatenate(
         [params.reshape(-1), segments[0].astype(WIDE), valid_count.astype(WIDE)]
     )
@@ -774,6 +802,20 @@
         else:
             vectors.append(lax.dynamic_index_in_dim(piece, batch_index, 0, False).reshape(1, -1))
     ga, ba, gm, bm, gf, bf, gh, bh = vectors
+    count = plan.rows * length
+    resid = tokens_low.astype(WIDE)
+    mean_attn, scale_attn = norm_stats(resid)
+    unit_attn = (resid - mean_attn) * scale_attn
+    normed_low = (unit_attn * ga + ba).astype(LOW)
+    normed_low, packed, cotangent, w_up, w_down, gm, bm, gf, bf, gh, bh = sync(
+        normed_low, packed, cotangent, w_up, w_down, gm, bm, gf, bf, gh, bh
+    )
+
+    near = gather_near(plan, normed_low)
+    ffn_own = jnp.concatenate([split_columns(plan, w) for w in (w_up, w_down.T)], axis=2)
+    slot = seq_index * slots + jnp.arange(slots, dtype=jnp.int32)
+    living = (slot < valid_count[0])[:, None]
+    grad_low = reorder(plan, jnp.where(living, cotangent[0], jnp.zeros((), LOW)), False, LOW)
     layer_rows = jnp.concatenate(
         [
             lax.dynamic_slice_in_dim(packed[:, params.size :], entry[r], 1, 0)
@@ -784,23 +826,18 @@
     info = jnp.concatenate(
         [entry[plan.rows :].reshape(plan.rows, ns), layer_rows[:, length:]], axis=1
     )
-    count = plan.rows * length
-    resid = tokens_low.astype(WIDE)
-    mean_attn, scale_attn = norm_stats(resid)
-    unit_attn = (resid - mean_attn) * scale_attn
-    normed_low = (unit_attn * ga + ba).astype(LOW)
-    normed_low, ffn_own, gm, bm, gf, bf, gh, bh = sync(
-        normed_low, ffn_own, gm, bm, gf, bf, gh, bh
-    )
-    up_w = gather_layers(ffn_own[:, :, :hidden_part])
-    down_wt = gather_layers(ffn_own[:, :, hidden_part:])
-
-    near = sync(*gather_near(plan, normed_low))
-    grad_low, *arrays = sync(grad_low, *gather_far(plan, near))
+    out_own = attn_own[:, :, 3 * hd :]
+    ffn_own, grad_low, seg_rows, info, out_own, near = sync(
+        ffn_own, grad_low, seg_rows, info, out_own, near
+    )
+    out_wt = gather_layers(out_own)
+    tables = xpos_tables(length)
+    grad_low, ffn_own, tables, arrays = sync(grad_low, ffn_own, tables, gather_far(plan, near))
+    ffn_own = exchange(ffn_own)
     grad_low = lax.ppermute(grad_low, BOTH, plan.there)
     normed, projected = pieces_matmul(
         arrays,
-        [attn_w],
+        [qkv_w],
         (0, 3 * hd, 3 * hd),
         plain_end,
         [],
@@ -808,13 +845,15 @@
         "project",
     )
     qkv, attended, log_total, stats_mix = attend(plan, info, projected, tables, seg_rows)
-    stats_mix, grad_low = sync(stats_mix, grad_low)
+    stats_mix, grad_low, ffn_own = sync(stats_mix, grad_low, ffn_own)
+    up_w = gather_layers(ffn_own[:, :, :hidden_part])
+    down_wt = gather_layers(ffn_own[:, :, hidden_part:])
     stats_mix = spread_stats(plan, stats_mix, hd)
     mixed, kept = block_parts(
         plan,
         [(attended, "rows"), (stats_mix, "lanes"), (gm, "whole"), (bm, "whole")],
-        attn_w,
-        (hd, 3),
+        out_wt,
+        (hd, 0),
         mixed_left,
         True,
         "out",
@@ -877,16 +916,22 @@
     grad_mid, gain_ffn_part, bias_ffn_part = norm_back(grad_ffn_in, gf, unit_ffn, scale_ffn)
     grad_mid = grad_mid + grad_low.astype(WIDE)
     (kept,) = block_parts(
-        plan, [(hidden_low, "rows")], down_wt, (hidden_part, 0), plain_left, False, "down"
-    )
-    kept, near, grad_down = sync(kept, gather_near(plan, grad_mid.astype(LOW)), grad_down)
+        plan,
+        [(hidden_low, "rows")],
+        down_wt,
+        (hidden_part, 0),
+        plain_left,
+        False,
+        "down",
+    )
+    kept, near = sync(kept, gather_near(plan, grad_mid.astype(LOW)))
     arrays = sync(*gather_far(plan, near))
     grad_down, arrays = sync(grad_down, arrays)
     grad_down = exchange(grad_down)
     mid_all, grad_mixed, sums_mix, vectors_mix = pieces_matmul(
         arrays,
-        [attn_w],
-        (3 * hd, hd, hd),
+        [out_wt],
+        (0, hd, hd),
         norm_back_end,
         [(attended, "rows"), (stats_mix, "lanes"), (gm, "whole"), (bm, "whole")],
         [((count, hd), "rows"), ((2, count), "lanes"), ((2, hd), "whole")],
@@ -895,48 +940,59 @@
     sums_mix, grad_down = sync(sums_mix, grad_down)
     grad_out = matmul(mid_all, mixed, (0, 0)).astype(LOW)
     sums_mix = spread_sums(plan, sums_mix, hd)
-    sums_mix, grad_out, kept = sync(sums_mix, grad_out, kept)
+    sums_mix, grad_out, grad_up, kept = sync(sums_mix, grad_out, grad_up, kept)
     grad_out = scatter_layers(plan, grad_out)
     grad_proj = attend_back(
         plan, info, qkv, attended, grad_mixed, stats_mix, sums_mix, gm, log_total, tables, seg_rows
     )
-    state, (grad_proj, grad_up) = reduce_first(plan, kept, grad_proj, grad_up)
-    grad_up = exchange(grad_up)
+    vectors = jnp.concatenate([vectors_mix, vectors_hid], axis=1)
+    for step in bits(ns)[:1]:
+        vectors = vectors + swap_over(vectors, "seq", step, ns)
+    state, (grad_proj, vectors) = reduce_first(plan, kept, grad_proj, vectors)
+    grad_qkv = matmul(normed, grad_proj, (0, 0)).astype(LOW)
+    grad_proj, grad_qkv, grad_up, grad_out = sync(grad_proj, grad_qkv, exchange(grad_up), grad_out)
+    grad_qkv = scatter_layers(plan, grad_qkv)
     output = (resid_mid + reduce_last(plan, state)).astype(LOW)
-    grad_qkv = matmul(normed, grad_proj, (0, 0)).astype(LOW)
-    grad_proj, grad_qkv, output, grad_up = sync(grad_proj, grad_qkv, output, grad_up)
-    grad_qkv = scatter_layers(plan, grad_qkv)
+    (kept,) = block_parts(
+        plan, [(grad_proj, "rows")], qkv_w, (3 * hd, 0), plain_left, False, "project_back"
+    )
+    for step in bits(ns)[1:]:
+        vectors = vectors + swap_over(vectors, "seq", step, ns)
+    state, (output, vectors) = reduce_first(plan, kept, output, vectors)
     output = lax.ppermute(output, BOTH, plan.back)
-    (kept,) = block_parts(
-        plan, [(grad_proj, "rows")], attn_w, (3 * hd, 0), plain_left, False, "project_back"
-    )
-    state, _ = reduce_first(plan, kept)
     grad_normed = reduce_last(plan, state)
     grad_resid, gain_attn_part, bias_attn_part = norm_back(
         grad_normed, ga, unit_attn, scale_attn
     )
-    grad_tokens = (grad_mid + grad_resid).astype(LOW)
-    grad_tokens, grad_qkv, grad_out = sync(grad_tokens, grad_qkv, grad_out)
+    whole = jnp.stack([gain_ffn_part, bias_ffn_part, gain_attn_part, bias_attn_part])
+    whole = whole.reshape(4, ns, nb, -1).transpose(2, 0, 1, 3).reshape(nb, 1, 4 * hd)
+    grad_tokens, grad_qkv, output = sync((grad_mid + grad_resid).astype(LOW), grad_qkv, output)
     grad_tokens = lax.ppermute(grad_tokens, BOTH, plan.back)
-    grad_qkv, grad_out = exchange(grad_qkv), exchange(grad_out)
-
-    whole = jnp.stack([gain_ffn_part, bias_ffn_part, gain_attn_part, bias_attn_part])
-    whole_sum = sum_over(sum_over(whole, "seq", ns), "batch", nb)
-    whole_sum = whole_sum.reshape(4, nb * ns, -1)
-    own = lax.dynamic_index_in_dim(whole_sum, seq_index * nb + batch_index, 1, False)
-    part_sum = sum_over(jnp.concatenate([vectors_mix, vectors_hid], axis=1), "seq", ns)
-    mixes = lax.dynamic_index_in_dim(part_sum[:, :hd].reshape(2, ns, -1), seq_index, 1, False)
-    hiddens = lax.dynamic_index_in_dim(part_sum[:, hd:].reshape(2, ns, -1), seq_index, 1, False)
-
-    grad_qkv = grad_qkv.reshape(nb, -1, 3, hd).transpose(1, 2, 0, 3)
-    grad_out, grad_up, grad_down = [join_columns(plan, g) for g in (grad_out, grad_up, grad_down)]
+    attn_grads = jnp.concatenate([grad_qkv, grad_out], axis=2)
+    rows = attn_grads.shape[1]
+    whole = jnp.broadcast_to(whole.astype(LOW), (nb, 16, 4 * hd))
+    attn_grads = exchange(jnp.concatenate([attn_grads, whole], axis=1))
+    own = jnp.sum(attn_grads[:, rows].astype(WIDE), axis=0).reshape(4, -1)
+    own = sum_over(own, "seq", ns).reshape(4, ns, -1)
+    own = lax.dynamic_index_in_dim(own, seq_index, 1, False)
+    grad_qkv, grad_out = attn_grads[:, :rows, : 3 * hd], attn_grads[:, :rows, 3 * hd :]
+    mixes = lax.dynamic_index_in_dim(vectors[:, :hd].reshape(2, ns, -1), seq_index, 1, False)
+    hiddens = lax.dynamic_index_in_dim(vectors[:, hd:].reshape(2, ns, -1), seq_index, 1, False)
+    grad_qkv = grad_qkv.reshape(nb, -1, 3, hd).transpose(1, 2, 0, 3).reshape(w_qkv.shape)
+    grad_qkv, grad_out = grad_qkv.astype(WIDE), join_columns(plan, grad_out).astype(WIDE).T
+    grad_up = join_columns(plan, grad_up).astype(WIDE)
+    grad_down = join_columns(plan, grad_down).astype(WIDE).T
+    output = reorder(plan, output, True, LOW)
+    grad_tokens, own, mixes, hiddens, grad_qkv, grad_out, grad_up, grad_down, output = sync(
+        grad_tokens, own, mixes, hiddens, grad_qkv, grad_out, grad_up, grad_down, output
+    )
     return (
-        to_outer(plan, output)[None],
-        to_outer(plan, grad_tokens).astype(WIDE)[None],
-        grad_qkv.reshape(w_qkv.shape).astype(WIDE),
-        grad_out.astype(WIDE).T,
-        grad_up.astype(WIDE),
-        grad_down.astype(WIDE).T,
+        output[None],
+        reorder(plan, grad_tokens, True, WIDE)[None],
+        grad_qkv,
+        grad_out,
+        grad_up,
+        grad_down,
         own[2],
         own[3],
         mixes[0],

time: 832 us -> 806 us (0.969)
  waiting for transfers between devices: 302 us -> 254 us
  starting transfers between devices: 120 us -> 145 us
  local copies, waits for them, and re-layouts: 71.1 us -> 51.9 us
  Pallas kernels: 208 us -> 224 us
    ppermute x92 -> x93, waiting for transfers between devices: 268 us -> 217 us  [swap_over(): return lax.ppermute(value, axis, [(i, i ^ step) for i in range(size)])]
    ppermute x92 -> x93, starting transfers between devices: 77.9 us -> 102 us  [swap_over(): return lax.ppermute(value, axis, [(i, i ^ step) for i in range(size)])]
    pallas_call x8 -> x12, Pallas kernels: 86.5 us -> 97.9 us  [part_call(): pl.pallas_call(functools.partial(part_kernel, n_in=len(ins), make_left=ma...]
    all_to_all x6 -> x5, waiting for transfers between devices: 34.2 us -> 37.4 us  [exchange(): return lax.all_to_all(pieces, 'batch', 0, 0, tiled=True)]
    all_to_all x6 -> x5, starting transfers between devices: 28.8 us -> 26.6 us  [exchange(): return lax.all_to_all(pieces, 'batch', 0, 0, tiled=True)]
    unnamed x139 -> x170, local copies, waits for them, and re-layouts: 22.3 us -> 20.4 us
  transfers between devices with their start and end apart: 109 -> 110, of which waited for: 67 -> 56; matrix products, arithmetic and copies ran while one was open for 17% -> 15% of each run, Pallas kernels for 23% -> 25%
where the time goes in v3:
time: 806 us; the launch traced here: 792 us
  waiting for transfers between devices  254 us (32%)
  Pallas kernels  224 us (28%)
  starting transfers between devices  145 us (18%)
  local copies, waits for them, and re-layouts  51.9 us (6%)
  other arithmetic  48.2 us (6%)
  matrix products  46.7 us (6%)
  between operations  20.9 us (3%)
    ppermute x93, waiting for transfers between devices, swap_over(): return lax.ppermute(value, axis, [(i, i ^ step) for i in range(size)])  217 us
    ppermute x93, starting transfers between devices, swap_over(): return lax.ppermute(value, axis, [(i, i ^ step) for i in range(size)])  102 us
    pallas_call x12, Pallas kernels, part_call(): pl.pallas_call(functools.partial(part_kernel, n_in=len(ins), make_left=ma...  97.9 us
    pallas_call x4, Pallas kernels, pieces_matmul(): pl.pallas_call(functools.partial(pieces_kernel, moves=moves, loads=loads,...  68.5 us
    dot_general x4, matrix products, matmul(): lax.dot_general(a, b, ((contract[:1], contract[1:]), ((), ())), preferred...  46.7 us
    all_to_all x5, waiting for transfers between devices, exchange(): return lax.all_to_all(pieces, 'batch', 0, 0, tiled=True)  37.4 us
    pallas_call x1, Pallas kernels, attend_back(): pl.pallas_call(functools.partial(attend_back_kernel, ns=plan.ns, slots=sl...  29.6 us
    all_to_all x5, starting transfers between devices, exchange(): return lax.all_to_all(pieces, 'batch', 0, 0, tiled=True)  26.6 us
  transfers between devices with their start and end apart: 110, of which 56 were waited for; matrix products, arithmetic and copies ran while one was open for 15% of the time, Pallas kernels for 25%

profile of v3, /device:TPU:4, one launch (start us, length us, event | category | flops | bytes accessed | tf_op | source)
XLA Modules:
  0.0 791.6 jit_solution(6356356908783513537)
XLA Ops:
  24.2 19.5 %all-to-all-done = bf16[8,64,1024]{2,1,0:T(8,128)(2,1)S(1)} async-done(((bf16[8,64,1024]{2,1,0:T(8,128)(2,1)}), bf16[8,64,1024]{2,1,0:T(8,128)(2,1)S(1)}, u32[]{:S(2)}, u32[]{:S(2)}) %all-to-all-start) | async-done | bytes 1048608 | tf_op jit(solution)/shard_map/all_to_all | solution.py:156
  43.9 11.1 %collective-permute-start.1 = (f32[1,896]{1,0:T(1,128)S(1)}, f32[1,896]{1,0:T(1,128)S(1)}, u32[]{:S(2)}, u32[]{:S(2)}) collective-permute-start(f32[1,896]{1,0:T(1,128)S(1)} %reshape.385), channel_id=1, source_target_pairs={{0,1},{1,0},{2,3},{3,2},{4,5},{5,4},{6,7},{7,6},{8,9},{9,8},{10,11... | collective-permute-start | bytes 10760 | tf_op jit(solution)/shard_map/ppermute | solution.py:57
  83.5 18.2 %collective-permute-done.7.refs_2_ = bf16[256,2048]{1,0:T(8,128)(2,1)S(1)} collective-permute-done((bf16[256,2048]{1,0:T(8,128)(2,1)S(1)}, bf16[256,2048]{1,0:T(8,128)(2,1)S(1)}, u32[]{:S(2)}, u32[]{:S(2)}) %collective-permute-start.7) | collective-permute-done | bytes 1048608 | tf_op jit(solution)/shard_map/ppermute | solution.py:57
  105.9 12.2 %collective-permute-done.12.refs_4_ = bf16[128,2048]{1,0:T(8,128)(2,1)S(1)} collective-permute-done((bf16[128,2048]{1,0:T(8,128)(2,1)S(1)}, bf16[128,2048]{1,0:T(8,128)(2,1)S(1)}, u32[]{:S(2)}, u32[]{:S(2)}) %collective-permute-start.12) | collective-permute-done | bytes 524320 | tf_op jit(solution)/shard_map/ppermute | solution.py:57
  131.7 13.7 %project.1 = (bf16[2048,2048]{1,0:T(8,128)(2,1)}, f32[2048,768]{1,0:T(8,128)}) custom-call(bf16[256,2048]{1,0:T(8,128)(2,1)} %copy-done.13, bf16[256,2048]{1,0:T(8,128)(2,1)} %copy-done.17, bf16[256,2048]{1,0:T(8,128)(2,1)} %copy-done.16, bf16[128,2048]{1,0:T(8,128)(2,1)} %copy-done.52, bf16[128,2048]{1,0:T(8,128)(2,1)} %copy-done.51, ...), custom_call_target="tpu_custom_call" | custom-call | tf_op jit(solution)/shard_map/project/pallas_call | solution.py:370
  145.5 23.3 %attend.1 = (bf16[2048,768]{1,0:T(8,128)(2,1)}, f32[2048,256]{1,0:T(8,128)}, f32[2048,128]{1,0:T(8,128)S(1)}, f32[2,2048]{1,0:T(2,128)S(1)}) custom-call(s32[2,5]{1,0:T(2,128)S(1)} %pad_add_fusion.info, f32[2048,768]{1,0:T(8,128)} %get-tuple-element.292.proj, f32[1024,128]{1,0:T(8,128)S(1)} %get-tuple-element.293.cos_q, ...), custom_call_target="tpu_custom_call" | custom-call | tf_op jit(solution)/shard_map/attend/pallas_call | solution.py:682
  228.6 10.4 %collective-permute-done.25 = bf16[256,1024]{1,0:T(8,128)(2,1)S(1)} collective-permute-done((bf16[256,1024]{1,0:T(8,128)(2,1)}, bf16[256,1024]{1,0:T(8,128)(2,1)S(1)}, u32[]{:S(2)}, u32[]{:S(2)}) %collective-permute-start.25) | collective-permute-done | bytes 524320 | tf_op jit(solution)/shard_map/ppermute | solution.py:57
  241.7 10.7 %collective-permute-done.26 = bf16[256,1024]{1,0:T(8,128)(2,1)S(1)} collective-permute-done((bf16[256,1024]{1,0:T(8,128)(2,1)S(1)}, bf16[256,1024]{1,0:T(8,128)(2,1)S(1)}, u32[]{:S(2)}, u32[]{:S(2)}) %collective-permute-start.26) | collective-permute-done | bytes 524320 | tf_op jit(solution)/shard_map/ppermute | solution.py:57
  259.5 20.5 %collective-permute-done.29.refs_2_ = bf16[256,2048]{1,0:T(8,128)(2,1)} collective-permute-done((bf16[256,2048]{1,0:T(8,128)(2,1)}, bf16[256,2048]{1,0:T(8,128)(2,1)}, u32[]{:S(2)}, u32[]{:S(2)}) %collective-permute-start.29) | collective-permute-done | bytes 1048608 | tf_op jit(solution)/shard_map/ppermute | solution.py:57
  285.9 12.0 %collective-permute-done.34.refs_4_ = bf16[128,2048]{1,0:T(8,128)(2,1)S(1)} collective-permute-done((bf16[128,2048]{1,0:T(8,128)(2,1)S(1)}, bf16[128,2048]{1,0:T(8,128)(2,1)S(1)}, u32[]{:S(2)}, u32[]{:S(2)}) %collective-permute-start.34) | collective-permute-done | bytes 524320 | tf_op jit(solution)/shard_map/ppermute | solution.py:57
  303.3 20.2 %up.1 = (bf16[2048,2048]{1,0:T(8,128)(2,1)}, f32[2048,1024]{1,0:T(8,128)}, f32[2048,1024]{1,0:T(8,128)}, f32[2,2048]{1,0:T(2,128)}) custom-call(bf16[256,2048]{1,0:T(8,128)(2,1)} %add_convert_fusion.refs_0_, bf16[256,2048]{1,0:T(8,128)(2,1)} %collective-permute-done.28.refs_1_, bf16[256,2048]{1,0:T(8,128)(2,1)} %collective-permute-done.29.refs_2_, ...), custom_call_target="tpu_custom_call" | custom-call | tf_op jit(solution)/shard_map/up/pallas_call | solution.py:370
  341.4 11.4 %collective-permute-done.43.refs_4_ = bf16[128,2048]{1,0:T(8,128)(2,1)} collective-permute-done((bf16[128,2048]{1,0:T(8,128)(2,1)}, bf16[128,2048]{1,0:T(8,128)(2,1)}, u32[]{:S(2)}, u32[]{:S(2)}) %collective-permute-start.43) | collective-permute-done | bytes 524320 | tf_op jit(solution)/shard_map/ppermute | solution.py:57
  356.2 21.5 %down_back.1 = (bf16[2048,2048]{1,0:T(8,128)(2,1)}, f32[2048,1024]{1,0:T(8,128)}, f32[2,2048]{1,0:T(2,128)}, f32[2,1024]{1,0:T(2,128)}, bf16[2048,1024]{1,0:T(8,128)(2,1)}) custom-call(bf16[256,2048]{1,0:T(8,128)(2,1)} %collective-permute-done.15.refs_0_, bf16[256,2048]{1,0:T(8,128)(2,1)} %collective-permute-done.37.refs_1_, ...), custom_call_target="tpu_custom_call" | custom-call | tf_op jit(solution)/shard_map/down_back/pallas_call | solution.py:370
  385.2 14.1 %convolution_convert_fusion.1 = bf16[2048,1024]{1,0:T(8,128)(2,1)} fusion(bf16[2048,2048]{1,0:T(8,128)(2,1)} %get-tuple-element.362, bf16[2048,1024]{1,0:T(8,128)(2,1)} %get-tuple-element.385.refs_0_), kind=kOutput, calls=%fused_computation.1 | convolution fusion | flops 8592031744 | bytes 16777216 | tf_op jit(solution)/shard_map/dot_general | solution.py:251
  400.4 13.3 %up_back_other.1 = (bf16[2048,1024]{1,0:T(8,128)(2,1)}, bf16[256,2048]{1,0:T(8,128)(2,1)}, bf16[256,2048]{1,0:T(8,128)(2,1)}, bf16[256,2048]{1,0:T(8,128)(2,1)}, bf16[256,2048]{1,0:T(8,128)(2,1)}) custom-call(f32[2048,1024]{1,0:T(8,128)} %get-tuple-element.359.refs_0_, f32[2048,1024]{1,0:T(8,128)} %get-tuple-element.355.refs_11_.refs_1_, ...), custom_call_target="tpu_custom_call" | custom-call | tf_op jit(solution)/shard_map/up_back_other/pallas_call | solution.py:501
  419.2 9.5 %up_back_own_x.1 = (bf16[2048,1024]{1,0:T(8,128)(2,1)}, bf16[512,1024]{1,0:T(8,128)(2,1)}, bf16[256,1024]{1,0:T(8,128)(2,1)}, f32[256,1024]{1,0:T(8,128)}) custom-call(f32[2048,1024]{1,0:T(8,128)} %get-tuple-element.359.refs_0_, f32[2048,1024]{1,0:T(8,128)} %get-tuple-element.355.refs_11_.refs_1_, ...), custom_call_target="tpu_custom_call", output_to_operand_aliasing={{0}: (9, {})} | custom-call | tf_op jit(solution)/shard_map/up_back_own_x/pallas_call | solution.py:501
  430.1 9.8 %up_back_own_y.1 = (bf16[2048,1024]{1,0:T(8,128)(2,1)}, bf16[256,1024]{1,0:T(8,128)(2,1)}, f32[256,2048]{1,0:T(8,128)}, f32[256,1024]{1,0:T(8,128)}) custom-call(f32[2048,1024]{1,0:T(8,128)} %get-tuple-element.359.refs_0_, f32[2048,1024]{1,0:T(8,128)} %get-tuple-element.355.refs_11_.refs_1_, ...), custom_call_target="tpu_custom_call", output_to_operand_aliasing={{0}: (9, {})} | custom-call | tf_op jit(solution)/shard_map/up_back_own_y/pallas_call | solution.py:501
  443.4 14.1 %convolution_convert_fusion = bf16[2048,1024]{1,0:T(8,128)(2,1)} fusion(bf16[2048,2048]{1,0:T(8,128)(2,1)} %get-tuple-element.375, bf16[2048,1024]{1,0:T(8,128)(2,1)} %get-tuple-element.376), kind=kOutput, calls=%fused_computation | convolution fusion | flops 8592031744 | bytes 16777216 | tf_op jit(solution)/shard_map/dot_general | solution.py:251
  457.5 7.9 %collective-permute-done.57 = bf16[256,1024]{1,0:T(8,128)(2,1)} collective-permute-done((bf16[256,1024]{1,0:T(8,128)(2,1)}, bf16[256,1024]{1,0:T(8,128)(2,1)}, u32[]{:S(2)}, u32[]{:S(2)}) %collective-permute-start.57) | collective-permute-done | bytes 524320 | tf_op jit(solution)/shard_map/ppermute | solution.py:57
  472.9 10.2 %down_other.1 = (bf16[256,2048]{1,0:T(8,128)(2,1)}, bf16[256,2048]{1,0:T(8,128)(2,1)}, bf16[256,2048]{1,0:T(8,128)(2,1)}, bf16[256,2048]{1,0:T(8,128)(2,1)}) custom-call(bf16[2048,1024]{1,0:T(8,128)(2,1)} %get-tuple-element.385.refs_0_, bf16[2048,1024]{1,0:T(8,128)(2,1)} %all-gather.11.cloned.1.call-done.refs_10_.refs_1_), custom_call_target="tpu_custom_call" | custom-call | tf_op jit(solution)/shard_map/down_other/pallas_call | solution.py:501
  492.9 7.5 down_own_x.1
  501.4 7.7 down_own_y.1
  518.9 13.0 %collective-permute-done.71.refs_4_ = bf16[128,2048]{1,0:T(8,128)(2,1)S(1)} collective-permute-done((bf16[128,2048]{1,0:T(8,128)(2,1)S(1)}, bf16[128,2048]{1,0:T(8,128)(2,1)S(1)}, u32[]{:S(2)}, u32[]{:S(2)}) %collective-permute-start.71) | collective-permute-done | bytes 524320 | tf_op jit(solution)/shard_map/ppermute | solution.py:57
  540.2 12.9 %out_back.1 = (bf16[2048,2048]{1,0:T(8,128)(2,1)}, f32[2048,256]{1,0:T(8,128)}, f32[2,2048]{1,0:T(2,128)}, f32[2,256]{1,0:T(2,128)}) custom-call(bf16[256,2048]{1,0:T(8,128)(2,1)} %copy-done.12, bf16[256,2048]{1,0:T(8,128)(2,1)} %copy-done.15, bf16[256,2048]{1,0:T(8,128)(2,1)} %copy-done.14, bf16[128,2048]{1,0:T(8,128)(2,1)} %copy-done.57, ...), custom_call_target="tpu_custom_call" | custom-call | tf_op jit(solution)/shard_map/out_back/pallas_call | solution.py:370
  562.0 7.1 convolution_convert_fusion.3
  581.7 29.6 %attend_back.1.refs_0_ = bf16[2048,768]{1,0:T(8,128)(2,1)} custom-call(s32[2,5]{1,0:T(2,128)S(1)} %pad_add_fusion.info, bf16[2048,768]{1,0:T(8,128)(2,1)} %get-tuple-element.439.qkv, f32[2048,256]{1,0:T(8,128)} %get-tuple-element.298.refs_0_.refs_11_.attended, f32[2048,256]{1,0:T(8,128)} %get-tuple-element.440.grad, f32[2,2048]{1,0:T(2,128)S(1)} %copy-done.3, ...), custom_call_target="tpu_custom_call" | custom-call | tf_op jit(solution)/shard_map/attend_back/pallas_call | solution.py:716
  611.4 11.4 %convolution_convert_fusion.2 = bf16[2048,768]{1,0:T(8,128)(2,1)} fusion(bf16[2048,2048]{1,0:T(8,128)(2,1)} %get-tuple-element.446, bf16[2048,768]{1,0:T(8,128)(2,1)} %attend_back.1.refs_0_), kind=kOutput, calls=%fused_computation.2 | convolution fusion | flops 6444023808 | bytes 14680064 | tf_op jit(solution)/shard_map/dot_general | solution.py:251
  622.8 8.7 %project_back_other.1 = (bf16[256,2048]{1,0:T(8,128)(2,1)}, bf16[256,2048]{1,0:T(8,128)(2,1)}, bf16[256,2048]{1,0:T(8,128)(2,1)}, bf16[256,2048]{1,0:T(8,128)(2,1)}) custom-call(bf16[2048,768]{1,0:T(8,128)(2,1)} %attend_back.1.refs_0_, bf16[2048,768]{1,0:T(8,128)(2,1)} %all-gather.5.cloned.1.call-done.refs_10_.refs_1_), custom_call_target="tpu_custom_call" | custom-call | tf_op jit(solution)/shard_map/project_back_other/pallas_call | solution.py:501
  669.1 9.4 %collective-permute-done.87 = bf16[256,1024]{1,0:T(8,128)(2,1)S(1)} collective-permute-done((bf16[256,1024]{1,0:T(8,128)(2,1)}, bf16[256,1024]{1,0:T(8,128)(2,1)S(1)}, u32[]{:S(2)}, u32[]{:S(2)}) %collective-permute-start.87) | collective-permute-done | bytes 524320 | tf_op jit(solution)/shard_map/ppermute | solution.py:57
  683.6 16.6 %collective-permute-done.91 = bf16[256,1024]{1,0:T(8,128)(2,1)S(1)} collective-permute-done((bf16[256,1024]{1,0:T(8,128)(2,1)S(1)}, bf16[256,1024]{1,0:T(8,128)(2,1)S(1)}, u32[]{:S(2)}, u32[]{:S(2)}) %collective-permute-start.91) | collective-permute-done | bytes 524320 | tf_op jit(solution)/shard_map/ppermute | solution.py:57
  731.3 16.8 %all-to-all-done.4 = bf16[8,80,1024]{2,1,0:T(8,128)(2,1)} async-done(((bf16[8,80,1024]{2,1,0:T(8,128)(2,1)}), bf16[8,80,1024]{2,1,0:T(8,128)(2,1)}, u32[]{:S(2)}, u32[]{:S(2)}) %all-to-all-start.4) | async-done | bytes 1310752 | tf_op jit(solution)/shard_map/all_to_all | solution.py:156
  752.7 18.5 %collective-permute-start.96 = (f32[4,256]{1,0:T(4,128)S(1)}, f32[4,256]{1,0:T(4,128)S(1)}, u32[]{:S(2)}, u32[]{:S(2)}) collective-permute-start(f32[4,256]{1,0:T(4,128)S(1)} %add.422), channel_id=1, source_target_pairs={{0,2},{1,3},{2,0},{3,1},{4,6},{5,7},{6,4},{7,5},{8,10},{9,11},{10,... | collective-permute-start | bytes 12296 | tf_op jit(solution)/shard_map/ppermute | solution.py:57
  (600 shorter events, 327.7 us)
Async XLA Ops:
  12.5 31.3 %collective-permute-start = (bf16[256,2048]{1,0:T(8,128)(2,1)S(1)}, bf16[256,2048]{1,0:T(8,128)(2,1)S(1)}, u32[]{:S(2)}, u32[]{:S(2)}) collective-permute-start(bf16[256,2048]{1,0:T(8,128)(2,1)S(1)} %reorder.4), channel_id=1, source_target_pairs={{0,22},{1,30},{2,6},{3,14},{4,12},{5,4},{6,28},{7,20},{8,21},{9,29... | collective-permute-start | bytes 3145736 | tf_op jit(solution)/shard_map/ppermute | solution.py:786
  16.9 26.9 %all-to-all-start = ((bf16[8,64,1024]{2,1,0:T(8,128)(2,1)}), bf16[8,64,1024]{2,1,0:T(8,128)(2,1)S(1)}, u32[]{:S(2)}, u32[]{:S(2)}) async-start(bf16[8,64,1024]{2,1,0:T(8,128)(2,1)} %pad_maximum_fusion.4), calls=%async_computation | async-start | bytes 2097152 | tf_op jit(solution)/shard_map/all_to_all | solution.py:156
  22.2 109.5 %all-gather.5.cloned.1.call-start = ((), (), s32[]{:S(2)}) async-start(), calls=%async_computation.9 | async-start | bytes 3932160 | tf_op jit(solution)/shard_map/all_gather | solution.py:161
  78.1 23.6 %collective-permute-start.7 = (bf16[256,2048]{1,0:T(8,128)(2,1)S(1)}, bf16[256,2048]{1,0:T(8,128)(2,1)S(1)}, u32[]{:S(2)}, u32[]{:S(2)}) collective-permute-start(bf16[256,2048]{1,0:T(8,128)(2,1)S(1)} %fusion.7.refs_0_), channel_id=1, source_target_pairs={{0,16},{4,20},{8,24},{12,28},{16,0},{20,4},{24,8},{28,12},{1,17},{... | collective-permute-start | bytes 3145736 | tf_op jit(solution)/shard_map/ppermute | solution.py:57
  80.0 23.1 %collective-permute-start.6 = (bf16[256,2048]{1,0:T(8,128)(2,1)S(1)}, bf16[256,2048]{1,0:T(8,128)(2,1)S(1)}, u32[]{:S(2)}, u32[]{:S(2)}) collective-permute-start(bf16[256,2048]{1,0:T(8,128)(2,1)S(1)} %fusion.7.refs_0_), channel_id=1, source_target_pairs={{0,8},{4,12},{8,0},{12,4},{16,24},{20,28},{24,16},{28,20},{1,9},{5... | collective-permute-start | bytes 3145736 | tf_op jit(solution)/shard_map/ppermute | solution.py:57
  122.7 47.0 %all-to-all-start.1 = ((bf16[8,64,2048]{2,1,0:T(8,128)(2,1)}), bf16[8,64,2048]{2,1,0:T(8,128)(2,1)}, u32[]{:S(2)}, u32[]{:S(2)}) async-start(bf16[8,64,2048]{2,1,0:T(8,128)(2,1)} %pad_maximum_fusion), calls=%async_computation.1 | async-start | bytes 4194304 | tf_op jit(solution)/shard_map/all_to_all | solution.py:156
  128.6 66.1 %all-gather.7.cloned.1.call-start = ((), (), s32[]{:S(2)}) async-start(), calls=%async_computation.10 | async-start | bytes 1310720 | tf_op jit(solution)/shard_map/all_gather | solution.py:161
  128.6 41.1 %collective-permute-start.15 = (bf16[256,2048]{1,0:T(8,128)(2,1)}, bf16[256,2048]{1,0:T(8,128)(2,1)}, u32[]{:S(2)}, u32[]{:S(2)}) collective-permute-start(bf16[256,2048]{1,0:T(8,128)(2,1)} %reorder.5), channel_id=1, source_target_pairs={{0,22},{1,30},{2,6},{3,14},{4,12},{5,4},{6,28},{7,20},{8,21},{9,29... | collective-permute-start | bytes 3145736 | tf_op jit(solution)/shard_map/ppermute | solution.py:837
  131.1 172.2 %all-gather.9.cloned.1.call-start = ((), (), s32[]{:S(2)}) async-start(), calls=%async_computation.11 | async-start | bytes 5242880 | tf_op jit(solution)/shard_map/all_gather | solution.py:161
  181.3 173.1 %all-gather.11.cloned.1.call-start = ((), (), s32[]{:S(2)}) async-start(), calls=%async_computation.12 | async-start | bytes 5242880 | tf_op jit(solution)/shard_map/all_gather | solution.py:161
  211.9 27.1 %collective-permute-start.23 = (bf16[512,1024]{1,0:T(8,128)(2,1)}, bf16[512,1024]{1,0:T(8,128)(2,1)S(1)}, u32[]{:S(2)}, u32[]{:S(2)}) collective-permute-start(bf16[512,1024]{1,0:T(8,128)(2,1)} %get-tuple-element.313), channel_id=1, source_target_pairs={{0,8},{4,12},{8,0},{12,4},{16,24},{20,28},{24,16},{28,20},{1,9},{5... | collective-permute-start | bytes 3145736 | tf_op jit(solution)/shard_map/ppermute | solution.py:57
  256.3 23.7 %collective-permute-start.29 = (bf16[256,2048]{1,0:T(8,128)(2,1)}, bf16[256,2048]{1,0:T(8,128)(2,1)}, u32[]{:S(2)}, u32[]{:S(2)}) collective-permute-start(bf16[256,2048]{1,0:T(8,128)(2,1)} %add_convert_fusion.refs_0_), channel_id=1, source_target_pairs={{0,16},{4,20},{8,24},{12,28},{16,0},{20,4},{24,8},{28,12},{1,17},{... | collective-permute-start | bytes 3145736 | tf_op jit(solution)/shard_map/ppermute | solution.py:57
  257.7 23.1 %collective-permute-start.28 = (bf16[256,2048]{1,0:T(8,128)(2,1)}, bf16[256,2048]{1,0:T(8,128)(2,1)}, u32[]{:S(2)}, u32[]{:S(2)}) collective-permute-start(bf16[256,2048]{1,0:T(8,128)(2,1)} %add_convert_fusion.refs_0_), channel_id=1, source_target_pairs={{0,8},{4,12},{8,0},{12,4},{16,24},{20,28},{24,16},{28,20},{1,9},{5... | collective-permute-start | bytes 3145736 | tf_op jit(solution)/shard_map/ppermute | solution.py:57
  259.2 276.1 %reduce-scatter.5.cloned.1.call-start = ((), (), s32[]{:S(2)}) async-start(), calls=%async_computation.13 | async-start | bytes 5242880 | tf_op jit(solution)/shard_map/reduce_scatter | solution.py:165
  301.8 25.5 %collective-permute-start.38 = (bf16[256,2048]{1,0:T(8,128)(2,1)}, bf16[256,2048]{1,0:T(8,128)(2,1)}, u32[]{:S(2)}, u32[]{:S(2)}) collective-permute-start(bf16[256,2048]{1,0:T(8,128)(2,1)} %collective-permute-done.15.refs_0_), channel_id=1, source_target_pairs={{0,16},{4,20},{8,24},{12,28},{16,0},{20,4},{24,8},{28,12},{1,17},{... | collective-permute-start | bytes 3145736 | tf_op jit(solution)/shard_map/ppermute | solution.py:57
  302.7 25.4 %collective-permute-start.37 = (bf16[256,2048]{1,0:T(8,128)(2,1)}, bf16[256,2048]{1,0:T(8,128)(2,1)}, u32[]{:S(2)}, u32[]{:S(2)}) collective-permute-start(bf16[256,2048]{1,0:T(8,128)(2,1)} %collective-permute-done.15.refs_0_), channel_id=1, source_target_pairs={{0,8},{4,12},{8,0},{12,4},{16,24},{20,28},{24,16},{28,20},{1,9},{5... | collective-permute-start | bytes 3145736 | tf_op jit(solution)/shard_map/ppermute | solution.py:57
  400.0 169.3 %reduce-scatter.7.cloned.1.call-start = ((), (), s32[]{:S(2)}) async-start(), calls=%async_computation.14 | async-start | bytes 5242880 | tf_op jit(solution)/shard_map/reduce_scatter | solution.py:165
  440.8 24.6 %collective-permute-start.57 = (bf16[256,1024]{1,0:T(8,128)(2,1)}, bf16[256,1024]{1,0:T(8,128)(2,1)}, u32[]{:S(2)}, u32[]{:S(2)}) collective-permute-start(bf16[256,1024]{1,0:T(8,128)(2,1)} %get-tuple-element.373), channel_id=1, source_target_pairs={{0,16},{4,20},{8,24},{12,28},{16,0},{20,4},{24,8},{28,12},{1,17},{... | collective-permute-start | bytes 1572872 | tf_op jit(solution)/shard_map/ppermute | solution.py:57
  442.0 24.9 %collective-permute-start.56 = (bf16[512,1024]{1,0:T(8,128)(2,1)}, bf16[512,1024]{1,0:T(8,128)(2,1)}, u32[]{:S(2)}, u32[]{:S(2)}) collective-permute-start(bf16[512,1024]{1,0:T(8,128)(2,1)} %get-tuple-element.372), channel_id=1, source_target_pairs={{0,8},{4,12},{8,0},{12,4},{16,24},{20,28},{24,16},{28,20},{1,9},{5... | collective-permute-start | bytes 3145736 | tf_op jit(solution)/shard_map/ppermute | solution.py:57
  491.3 24.8 %collective-permute-start.66 = (bf16[256,2048]{1,0:T(8,128)(2,1)S(1)}, bf16[256,2048]{1,0:T(8,128)(2,1)S(1)}, u32[]{:S(2)}, u32[]{:S(2)}) collective-permute-start(bf16[256,2048]{1,0:T(8,128)(2,1)S(1)} %get-tuple-element.414.refs_0_), channel_id=1, source_target_pairs={{0,16},{4,20},{8,24},{12,28},{16,0},{20,4},{24,8},{28,12},{1,17},{... | collective-permute-start | bytes 3145736 | tf_op jit(solution)/shard_map/ppermute | solution.py:57
  492.0 25.0 %collective-permute-start.65 = (bf16[256,2048]{1,0:T(8,128)(2,1)S(1)}, bf16[256,2048]{1,0:T(8,128)(2,1)S(1)}, u32[]{:S(2)}, u32[]{:S(2)}) collective-permute-start(bf16[256,2048]{1,0:T(8,128)(2,1)S(1)} %get-tuple-element.414.refs_0_), channel_id=1, source_target_pairs={{0,8},{4,12},{8,0},{12,4},{16,24},{20,28},{24,16},{28,20},{1,9},{5... | collective-permute-start | bytes 3145736 | tf_op jit(solution)/shard_map/ppermute | solution.py:57
  540.2 82.6 %reduce-scatter.9.cloned.1.call-start = ((), (), s32[]{:S(2)}) async-start(), calls=%async_computation.15 | async-start | bytes 1310720 | tf_op jit(solution)/shard_map/reduce_scatter | solution.py:165
  569.3 42.1 %collective-permute-start.77 = (bf16[512,1024]{1,0:T(8,128)(2,1)}, bf16[512,1024]{1,0:T(8,128)(2,1)}, u32[]{:S(2)}, u32[]{:S(2)}) collective-permute-start(bf16[512,1024]{1,0:T(8,128)(2,1)} %get-tuple-element.436), channel_id=1, source_target_pairs={{0,8},{4,12},{8,0},{12,4},{16,24},{20,28},{24,16},{28,20},{1,9},{5... | collective-permute-start | bytes 3145736 | tf_op jit(solution)/shard_map/ppermute | solution.py:57
  569.8 41.5 %collective-permute-start.78 = (bf16[256,1024]{1,0:T(8,128)(2,1)}, bf16[256,1024]{1,0:T(8,128)(2,1)}, u32[]{:S(2)}, u32[]{:S(2)}) collective-permute-start(bf16[256,1024]{1,0:T(8,128)(2,1)} %get-tuple-element.437), channel_id=1, source_target_pairs={{0,16},{4,20},{8,24},{12,28},{16,0},{20,4},{24,8},{28,12},{1,17},{... | collective-permute-start | bytes 1572872 | tf_op jit(solution)/shard_map/ppermute | solution.py:57
  570.5 40.9 %collective-permute-start.79 = (bf16[256,1024]{1,0:T(8,128)(2,1)}, bf16[256,1024]{1,0:T(8,128)(2,1)}, u32[]{:S(2)}, u32[]{:S(2)}) collective-permute-start(bf16[256,1024]{1,0:T(8,128)(2,1)} %get-tuple-element.438), channel_id=1, source_target_pairs={{0,16},{4,20},{8,24},{12,28},{16,0},{20,4},{24,8},{28,12},{1,17},{... | collective-permute-start | bytes 1572872 | tf_op jit(solution)/shard_map/ppermute | solution.py:57
  575.7 47.1 %all-to-all-start.3 = ((bf16[8,64,1024]{2,1,0:T(8,128)(2,1)}), bf16[8,64,1024]{2,1,0:T(8,128)(2,1)}, u32[]{:S(2)}, u32[]{:S(2)}) async-start(bf16[8,64,1024]{2,1,0:T(8,128)(2,1)} %bitcast.128), calls=%async_computation.5 | async-start | bytes 2097152 | tf_op jit(solution)/shard_map/all_to_all | solution.py:156
  580.5 130.1 %reduce-scatter.11.cloned.1.call-start = ((), (), s32[]{:S(2)}) async-start(), calls=%async_computation.16 | async-start | bytes 3932160 | tf_op jit(solution)/shard_map/reduce_scatter | solution.py:165
  646.4 32.1 %collective-permute-start.85 = (bf16[512,1024]{1,0:T(8,128)(2,1)}, bf16[512,1024]{1,0:T(8,128)(2,1)S(1)}, u32[]{:S(2)}, u32[]{:S(2)}) collective-permute-start(bf16[512,1024]{1,0:T(8,128)(2,1)} %get-tuple-element.455), channel_id=1, source_target_pairs={{0,8},{4,12},{8,0},{12,4},{16,24},{20,28},{24,16},{28,20},{1,9},{5... | collective-permute-start | bytes 3145736 | tf_op jit(solution)/shard_map/ppermute | solution.py:57
  680.3 30.2 %collective-permute-start.93 = (bf16[256,2048]{1,0:T(8,128)(2,1)}, bf16[256,2048]{1,0:T(8,128)(2,1)S(1)}, u32[]{:S(2)}, u32[]{:S(2)}) collective-permute-start(bf16[256,2048]{1,0:T(8,128)(2,1)} %fusion.15), channel_id=1, source_target_pairs={{22,0},{30,1},{6,2},{14,3},{12,4},{4,5},{28,6},{20,7},{21,8},{29,9... | collective-permute-start | bytes 3145736 | tf_op jit(solution)/shard_map/ppermute | solution.py:962
  712.9 35.1 %all-to-all-start.4 = ((bf16[8,80,1024]{2,1,0:T(8,128)(2,1)}), bf16[8,80,1024]{2,1,0:T(8,128)(2,1)}, u32[]{:S(2)}, u32[]{:S(2)}) async-start(bf16[8,80,1024]{2,1,0:T(8,128)(2,1)} %pad_maximum_fusion.3), calls=%async_computation.8 | async-start | bytes 2621440 | tf_op jit(solution)/shard_map/all_to_all | solution.py:156
  721.5 59.5 %collective-permute-start.94 = (bf16[256,2048]{1,0:T(8,128)(2,1)}, bf16[256,2048]{1,0:T(8,128)(2,1)S(1)}, u32[]{:S(2)}, u32[]{:S(2)}) collective-permute-start(bf16[256,2048]{1,0:T(8,128)(2,1)} %fusion.12), channel_id=1, source_target_pairs={{22,0},{30,1},{6,2},{14,3},{12,4},{4,5},{28,6},{20,7},{21,8},{29,9... | collective-permute-start | bytes 3145736 | tf_op jit(solution)/shard_map/ppermute | solution.py:970
  752.7 28.1 %collective-permute-start.96 = (f32[4,256]{1,0:T(4,128)S(1)}, f32[4,256]{1,0:T(4,128)S(1)}, u32[]{:S(2)}, u32[]{:S(2)}) collective-permute-start(f32[4,256]{1,0:T(4,128)S(1)} %add.422), channel_id=1, source_target_pairs={{0,2},{1,3},{2,0},{3,1},{4,6},{5,7},{6,4},{7,5},{8,10},{9,11},{10,... | collective-permute-start | bytes 12296 | tf_op jit(solution)/shard_map/ppermute | solution.py:57
  (161 other events, 1605.4 us)
Sparse Core Ops, SparseCore 0:
  60.1 63.9 all-gather.4
  131.2 40.6 all-gather.6
  181.4 88.6 all-gather.8
  271.5 79.2 all-gather.10
  400.1 75.9 reduce-scatter.4
  478.3 77.2 reduce-scatter.6
  572.0 27.2 reduce-scatter.8
  622.9 60.5 reduce-scatter.10

commit v4 on v3

--- a/solution.py
+++ b/solution.py
@@ -16,9 +16,9 @@
 WIDE = jnp.float32
 BOTH = ("batch", "seq")
 
-LAYER = (2, 0, 1, 2, 1, 3, 3, 0)
-PLACE = (1, 1, 1, 0, 0, 1, 0, 0)
-TURN = ((1, 1), (3, 2), (0, 2), (3, 1))
+LAYER = (3, 0, 1, 2, 2, 1, 0, 3)
+PLACE = (0, 1, 1, 1, 0, 0, 0, 1)
+TURN = ((3, 0), (2, 1), (1, 2), (3, 0))
 
 
 class Plan:
@@ -587,8 +587,8 @@
     column = lax.broadcasted_iota(jnp.int32, (STRIPE, 128), 1) == head
     for i in range(length // STRIPE):
         low, high = i * STRIPE, (i + 1) * STRIPE
-        queries = jnp.where(mine, qkv[low:high, :hd], jnp.zeros((), LOW))
-        scores = matmul(queries, qkv[:high, hd : 2 * hd], (1, 1)) * 0.125 + bias[low:high, :high]
+        queries = jnp.where(mine, qkv[low:high, :hd] * 0.125, jnp.zeros((), LOW))
+        scores = matmul(queries, qkv[:high, hd : 2 * hd], (1, 1)) + bias[low:high, :high]
         top = jnp.max(scores, axis=-1, keepdims=True)
         weight = jnp.exp(scores - top)
         total = jnp.sum(weight, axis=-1, keepdims=True)
@@ -640,14 +640,14 @@
     keys_mine = jnp.where(mine_all, qkv[:, hd : 2 * hd], nothing)
     for i in range(length // STRIPE):
         low, high = i * STRIPE, (i + 1) * STRIPE
-        queries = jnp.where(mine, qkv[low:high, :hd], nothing)
+        queries = jnp.where(mine, qkv[low:high, :hd] * 0.125, nothing)
         upstream = jnp.where(mine, grad_low[low:high], nothing)
         delta = jnp.sum(jnp.where(mine, product[low:high], 0.0), axis=-1, keepdims=True)
         log_sum = jnp.sum(jnp.where(column, log_total[low:high], 0.0), axis=-1, keepdims=True)
-        scores = matmul(queries, qkv[:high, hd : 2 * hd], (1, 1)) * 0.125 + bias[low:high, :high]
+        scores = matmul(queries, qkv[:high, hd : 2 * hd], (1, 1)) + bias[low:high, :high]
         prob = jnp.exp(scores - log_sum)
         grad_prob = matmul(upstream, qkv[:high, 2 * hd :], (1, 1))
-        grad_s = (prob * (grad_prob - delta) * 0.125).astype(LOW)
+        grad_s = (prob * (grad_prob - delta)).astype(LOW)
         grad_q[low:high] += matmul(grad_s, keys_mine[:high], (1, 0))
         grad_k[:high] += matmul(grad_s, queries, (0, 0))
         grad_v[:high] += matmul(prob.astype(LOW), upstream, (0, 0))
@@ -656,9 +656,9 @@
     def _():
         for q in range(ns):
             target, low, high = place(q), q * slots, (q + 1) * slots
-            tables = (cos_q, sin_q, grad_q), (cos_k, sin_k, grad_k)
-            for part, (cosine, sine, total) in enumerate(tables):
-                cosine, sine = cosine[low:high], sine[low:high]
+            tables = (cos_q, sin_q, grad_q, 0.125), (cos_k, sin_k, grad_k, 1.0)
+            for part, (cosine, sine, total, scale) in enumerate(tables):
+                cosine, sine = cosine[low:high] * scale, sine[low:high] * scale
                 for pair in range(hd // 128):
                     values = total[low:high, pair * 128 : pair * 128 + 128]
                     turned = values * cosine - swap_halves(values) * sine
@@ -965,15 +965,15 @@
         grad_normed, ga, unit_attn, scale_attn
     )
     whole = jnp.stack([gain_ffn_part, bias_ffn_part, gain_attn_part, bias_attn_part])
+    whole = sum_over(whole, "seq", ns)
     whole = whole.reshape(4, ns, nb, -1).transpose(2, 0, 1, 3).reshape(nb, 1, 4 * hd)
-    grad_tokens, grad_qkv, output = sync((grad_mid + grad_resid).astype(LOW), grad_qkv, output)
+    grad_tokens, grad_qkv, whole = sync((grad_mid + grad_resid).astype(LOW), grad_qkv, whole)
     grad_tokens = lax.ppermute(grad_tokens, BOTH, plan.back)
     attn_grads = jnp.concatenate([grad_qkv, grad_out], axis=2)
     rows = attn_grads.shape[1]
     whole = jnp.broadcast_to(whole.astype(LOW), (nb, 16, 4 * hd))
     attn_grads = exchange(jnp.concatenate([attn_grads, whole], axis=1))
-    own = jnp.sum(attn_grads[:, rows].astype(WIDE), axis=0).reshape(4, -1)
-    own = sum_over(own, "seq", ns).reshape(4, ns, -1)
+    own = jnp.sum(attn_grads[:, rows].astype(WIDE), axis=0).reshape(4, ns, -1)
     own = lax.dynamic_index_in_dim(own, seq_index, 1, False)
     grad_qkv, grad_out = attn_grads[:, :rows, : 3 * hd], attn_grads[:, :rows, 3 * hd :]
     mixes = lax.dynamic_index_in_dim(vectors[:, :hd].reshape(2, ns, -1), seq_index, 1, False)

time: 806 us -> 783 us (0.971)
  starting transfers between devices: 145 us -> 99.5 us
  waiting for transfers between devices: 254 us -> 288 us
    ppermute x93, starting transfers between devices: 102 us -> 56.9 us  [swap_over(): return lax.ppermute(value, axis, [(i, i ^ step) for i in range(size)])]
    ppermute x1, waiting for transfers between devices: 0.01 us -> 19.1 us  [shards(): output = lax.ppermute(output, BOTH, plan.back)]
    ppermute x1, waiting for transfers between devices: 0.01 us -> 13 us  [shards(): grad_low = lax.ppermute(grad_low, BOTH, plan.there)]
    all_to_all x5, waiting for transfers between devices: 37.4 us -> 25.5 us  [exchange(): return lax.all_to_all(pieces, 'batch', 0, 0, tiled=True)]
    unnamed x170 -> x166, local copies, waits for them, and re-layouts: 20.4 us -> 19.9 us
  transfers between devices with their start and end apart: 110 -> 110, of which waited for: 56 -> 62; matrix products, arithmetic and copies ran while one was open for 15% -> 15% of each run, Pallas kernels for 25% -> 25%
where the time goes in v4:
time: 783 us; the launch traced here: 774 us
  waiting for transfers between devices  288 us (37%)
  Pallas kernels  224 us (29%)
  starting transfers between devices  99.5 us (13%)
  local copies, waits for them, and re-layouts  49.3 us (6%)
  matrix products  46.6 us (6%)
  other arithmetic  45.5 us (6%)
  between operations  20.9 us (3%)
    ppermute x93, waiting for transfers between devices, swap_over(): return lax.ppermute(value, axis, [(i, i ^ step) for i in range(size)])  218 us
    pallas_call x12, Pallas kernels, part_call(): pl.pallas_call(functools.partial(part_kernel, n_in=len(ins), make_left=ma...  98.2 us
    pallas_call x4, Pallas kernels, pieces_matmul(): pl.pallas_call(functools.partial(pieces_kernel, moves=moves, loads=loads,...  68.4 us
    ppermute x93, starting transfers between devices, swap_over(): return lax.ppermute(value, axis, [(i, i ^ step) for i in range(size)])  56.9 us
    dot_general x4, matrix products, matmul(): lax.dot_general(a, b, ((contract[:1], contract[1:]), ((), ())), preferred...  46.6 us
    pallas_call x1, Pallas kernels, attend_back(): pl.pallas_call(functools.partial(attend_back_kernel, ns=plan.ns, slots=sl...  29.5 us
    all_to_all x5, waiting for transfers between devices, exchange(): return lax.all_to_all(pieces, 'batch', 0, 0, tiled=True)  25.5 us
    all_to_all x5, starting transfers between devices, exchange(): return lax.all_to_all(pieces, 'batch', 0, 0, tiled=True)  25 us
  transfers between devices with their start and end apart: 110, of which 62 were waited for; matrix products, arithmetic and copies ran while one was open for 15% of the time, Pallas kernels for 25%

profile of v4, /device:TPU:4, one launch (start us, length us, event | category | flops | bytes accessed | tf_op | source)
XLA Modules:
  0.0 774.1 jit_solution(6691411801145013908)
XLA Ops:
  27.3 20.1 %all-to-all-done = bf16[8,64,1024]{2,1,0:T(8,128)(2,1)S(1)} async-done(((bf16[8,64,1024]{2,1,0:T(8,128)(2,1)}), bf16[8,64,1024]{2,1,0:T(8,128)(2,1)S(1)}, u32[]{:S(2)}, u32[]{:S(2)}) %all-to-all-start) | async-done | bytes 1048608 | tf_op jit(solution)/shard_map/all_to_all | solution.py:156
  85.4 15.6 %collective-permute-done.7.refs_2_ = bf16[256,2048]{1,0:T(8,128)(2,1)S(1)} collective-permute-done((bf16[256,2048]{1,0:T(8,128)(2,1)S(1)}, bf16[256,2048]{1,0:T(8,128)(2,1)S(1)}, u32[]{:S(2)}, u32[]{:S(2)}) %collective-permute-start.7) | collective-permute-done | bytes 1048608 | tf_op jit(solution)/shard_map/ppermute | solution.py:57
  104.8 12.6 %collective-permute-done.12.refs_4_ = bf16[128,2048]{1,0:T(8,128)(2,1)S(1)} collective-permute-done((bf16[128,2048]{1,0:T(8,128)(2,1)S(1)}, bf16[128,2048]{1,0:T(8,128)(2,1)S(1)}, u32[]{:S(2)}, u32[]{:S(2)}) %collective-permute-start.12) | collective-permute-done | bytes 524320 | tf_op jit(solution)/shard_map/ppermute | solution.py:57
  134.0 13.7 %project.1 = (bf16[2048,2048]{1,0:T(8,128)(2,1)}, f32[2048,768]{1,0:T(8,128)}) custom-call(bf16[256,2048]{1,0:T(8,128)(2,1)} %copy-done.13, bf16[256,2048]{1,0:T(8,128)(2,1)} %copy-done.18, bf16[256,2048]{1,0:T(8,128)(2,1)} %copy-done.17, bf16[128,2048]{1,0:T(8,128)(2,1)} %copy-done.53, bf16[128,2048]{1,0:T(8,128)(2,1)} %copy-done.52, ...), custom_call_target="tpu_custom_call" | custom-call | tf_op jit(solution)/shard_map/project/pallas_call | solution.py:370
  147.7 23.1 %attend.1 = (bf16[2048,768]{1,0:T(8,128)(2,1)}, f32[2048,256]{1,0:T(8,128)}, f32[2048,128]{1,0:T(8,128)S(1)}, f32[2,2048]{1,0:T(2,128)S(1)}) custom-call(s32[2,5]{1,0:T(2,128)S(1)} %pad_add_fusion.info, f32[2048,768]{1,0:T(8,128)} %get-tuple-element.292.proj, f32[1024,128]{1,0:T(8,128)S(1)} %get-tuple-element.293.cos_q, ...), custom_call_target="tpu_custom_call" | custom-call | tf_op jit(solution)/shard_map/attend/pallas_call | solution.py:682
  171.8 13.0 %collective-permute-done.15.refs_0_ = bf16[256,2048]{1,0:T(8,128)(2,1)} collective-permute-done((bf16[256,2048]{1,0:T(8,128)(2,1)}, bf16[256,2048]{1,0:T(8,128)(2,1)}, u32[]{:S(2)}, u32[]{:S(2)}) %collective-permute-start.15) | collective-permute-done | bytes 1048608 | tf_op jit(solution)/shard_map/ppermute | solution.py:837
  229.0 10.1 %collective-permute-done.25 = bf16[256,1024]{1,0:T(8,128)(2,1)S(1)} collective-permute-done((bf16[256,1024]{1,0:T(8,128)(2,1)}, bf16[256,1024]{1,0:T(8,128)(2,1)S(1)}, u32[]{:S(2)}, u32[]{:S(2)}) %collective-permute-start.25) | collective-permute-done | bytes 524320 | tf_op jit(solution)/shard_map/ppermute | solution.py:57
  240.3 11.9 %collective-permute-done.26 = bf16[256,1024]{1,0:T(8,128)(2,1)S(1)} collective-permute-done((bf16[256,1024]{1,0:T(8,128)(2,1)S(1)}, bf16[256,1024]{1,0:T(8,128)(2,1)S(1)}, u32[]{:S(2)}, u32[]{:S(2)}) %collective-permute-start.26) | collective-permute-done | bytes 524320 | tf_op jit(solution)/shard_map/ppermute | solution.py:57
  258.5 21.2 %collective-permute-done.29.refs_2_ = bf16[256,2048]{1,0:T(8,128)(2,1)} collective-permute-done((bf16[256,2048]{1,0:T(8,128)(2,1)}, bf16[256,2048]{1,0:T(8,128)(2,1)}, u32[]{:S(2)}, u32[]{:S(2)}) %collective-permute-start.29) | collective-permute-done | bytes 1048608 | tf_op jit(solution)/shard_map/ppermute | solution.py:57
  285.4 11.6 %collective-permute-done.34.refs_4_ = bf16[128,2048]{1,0:T(8,128)(2,1)S(1)} collective-permute-done((bf16[128,2048]{1,0:T(8,128)(2,1)S(1)}, bf16[128,2048]{1,0:T(8,128)(2,1)S(1)}, u32[]{:S(2)}, u32[]{:S(2)}) %collective-permute-start.34) | collective-permute-done | bytes 524320 | tf_op jit(solution)/shard_map/ppermute | solution.py:57
  302.9 20.2 %up.1 = (bf16[2048,2048]{1,0:T(8,128)(2,1)}, f32[2048,1024]{1,0:T(8,128)}, f32[2048,1024]{1,0:T(8,128)}, f32[2,2048]{1,0:T(2,128)}) custom-call(bf16[256,2048]{1,0:T(8,128)(2,1)} %add_convert_fusion.refs_0_, bf16[256,2048]{1,0:T(8,128)(2,1)} %collective-permute-done.28.refs_1_, bf16[256,2048]{1,0:T(8,128)(2,1)} %collective-permute-done.29.refs_2_, ...), custom_call_target="tpu_custom_call" | custom-call | tf_op jit(solution)/shard_map/up/pallas_call | solution.py:370
  340.8 11.5 %collective-permute-done.43.refs_4_ = bf16[128,2048]{1,0:T(8,128)(2,1)} collective-permute-done((bf16[128,2048]{1,0:T(8,128)(2,1)}, bf16[128,2048]{1,0:T(8,128)(2,1)}, u32[]{:S(2)}, u32[]{:S(2)}) %collective-permute-start.43) | collective-permute-done | bytes 524320 | tf_op jit(solution)/shard_map/ppermute | solution.py:57
  355.8 21.5 %down_back.1 = (bf16[2048,2048]{1,0:T(8,128)(2,1)}, f32[2048,1024]{1,0:T(8,128)}, f32[2,2048]{1,0:T(2,128)}, f32[2,1024]{1,0:T(2,128)}, bf16[2048,1024]{1,0:T(8,128)(2,1)}) custom-call(bf16[256,2048]{1,0:T(8,128)(2,1)} %collective-permute-done.15.refs_0_, bf16[256,2048]{1,0:T(8,128)(2,1)} %collective-permute-done.37.refs_1_, ...), custom_call_target="tpu_custom_call" | custom-call | tf_op jit(solution)/shard_map/down_back/pallas_call | solution.py:370
  384.6 14.1 %convolution_convert_fusion.1 = bf16[2048,1024]{1,0:T(8,128)(2,1)} fusion(bf16[2048,2048]{1,0:T(8,128)(2,1)} %get-tuple-element.362, bf16[2048,1024]{1,0:T(8,128)(2,1)} %get-tuple-element.385.refs_0_), kind=kOutput, calls=%fused_computation.1 | convolution fusion | flops 8592031744 | bytes 16777216 | tf_op jit(solution)/shard_map/dot_general | solution.py:251
  399.8 13.6 %up_back_other.1 = (bf16[2048,1024]{1,0:T(8,128)(2,1)}, bf16[256,2048]{1,0:T(8,128)(2,1)}, bf16[256,2048]{1,0:T(8,128)(2,1)}, bf16[256,2048]{1,0:T(8,128)(2,1)}, bf16[256,2048]{1,0:T(8,128)(2,1)}) custom-call(f32[2048,1024]{1,0:T(8,128)} %get-tuple-element.359.refs_0_, f32[2048,1024]{1,0:T(8,128)} %get-tuple-element.355.refs_11_.refs_1_, ...), custom_call_target="tpu_custom_call" | custom-call | tf_op jit(solution)/shard_map/up_back_other/pallas_call | solution.py:501
  418.9 9.6 %up_back_own_x.1 = (bf16[2048,1024]{1,0:T(8,128)(2,1)}, bf16[512,1024]{1,0:T(8,128)(2,1)}, bf16[256,1024]{1,0:T(8,128)(2,1)}, f32[256,1024]{1,0:T(8,128)}) custom-call(f32[2048,1024]{1,0:T(8,128)} %get-tuple-element.359.refs_0_, f32[2048,1024]{1,0:T(8,128)} %get-tuple-element.355.refs_11_.refs_1_, ...), custom_call_target="tpu_custom_call", output_to_operand_aliasing={{0}: (9, {})} | custom-call | tf_op jit(solution)/shard_map/up_back_own_x/pallas_call | solution.py:501
  429.7 9.8 %up_back_own_y.1 = (bf16[2048,1024]{1,0:T(8,128)(2,1)}, bf16[256,1024]{1,0:T(8,128)(2,1)}, f32[256,2048]{1,0:T(8,128)}, f32[256,1024]{1,0:T(8,128)}) custom-call(f32[2048,1024]{1,0:T(8,128)} %get-tuple-element.359.refs_0_, f32[2048,1024]{1,0:T(8,128)} %get-tuple-element.355.refs_11_.refs_1_, ...), custom_call_target="tpu_custom_call", output_to_operand_aliasing={{0}: (9, {})} | custom-call | tf_op jit(solution)/shard_map/up_back_own_y/pallas_call | solution.py:501
  443.0 14.1 %convolution_convert_fusion = bf16[2048,1024]{1,0:T(8,128)(2,1)} fusion(bf16[2048,2048]{1,0:T(8,128)(2,1)} %get-tuple-element.375, bf16[2048,1024]{1,0:T(8,128)(2,1)} %get-tuple-element.376), kind=kOutput, calls=%fused_computation | convolution fusion | flops 8592031744 | bytes 16777216 | tf_op jit(solution)/shard_map/dot_general | solution.py:251
  457.1 8.0 %collective-permute-done.57 = bf16[256,1024]{1,0:T(8,128)(2,1)} collective-permute-done((bf16[256,1024]{1,0:T(8,128)(2,1)}, bf16[256,1024]{1,0:T(8,128)(2,1)}, u32[]{:S(2)}, u32[]{:S(2)}) %collective-permute-start.57) | collective-permute-done | bytes 524320 | tf_op jit(solution)/shard_map/ppermute | solution.py:57
  472.5 10.2 %down_other.1 = (bf16[256,2048]{1,0:T(8,128)(2,1)}, bf16[256,2048]{1,0:T(8,128)(2,1)}, bf16[256,2048]{1,0:T(8,128)(2,1)}, bf16[256,2048]{1,0:T(8,128)(2,1)}) custom-call(bf16[2048,1024]{1,0:T(8,128)(2,1)} %get-tuple-element.385.refs_0_, bf16[2048,1024]{1,0:T(8,128)(2,1)} %all-gather.11.cloned.1.call-done.refs_10_.refs_1_), custom_call_target="tpu_custom_call" | custom-call | tf_op jit(solution)/shard_map/down_other/pallas_call | solution.py:501
  492.2 7.5 down_own_x.1
  500.7 7.7 %down_own_y.1 = (bf16[256,1024]{1,0:T(8,128)(2,1)}, f32[256,2048]{1,0:T(8,128)}, f32[256,1024]{1,0:T(8,128)}) custom-call(bf16[2048,1024]{1,0:T(8,128)(2,1)} %get-tuple-element.385.refs_0_, bf16[2048,1024]{1,0:T(8,128)(2,1)} %all-gather.11.cloned.1.call-done.refs_10_.refs_1_, bf16[256,2048]{1,0:T(8,128)(2,1)} %copy-done.24, ...), custom_call_target="tpu_custom_call" | custom-call | tf_op jit(solution)/shard_map/down_own_y/pallas_call | solution.py:501
  508.4 7.0 collective-permute-done.66.refs_2_
  518.3 13.4 %collective-permute-done.71.refs_4_ = bf16[128,2048]{1,0:T(8,128)(2,1)S(1)} collective-permute-done((bf16[128,2048]{1,0:T(8,128)(2,1)S(1)}, bf16[128,2048]{1,0:T(8,128)(2,1)S(1)}, u32[]{:S(2)}, u32[]{:S(2)}) %collective-permute-start.71) | collective-permute-done | bytes 524320 | tf_op jit(solution)/shard_map/ppermute | solution.py:57
  539.6 12.9 %out_back.1 = (bf16[2048,2048]{1,0:T(8,128)(2,1)}, f32[2048,256]{1,0:T(8,128)}, f32[2,2048]{1,0:T(2,128)}, f32[2,256]{1,0:T(2,128)}) custom-call(bf16[256,2048]{1,0:T(8,128)(2,1)} %copy-done.12, bf16[256,2048]{1,0:T(8,128)(2,1)} %copy-done.16, bf16[256,2048]{1,0:T(8,128)(2,1)} %copy-done.15, bf16[128,2048]{1,0:T(8,128)(2,1)} %copy-done.58, ...), custom_call_target="tpu_custom_call" | custom-call | tf_op jit(solution)/shard_map/out_back/pallas_call | solution.py:370
  561.4 7.1 convolution_convert_fusion.3
  581.0 29.5 %attend_back.1.refs_0_ = bf16[2048,768]{1,0:T(8,128)(2,1)} custom-call(s32[2,5]{1,0:T(2,128)S(1)} %pad_add_fusion.info, bf16[2048,768]{1,0:T(8,128)(2,1)} %get-tuple-element.439.qkv, f32[2048,256]{1,0:T(8,128)} %get-tuple-element.298.refs_0_.refs_11_.attended, f32[2048,256]{1,0:T(8,128)} %get-tuple-element.440.grad, f32[2,2048]{1,0:T(2,128)S(1)} %copy-done.3, ...), custom_call_target="tpu_custom_call" | custom-call | tf_op jit(solution)/shard_map/attend_back/pallas_call | solution.py:716
  610.6 11.4 %convolution_convert_fusion.2 = bf16[2048,768]{1,0:T(8,128)(2,1)} fusion(bf16[2048,2048]{1,0:T(8,128)(2,1)} %get-tuple-element.446, bf16[2048,768]{1,0:T(8,128)(2,1)} %attend_back.1.refs_0_), kind=kOutput, calls=%fused_computation.2 | convolution fusion | flops 6444023808 | bytes 14680064 | tf_op jit(solution)/shard_map/dot_general | solution.py:251
  621.9 8.6 %project_back_other.1 = (bf16[256,2048]{1,0:T(8,128)(2,1)}, bf16[256,2048]{1,0:T(8,128)(2,1)}, bf16[256,2048]{1,0:T(8,128)(2,1)}, bf16[256,2048]{1,0:T(8,128)(2,1)}) custom-call(bf16[2048,768]{1,0:T(8,128)(2,1)} %attend_back.1.refs_0_, bf16[2048,768]{1,0:T(8,128)(2,1)} %all-gather.5.cloned.1.call-done.refs_10_.refs_1_), custom_call_target="tpu_custom_call" | custom-call | tf_op jit(solution)/shard_map/project_back_other/pallas_call | solution.py:501
  668.9 9.4 %collective-permute-done.87 = bf16[256,1024]{1,0:T(8,128)(2,1)S(1)} collective-permute-done((bf16[256,1024]{1,0:T(8,128)(2,1)}, bf16[256,1024]{1,0:T(8,128)(2,1)S(1)}, u32[]{:S(2)}, u32[]{:S(2)}) %collective-permute-start.87) | collective-permute-done | bytes 524320 | tf_op jit(solution)/shard_map/ppermute | solution.py:57
  679.7 10.9 %collective-permute-done.91 = bf16[256,1024]{1,0:T(8,128)(2,1)S(1)} collective-permute-done((bf16[256,1024]{1,0:T(8,128)(2,1)S(1)}, bf16[256,1024]{1,0:T(8,128)(2,1)S(1)}, u32[]{:S(2)}, u32[]{:S(2)}) %collective-permute-start.91) | collective-permute-done | bytes 524320 | tf_op jit(solution)/shard_map/ppermute | solution.py:57
  722.4 19.1 %collective-permute-done.96.values = bf16[256,2048]{1,0:T(8,128)(2,1)S(1)} collective-permute-done((bf16[256,2048]{1,0:T(8,128)(2,1)S(1)}, bf16[256,2048]{1,0:T(8,128)(2,1)S(1)}, u32[]{:S(2)}, u32[]{:S(2)}) %collective-permute-start.96) | collective-permute-done | bytes 1048608 | tf_op jit(solution)/shard_map/ppermute | solution.py:962
  (592 shorter events, 323.3 us)
Async XLA Ops:
  13.9 40.2 %collective-permute-start = (bf16[256,2048]{1,0:T(8,128)(2,1)S(1)}, bf16[256,2048]{1,0:T(8,128)(2,1)S(1)}, u32[]{:S(2)}, u32[]{:S(2)}) collective-permute-start(bf16[256,2048]{1,0:T(8,128)(2,1)S(1)} %reorder.4), channel_id=1, source_target_pairs={{0,27},{1,19},{2,11},{3,3},{4,4},{5,12},{6,20},{7,28},{8,13},{9,5}... | collective-permute-start | bytes 3145736 | tf_op jit(solution)/shard_map/ppermute | solution.py:786
  19.2 28.2 %all-to-all-start = ((bf16[8,64,1024]{2,1,0:T(8,128)(2,1)}), bf16[8,64,1024]{2,1,0:T(8,128)(2,1)S(1)}, u32[]{:S(2)}, u32[]{:S(2)}) async-start(bf16[8,64,1024]{2,1,0:T(8,128)(2,1)} %pad_maximum_fusion.4), calls=%async_computation | async-start | bytes 2097152 | tf_op jit(solution)/shard_map/all_to_all | solution.py:156
  25.2 108.7 %all-gather.5.cloned.1.call-start = ((), (), s32[]{:S(2)}) async-start(), calls=%async_computation.9 | async-start | bytes 3932160 | tf_op jit(solution)/shard_map/all_gather | solution.py:161
  77.4 23.6 %collective-permute-start.7 = (bf16[256,2048]{1,0:T(8,128)(2,1)S(1)}, bf16[256,2048]{1,0:T(8,128)(2,1)S(1)}, u32[]{:S(2)}, u32[]{:S(2)}) collective-permute-start(bf16[256,2048]{1,0:T(8,128)(2,1)S(1)} %fusion.7.refs_0_), channel_id=1, source_target_pairs={{0,16},{4,20},{8,24},{12,28},{16,0},{20,4},{24,8},{28,12},{1,17},{... | collective-permute-start | bytes 3145736 | tf_op jit(solution)/shard_map/ppermute | solution.py:57
  79.4 23.1 %collective-permute-start.6 = (bf16[256,2048]{1,0:T(8,128)(2,1)S(1)}, bf16[256,2048]{1,0:T(8,128)(2,1)S(1)}, u32[]{:S(2)}, u32[]{:S(2)}) collective-permute-start(bf16[256,2048]{1,0:T(8,128)(2,1)S(1)} %fusion.7.refs_0_), channel_id=1, source_target_pairs={{0,8},{4,12},{8,0},{12,4},{16,24},{20,28},{24,16},{28,20},{1,9},{5... | collective-permute-start | bytes 3145736 | tf_op jit(solution)/shard_map/ppermute | solution.py:57
  123.0 61.8 %all-to-all-start.1 = ((bf16[8,64,2048]{2,1,0:T(8,128)(2,1)}), bf16[8,64,2048]{2,1,0:T(8,128)(2,1)}, u32[]{:S(2)}, u32[]{:S(2)}) async-start(bf16[8,64,2048]{2,1,0:T(8,128)(2,1)} %pad_maximum_fusion), calls=%async_computation.1 | async-start | bytes 4194304 | tf_op jit(solution)/shard_map/all_to_all | solution.py:156
  127.6 67.4 %all-gather.7.cloned.1.call-start = ((), (), s32[]{:S(2)}) async-start(), calls=%async_computation.10 | async-start | bytes 1310720 | tf_op jit(solution)/shard_map/all_gather | solution.py:161
  127.6 57.2 %collective-permute-start.15 = (bf16[256,2048]{1,0:T(8,128)(2,1)}, bf16[256,2048]{1,0:T(8,128)(2,1)}, u32[]{:S(2)}, u32[]{:S(2)}) collective-permute-start(bf16[256,2048]{1,0:T(8,128)(2,1)} %reorder.5), channel_id=1, source_target_pairs={{0,27},{1,19},{2,11},{3,3},{4,4},{5,12},{6,20},{7,28},{8,13},{9,5}... | collective-permute-start | bytes 3145736 | tf_op jit(solution)/shard_map/ppermute | solution.py:837
  133.3 169.6 %all-gather.9.cloned.1.call-start = ((), (), s32[]{:S(2)}) async-start(), calls=%async_computation.11 | async-start | bytes 5242880 | tf_op jit(solution)/shard_map/all_gather | solution.py:161
  189.5 164.4 %all-gather.11.cloned.1.call-start = ((), (), s32[]{:S(2)}) async-start(), calls=%async_computation.12 | async-start | bytes 5242880 | tf_op jit(solution)/shard_map/all_gather | solution.py:161
  212.4 26.7 %collective-permute-start.23 = (bf16[512,1024]{1,0:T(8,128)(2,1)}, bf16[512,1024]{1,0:T(8,128)(2,1)S(1)}, u32[]{:S(2)}, u32[]{:S(2)}) collective-permute-start(bf16[512,1024]{1,0:T(8,128)(2,1)} %get-tuple-element.313), channel_id=1, source_target_pairs={{0,8},{4,12},{8,0},{12,4},{16,24},{20,28},{24,16},{28,20},{1,9},{5... | collective-permute-start | bytes 3145736 | tf_op jit(solution)/shard_map/ppermute | solution.py:57
  256.1 23.5 %collective-permute-start.29 = (bf16[256,2048]{1,0:T(8,128)(2,1)}, bf16[256,2048]{1,0:T(8,128)(2,1)}, u32[]{:S(2)}, u32[]{:S(2)}) collective-permute-start(bf16[256,2048]{1,0:T(8,128)(2,1)} %add_convert_fusion.refs_0_), channel_id=1, source_target_pairs={{0,16},{4,20},{8,24},{12,28},{16,0},{20,4},{24,8},{28,12},{1,17},{... | collective-permute-start | bytes 3145736 | tf_op jit(solution)/shard_map/ppermute | solution.py:57
  256.5 23.5 %collective-permute-start.28 = (bf16[256,2048]{1,0:T(8,128)(2,1)}, bf16[256,2048]{1,0:T(8,128)(2,1)}, u32[]{:S(2)}, u32[]{:S(2)}) collective-permute-start(bf16[256,2048]{1,0:T(8,128)(2,1)} %add_convert_fusion.refs_0_), channel_id=1, source_target_pairs={{0,8},{4,12},{8,0},{12,4},{16,24},{20,28},{24,16},{28,20},{1,9},{5... | collective-permute-start | bytes 3145736 | tf_op jit(solution)/shard_map/ppermute | solution.py:57
  258.2 276.8 %reduce-scatter.5.cloned.1.call-start = ((), (), s32[]{:S(2)}) async-start(), calls=%async_computation.13 | async-start | bytes 5242880 | tf_op jit(solution)/shard_map/reduce_scatter | solution.py:165
  301.1 25.5 %collective-permute-start.38 = (bf16[256,2048]{1,0:T(8,128)(2,1)}, bf16[256,2048]{1,0:T(8,128)(2,1)}, u32[]{:S(2)}, u32[]{:S(2)}) collective-permute-start(bf16[256,2048]{1,0:T(8,128)(2,1)} %collective-permute-done.15.refs_0_), channel_id=1, source_target_pairs={{0,16},{4,20},{8,24},{12,28},{16,0},{20,4},{24,8},{28,12},{1,17},{... | collective-permute-start | bytes 3145736 | tf_op jit(solution)/shard_map/ppermute | solution.py:57
  302.3 25.2 %collective-permute-start.37 = (bf16[256,2048]{1,0:T(8,128)(2,1)}, bf16[256,2048]{1,0:T(8,128)(2,1)}, u32[]{:S(2)}, u32[]{:S(2)}) collective-permute-start(bf16[256,2048]{1,0:T(8,128)(2,1)} %collective-permute-done.15.refs_0_), channel_id=1, source_target_pairs={{0,8},{4,12},{8,0},{12,4},{16,24},{20,28},{24,16},{28,20},{1,9},{5... | collective-permute-start | bytes 3145736 | tf_op jit(solution)/shard_map/ppermute | solution.py:57
  330.6 22.1 %collective-permute-start.39 = (bf16[256,2048]{1,0:T(8,128)(2,1)}, bf16[256,2048]{1,0:T(8,128)(2,1)}, u32[]{:S(2)}, u32[]{:S(2)}) collective-permute-start(bf16[256,2048]{1,0:T(8,128)(2,1)} %collective-permute-done.15.refs_0_), channel_id=1, source_target_pairs={{0,4},{4,0},{8,12},{12,8},{16,20},{20,16},{24,28},{28,24},{1,5},{5... | collective-permute-start | bytes 3145736 | tf_op jit(solution)/shard_map/ppermute | solution.py:57
  399.4 169.2 %reduce-scatter.7.cloned.1.call-start = ((), (), s32[]{:S(2)}) async-start(), calls=%async_computation.14 | async-start | bytes 5242880 | tf_op jit(solution)/shard_map/reduce_scatter | solution.py:165
  440.3 24.8 %collective-permute-start.57 = (bf16[256,1024]{1,0:T(8,128)(2,1)}, bf16[256,1024]{1,0:T(8,128)(2,1)}, u32[]{:S(2)}, u32[]{:S(2)}) collective-permute-start(bf16[256,1024]{1,0:T(8,128)(2,1)} %get-tuple-element.373), channel_id=1, source_target_pairs={{0,16},{4,20},{8,24},{12,28},{16,0},{20,4},{24,8},{28,12},{1,17},{... | collective-permute-start | bytes 1572872 | tf_op jit(solution)/shard_map/ppermute | solution.py:57
  441.6 24.9 %collective-permute-start.56 = (bf16[512,1024]{1,0:T(8,128)(2,1)}, bf16[512,1024]{1,0:T(8,128)(2,1)}, u32[]{:S(2)}, u32[]{:S(2)}) collective-permute-start(bf16[512,1024]{1,0:T(8,128)(2,1)} %get-tuple-element.372), channel_id=1, source_target_pairs={{0,8},{4,12},{8,0},{12,4},{16,24},{20,28},{24,16},{28,20},{1,9},{5... | collective-permute-start | bytes 3145736 | tf_op jit(solution)/shard_map/ppermute | solution.py:57
  491.0 24.5 %collective-permute-start.66 = (bf16[256,2048]{1,0:T(8,128)(2,1)S(1)}, bf16[256,2048]{1,0:T(8,128)(2,1)S(1)}, u32[]{:S(2)}, u32[]{:S(2)}) collective-permute-start(bf16[256,2048]{1,0:T(8,128)(2,1)S(1)} %get-tuple-element.414.refs_0_), channel_id=1, source_target_pairs={{0,16},{4,20},{8,24},{12,28},{16,0},{20,4},{24,8},{28,12},{1,17},{... | collective-permute-start | bytes 3145736 | tf_op jit(solution)/shard_map/ppermute | solution.py:57
  491.8 25.0 %collective-permute-start.65 = (bf16[256,2048]{1,0:T(8,128)(2,1)S(1)}, bf16[256,2048]{1,0:T(8,128)(2,1)S(1)}, u32[]{:S(2)}, u32[]{:S(2)}) collective-permute-start(bf16[256,2048]{1,0:T(8,128)(2,1)S(1)} %get-tuple-element.414.refs_0_), channel_id=1, source_target_pairs={{0,8},{4,12},{8,0},{12,4},{16,24},{20,28},{24,16},{28,20},{1,9},{5... | collective-permute-start | bytes 3145736 | tf_op jit(solution)/shard_map/ppermute | solution.py:57
  539.6 82.4 %reduce-scatter.9.cloned.1.call-start = ((), (), s32[]{:S(2)}) async-start(), calls=%async_computation.15 | async-start | bytes 1310720 | tf_op jit(solution)/shard_map/reduce_scatter | solution.py:165
  568.6 42.0 %collective-permute-start.77 = (bf16[512,1024]{1,0:T(8,128)(2,1)}, bf16[512,1024]{1,0:T(8,128)(2,1)}, u32[]{:S(2)}, u32[]{:S(2)}) collective-permute-start(bf16[512,1024]{1,0:T(8,128)(2,1)} %get-tuple-element.436), channel_id=1, source_target_pairs={{0,8},{4,12},{8,0},{12,4},{16,24},{20,28},{24,16},{28,20},{1,9},{5... | collective-permute-start | bytes 3145736 | tf_op jit(solution)/shard_map/ppermute | solution.py:57
  569.2 41.4 %collective-permute-start.78 = (bf16[256,1024]{1,0:T(8,128)(2,1)}, bf16[256,1024]{1,0:T(8,128)(2,1)}, u32[]{:S(2)}, u32[]{:S(2)}) collective-permute-start(bf16[256,1024]{1,0:T(8,128)(2,1)} %get-tuple-element.437), channel_id=1, source_target_pairs={{0,16},{4,20},{8,24},{12,28},{16,0},{20,4},{24,8},{28,12},{1,17},{... | collective-permute-start | bytes 1572872 | tf_op jit(solution)/shard_map/ppermute | solution.py:57
  569.8 40.7 %collective-permute-start.79 = (bf16[256,1024]{1,0:T(8,128)(2,1)}, bf16[256,1024]{1,0:T(8,128)(2,1)}, u32[]{:S(2)}, u32[]{:S(2)}) collective-permute-start(bf16[256,1024]{1,0:T(8,128)(2,1)} %get-tuple-element.438), channel_id=1, source_target_pairs={{0,16},{4,20},{8,24},{12,28},{16,0},{20,4},{24,8},{28,12},{1,17},{... | collective-permute-start | bytes 1572872 | tf_op jit(solution)/shard_map/ppermute | solution.py:57
  575.0 47.0 %all-to-all-start.3 = ((bf16[8,64,1024]{2,1,0:T(8,128)(2,1)}), bf16[8,64,1024]{2,1,0:T(8,128)(2,1)}, u32[]{:S(2)}, u32[]{:S(2)}) async-start(bf16[8,64,1024]{2,1,0:T(8,128)(2,1)} %bitcast.134), calls=%async_computation.5 | async-start | bytes 2097152 | tf_op jit(solution)/shard_map/all_to_all | solution.py:156
  579.8 123.5 %reduce-scatter.11.cloned.1.call-start = ((), (), s32[]{:S(2)}) async-start(), calls=%async_computation.16 | async-start | bytes 3932160 | tf_op jit(solution)/shard_map/reduce_scatter | solution.py:165
  646.7 31.5 %collective-permute-start.85 = (bf16[512,1024]{1,0:T(8,128)(2,1)}, bf16[512,1024]{1,0:T(8,128)(2,1)S(1)}, u32[]{:S(2)}, u32[]{:S(2)}) collective-permute-start(bf16[512,1024]{1,0:T(8,128)(2,1)} %get-tuple-element.455), channel_id=1, source_target_pairs={{0,8},{4,12},{8,0},{12,4},{16,24},{20,28},{24,16},{28,20},{1,9},{5... | collective-permute-start | bytes 3145736 | tf_op jit(solution)/shard_map/ppermute | solution.py:57
  705.8 41.3 %all-to-all-start.4 = ((bf16[8,80,1024]{2,1,0:T(8,128)(2,1)}), bf16[8,80,1024]{2,1,0:T(8,128)(2,1)}, u32[]{:S(2)}, u32[]{:S(2)}) async-start(bf16[8,80,1024]{2,1,0:T(8,128)(2,1)} %pad_maximum_fusion.3), calls=%async_computation.8 | async-start | bytes 2621440 | tf_op jit(solution)/shard_map/all_to_all | solution.py:156
  710.8 30.6 %collective-permute-start.96 = (bf16[256,2048]{1,0:T(8,128)(2,1)S(1)}, bf16[256,2048]{1,0:T(8,128)(2,1)S(1)}, u32[]{:S(2)}, u32[]{:S(2)}) collective-permute-start(bf16[256,2048]{1,0:T(8,128)(2,1)S(1)} %copy-done.23), channel_id=1, source_target_pairs={{27,0},{19,1},{11,2},{3,3},{4,4},{12,5},{20,6},{28,7},{13,8},{5,9}... | collective-permute-start | bytes 3145736 | tf_op jit(solution)/shard_map/ppermute | solution.py:962
  717.1 46.4 %collective-permute-start.95 = (bf16[256,2048]{1,0:T(8,128)(2,1)}, bf16[256,2048]{1,0:T(8,128)(2,1)S(1)}, u32[]{:S(2)}, u32[]{:S(2)}) collective-permute-start(bf16[256,2048]{1,0:T(8,128)(2,1)} %fusion.12), channel_id=1, source_target_pairs={{27,0},{19,1},{11,2},{3,3},{4,4},{12,5},{20,6},{28,7},{13,8},{5,9}... | collective-permute-start | bytes 3145736 | tf_op jit(solution)/shard_map/ppermute | solution.py:971
  (159 other events, 1618.2 us)
Sparse Core Ops, SparseCore 0:
  59.4 64.7 all-gather.4
  133.5 39.1 all-gather.6
  189.6 80.4 all-gather.8
  271.5 79.2 all-gather.10
  399.5 76.5 reduce-scatter.4
  478.3 77.2 reduce-scatter.6
  571.3 27.8 reduce-scatter.8
  630.8 61.1 reduce-scatter.10

commit v5 on v4

--- a/solution.py
+++ b/solution.py
@@ -133,13 +133,14 @@
     return (first, second, to_x, to_y), others
 
 
-def reduce_last(plan, state):
+def reduce_last(plan, state, *others):
     if not plan.fast:
-        return state
+        return state, others
     first, second, to_x, to_y = state
     from_x, from_y = swap_over(to_x, "batch", 2, 8), swap_over(to_y, "batch", 4, 8)
-    from_x, from_y = sync(from_x, from_y)
-    return jnp.concatenate([first + from_y.astype(WIDE), second + from_x.astype(WIDE)], axis=1)
+    from_x, from_y, *others = sync(from_x, from_y, *others)
+    total = jnp.concatenate([first + from_y.astype(WIDE), second + from_x.astype(WIDE)], axis=1)
+    return total, others
 
 
 def split_columns(plan, shard):
@@ -859,7 +860,7 @@
         "out",
     )
     state, _ = reduce_first(plan, kept)
-    resid_mid = resid + reduce_last(plan, state)
+    resid_mid = resid + reduce_last(plan, state)[0]
 
     mean_ffn, scale_ffn = norm_stats(resid_mid)
     unit_ffn = (resid_mid - mean_ffn) * scale_ffn
@@ -912,7 +913,7 @@
     grad_up = matmul(ffn_in, grad_hidden, (0, 0)).astype(LOW)
     state, (grad_up, hidden_low) = reduce_first(plan, kept, grad_up, hidden_low)
     grad_up = scatter_layers(plan, grad_up)
-    grad_ffn_in = reduce_last(plan, state)
+    grad_ffn_in, _ = reduce_last(plan, state)
     grad_mid, gain_ffn_part, bias_ffn_part = norm_back(grad_ffn_in, gf, unit_ffn, scale_ffn)
     grad_mid = grad_mid + grad_low.astype(WIDE)
     (kept,) = block_parts(
@@ -949,10 +950,13 @@
     for step in bits(ns)[:1]:
         vectors = vectors + swap_over(vectors, "seq", step, ns)
     state, (grad_proj, vectors) = reduce_first(plan, kept, grad_proj, vectors)
+    grad_proj, state = sync(grad_proj, state)
     grad_qkv = matmul(normed, grad_proj, (0, 0)).astype(LOW)
-    grad_proj, grad_qkv, grad_up, grad_out = sync(grad_proj, grad_qkv, exchange(grad_up), grad_out)
+    total, (grad_proj, grad_qkv, grad_up, grad_out) = reduce_last(
+        plan, state, grad_proj, grad_qkv, exchange(grad_up), grad_out
+    )
     grad_qkv = scatter_layers(plan, grad_qkv)
-    output = (resid_mid + reduce_last(plan, state)).astype(LOW)
+    output = (resid_mid + total).astype(LOW)
     (kept,) = block_parts(
         plan, [(grad_proj, "rows")], qkv_w, (3 * hd, 0), plain_left, False, "project_back"
     )
@@ -960,7 +964,7 @@
         vectors = vectors + swap_over(vectors, "seq", step, ns)
     state, (output, vectors) = reduce_first(plan, kept, output, vectors)
     output = lax.ppermute(output, BOTH, plan.back)
-    grad_normed = reduce_last(plan, state)
+    grad_normed, _ = reduce_last(plan, state)
     grad_resid, gain_attn_part, bias_attn_part = norm_back(
         grad_normed, ga, unit_attn, scale_attn
     )

time: 783 us -> 788 us (level)
    unnamed x166 -> x170, local copies, waits for them, and re-layouts: 19.9 us -> 20.1 us
  transfers between devices with their start and end apart: 110 -> 110, of which waited for: 62 -> 63; matrix products, arithmetic and copies ran while one was open for 15% -> 15% of each run, Pallas kernels for 25% -> 26%
where the time goes in v5:
time: 788 us; the launch traced here: 778 us
  waiting for transfers between devices  287 us (36%)
  Pallas kernels  225 us (29%)
  starting transfers between devices  103 us (13%)
  local copies, waits for them, and re-layouts  49.5 us (6%)
  other arithmetic  47.4 us (6%)
  matrix products  45.7 us (6%)
  between operations  20.9 us (3%)
    ppermute x93, waiting for transfers between devices, swap_over(): return lax.ppermute(value, axis, [(i, i ^ step) for i in range(size)])  217 us
    pallas_call x12, Pallas kernels, part_call(): pl.pallas_call(functools.partial(part_kernel, n_in=len(ins), make_left=ma...  98.2 us
    pallas_call x4, Pallas kernels, pieces_matmul(): pl.pallas_call(functools.partial(pieces_kernel, moves=moves, loads=loads,...  68.4 us
    ppermute x93, starting transfers between devices, swap_over(): return lax.ppermute(value, axis, [(i, i ^ step) for i in range(size)])  59.5 us
    dot_general x4, matrix products, matmul(): lax.dot_general(a, b, ((contract[:1], contract[1:]), ((), ())), preferred...  45.7 us
    pallas_call x1, Pallas kernels, attend_back(): pl.pallas_call(functools.partial(attend_back_kernel, ns=plan.ns, slots=sl...  29.9 us
    all_to_all x5, waiting for transfers between devices, exchange(): return lax.all_to_all(pieces, 'batch', 0, 0, tiled=True)  25.5 us
    all_to_all x5, starting transfers between devices, exchange(): return lax.all_to_all(pieces, 'batch', 0, 0, tiled=True)  25.2 us
  transfers between devices with their start and end apart: 110, of which 63 were waited for; matrix products, arithmetic and copies ran while one was open for 15% of the time, Pallas kernels for 26%

profile of v5, /device:TPU:4, one launch (start us, length us, event | category | flops | bytes accessed | tf_op | source)
XLA Modules:
  0.0 778.0 jit_solution(8488457736602764880)
XLA Ops:
  27.3 20.1 %all-to-all-done = bf16[8,64,1024]{2,1,0:T(8,128)(2,1)S(1)} async-done(((bf16[8,64,1024]{2,1,0:T(8,128)(2,1)}), bf16[8,64,1024]{2,1,0:T(8,128)(2,1)S(1)}, u32[]{:S(2)}, u32[]{:S(2)}) %all-to-all-start) | async-done | bytes 1048608 | tf_op jit(solution)/shard_map/all_to_all | solution.py:157
  85.4 15.6 %collective-permute-done.7.refs_2_ = bf16[256,2048]{1,0:T(8,128)(2,1)S(1)} collective-permute-done((bf16[256,2048]{1,0:T(8,128)(2,1)S(1)}, bf16[256,2048]{1,0:T(8,128)(2,1)S(1)}, u32[]{:S(2)}, u32[]{:S(2)}) %collective-permute-start.7) | collective-permute-done | bytes 1048608 | tf_op jit(solution)/shard_map/ppermute | solution.py:57
  104.9 12.6 %collective-permute-done.12.refs_4_ = bf16[128,2048]{1,0:T(8,128)(2,1)S(1)} collective-permute-done((bf16[128,2048]{1,0:T(8,128)(2,1)S(1)}, bf16[128,2048]{1,0:T(8,128)(2,1)S(1)}, u32[]{:S(2)}, u32[]{:S(2)}) %collective-permute-start.12) | collective-permute-done | bytes 524320 | tf_op jit(solution)/shard_map/ppermute | solution.py:57
  133.9 13.8 %project.1 = (bf16[2048,2048]{1,0:T(8,128)(2,1)}, f32[2048,768]{1,0:T(8,128)}) custom-call(bf16[256,2048]{1,0:T(8,128)(2,1)} %copy-done.16, bf16[256,2048]{1,0:T(8,128)(2,1)} %copy-done.21, bf16[256,2048]{1,0:T(8,128)(2,1)} %copy-done.20, bf16[128,2048]{1,0:T(8,128)(2,1)} %copy-done.55, bf16[128,2048]{1,0:T(8,128)(2,1)} %copy-done.54, ...), custom_call_target="tpu_custom_call" | custom-call | tf_op jit(solution)/shard_map/project/pallas_call | solution.py:371
  147.7 23.1 %attend.1 = (bf16[2048,768]{1,0:T(8,128)(2,1)}, f32[2048,256]{1,0:T(8,128)}, f32[2048,128]{1,0:T(8,128)S(1)}, f32[2,2048]{1,0:T(2,128)S(1)}) custom-call(s32[2,5]{1,0:T(2,128)S(1)} %pad_add_fusion.info, f32[2048,768]{1,0:T(8,128)} %get-tuple-element.297.proj, f32[1024,128]{1,0:T(8,128)S(1)} %get-tuple-element.298.cos_q, ...), custom_call_target="tpu_custom_call" | custom-call | tf_op jit(solution)/shard_map/attend/pallas_call | solution.py:683
  171.7 13.0 %collective-permute-done.15.refs_0_ = bf16[256,2048]{1,0:T(8,128)(2,1)} collective-permute-done((bf16[256,2048]{1,0:T(8,128)(2,1)}, bf16[256,2048]{1,0:T(8,128)(2,1)}, u32[]{:S(2)}, u32[]{:S(2)}) %collective-permute-start.15) | collective-permute-done | bytes 1048608 | tf_op jit(solution)/shard_map/ppermute | solution.py:838
  228.9 10.1 %collective-permute-done.25 = bf16[256,1024]{1,0:T(8,128)(2,1)S(1)} collective-permute-done((bf16[256,1024]{1,0:T(8,128)(2,1)}, bf16[256,1024]{1,0:T(8,128)(2,1)S(1)}, u32[]{:S(2)}, u32[]{:S(2)}) %collective-permute-start.25) | collective-permute-done | bytes 524320 | tf_op jit(solution)/shard_map/ppermute | solution.py:57
  240.3 11.9 %collective-permute-done.26 = bf16[256,1024]{1,0:T(8,128)(2,1)S(1)} collective-permute-done((bf16[256,1024]{1,0:T(8,128)(2,1)S(1)}, bf16[256,1024]{1,0:T(8,128)(2,1)S(1)}, u32[]{:S(2)}, u32[]{:S(2)}) %collective-permute-start.26) | collective-permute-done | bytes 524320 | tf_op jit(solution)/shard_map/ppermute | solution.py:57
  258.4 21.1 %collective-permute-done.29.refs_2_ = bf16[256,2048]{1,0:T(8,128)(2,1)} collective-permute-done((bf16[256,2048]{1,0:T(8,128)(2,1)}, bf16[256,2048]{1,0:T(8,128)(2,1)}, u32[]{:S(2)}, u32[]{:S(2)}) %collective-permute-start.29) | collective-permute-done | bytes 1048608 | tf_op jit(solution)/shard_map/ppermute | solution.py:57
  285.4 11.6 %collective-permute-done.34.refs_4_ = bf16[128,2048]{1,0:T(8,128)(2,1)S(1)} collective-permute-done((bf16[128,2048]{1,0:T(8,128)(2,1)S(1)}, bf16[128,2048]{1,0:T(8,128)(2,1)S(1)}, u32[]{:S(2)}, u32[]{:S(2)}) %collective-permute-start.34) | collective-permute-done | bytes 524320 | tf_op jit(solution)/shard_map/ppermute | solution.py:57
  302.9 20.2 %up.1 = (bf16[2048,2048]{1,0:T(8,128)(2,1)}, f32[2048,1024]{1,0:T(8,128)}, f32[2048,1024]{1,0:T(8,128)}, f32[2,2048]{1,0:T(2,128)}) custom-call(bf16[256,2048]{1,0:T(8,128)(2,1)} %add_convert_fusion.refs_0_, bf16[256,2048]{1,0:T(8,128)(2,1)} %collective-permute-done.28.refs_1_, bf16[256,2048]{1,0:T(8,128)(2,1)} %collective-permute-done.29.refs_2_, ...), custom_call_target="tpu_custom_call" | custom-call | tf_op jit(solution)/shard_map/up/pallas_call | solution.py:371
  340.7 11.5 %collective-permute-done.43.refs_4_ = bf16[128,2048]{1,0:T(8,128)(2,1)} collective-permute-done((bf16[128,2048]{1,0:T(8,128)(2,1)}, bf16[128,2048]{1,0:T(8,128)(2,1)}, u32[]{:S(2)}, u32[]{:S(2)}) %collective-permute-start.43) | collective-permute-done | bytes 524320 | tf_op jit(solution)/shard_map/ppermute | solution.py:57
  355.7 21.5 %down_back.1 = (bf16[2048,2048]{1,0:T(8,128)(2,1)}, f32[2048,1024]{1,0:T(8,128)}, f32[2,2048]{1,0:T(2,128)}, f32[2,1024]{1,0:T(2,128)}, bf16[2048,1024]{1,0:T(8,128)(2,1)}) custom-call(bf16[256,2048]{1,0:T(8,128)(2,1)} %collective-permute-done.15.refs_0_, bf16[256,2048]{1,0:T(8,128)(2,1)} %collective-permute-done.37.refs_1_, ...), custom_call_target="tpu_custom_call" | custom-call | tf_op jit(solution)/shard_map/down_back/pallas_call | solution.py:371
  384.5 14.1 %convolution_convert_fusion.1 = bf16[2048,1024]{1,0:T(8,128)(2,1)} fusion(bf16[2048,2048]{1,0:T(8,128)(2,1)} %get-tuple-element.367, bf16[2048,1024]{1,0:T(8,128)(2,1)} %get-tuple-element.390.refs_0_), kind=kOutput, calls=%fused_computation.1 | convolution fusion | flops 8592031744 | bytes 16777216 | tf_op jit(solution)/shard_map/dot_general | solution.py:252
  399.8 13.6 %up_back_other.1 = (bf16[2048,1024]{1,0:T(8,128)(2,1)}, bf16[256,2048]{1,0:T(8,128)(2,1)}, bf16[256,2048]{1,0:T(8,128)(2,1)}, bf16[256,2048]{1,0:T(8,128)(2,1)}, bf16[256,2048]{1,0:T(8,128)(2,1)}) custom-call(f32[2048,1024]{1,0:T(8,128)} %get-tuple-element.364.refs_0_, f32[2048,1024]{1,0:T(8,128)} %get-tuple-element.360.refs_11_.refs_1_, ...), custom_call_target="tpu_custom_call" | custom-call | tf_op jit(solution)/shard_map/up_back_other/pallas_call | solution.py:502
  418.8 9.5 %up_back_own_x.1 = (bf16[2048,1024]{1,0:T(8,128)(2,1)}, bf16[512,1024]{1,0:T(8,128)(2,1)}, bf16[256,1024]{1,0:T(8,128)(2,1)}, f32[256,1024]{1,0:T(8,128)}) custom-call(f32[2048,1024]{1,0:T(8,128)} %get-tuple-element.364.refs_0_, f32[2048,1024]{1,0:T(8,128)} %get-tuple-element.360.refs_11_.refs_1_, ...), custom_call_target="tpu_custom_call", output_to_operand_aliasing={{0}: (9, {})} | custom-call | tf_op jit(solution)/shard_map/up_back_own_x/pallas_call | solution.py:502
  429.7 9.8 %up_back_own_y.1 = (bf16[2048,1024]{1,0:T(8,128)(2,1)}, bf16[256,1024]{1,0:T(8,128)(2,1)}, f32[256,2048]{1,0:T(8,128)}, f32[256,1024]{1,0:T(8,128)}) custom-call(f32[2048,1024]{1,0:T(8,128)} %get-tuple-element.364.refs_0_, f32[2048,1024]{1,0:T(8,128)} %get-tuple-element.360.refs_11_.refs_1_, ...), custom_call_target="tpu_custom_call", output_to_operand_aliasing={{0}: (9, {})} | custom-call | tf_op jit(solution)/shard_map/up_back_own_y/pallas_call | solution.py:502
  443.0 14.1 %convolution_convert_fusion = bf16[2048,1024]{1,0:T(8,128)(2,1)} fusion(bf16[2048,2048]{1,0:T(8,128)(2,1)} %get-tuple-element.380, bf16[2048,1024]{1,0:T(8,128)(2,1)} %get-tuple-element.381), kind=kOutput, calls=%fused_computation | convolution fusion | flops 8592031744 | bytes 16777216 | tf_op jit(solution)/shard_map/dot_general | solution.py:252
  457.1 8.0 %collective-permute-done.57 = bf16[256,1024]{1,0:T(8,128)(2,1)} collective-permute-done((bf16[256,1024]{1,0:T(8,128)(2,1)}, bf16[256,1024]{1,0:T(8,128)(2,1)}, u32[]{:S(2)}, u32[]{:S(2)}) %collective-permute-start.57) | collective-permute-done | bytes 524320 | tf_op jit(solution)/shard_map/ppermute | solution.py:57
  472.4 10.2 %down_other.1 = (bf16[256,2048]{1,0:T(8,128)(2,1)}, bf16[256,2048]{1,0:T(8,128)(2,1)}, bf16[256,2048]{1,0:T(8,128)(2,1)}, bf16[256,2048]{1,0:T(8,128)(2,1)}) custom-call(bf16[2048,1024]{1,0:T(8,128)(2,1)} %get-tuple-element.390.refs_0_, bf16[2048,1024]{1,0:T(8,128)(2,1)} %all-gather.11.cloned.1.call-done.refs_10_.refs_1_), custom_call_target="tpu_custom_call" | custom-call | tf_op jit(solution)/shard_map/down_other/pallas_call | solution.py:502
  492.2 7.5 down_own_x.1
  500.7 7.7 down_own_y.1
  508.4 7.0 collective-permute-done.66.refs_2_
  518.3 13.5 %collective-permute-done.71.refs_4_ = bf16[128,2048]{1,0:T(8,128)(2,1)S(1)} collective-permute-done((bf16[128,2048]{1,0:T(8,128)(2,1)S(1)}, bf16[128,2048]{1,0:T(8,128)(2,1)S(1)}, u32[]{:S(2)}, u32[]{:S(2)}) %collective-permute-start.71) | collective-permute-done | bytes 524320 | tf_op jit(solution)/shard_map/ppermute | solution.py:57
  539.5 12.9 %out_back.1 = (bf16[2048,2048]{1,0:T(8,128)(2,1)}, f32[2048,256]{1,0:T(8,128)}, f32[2,2048]{1,0:T(2,128)}, f32[2,256]{1,0:T(2,128)}) custom-call(bf16[256,2048]{1,0:T(8,128)(2,1)} %copy-done.13, bf16[256,2048]{1,0:T(8,128)(2,1)} %copy-done.19, bf16[256,2048]{1,0:T(8,128)(2,1)} %copy-done.18, bf16[128,2048]{1,0:T(8,128)(2,1)} %copy-done.60, ...), custom_call_target="tpu_custom_call" | custom-call | tf_op jit(solution)/shard_map/out_back/pallas_call | solution.py:371
  561.3 7.1 convolution_convert_fusion.3
  581.0 29.9 %attend_back.1.refs_0_ = bf16[2048,768]{1,0:T(8,128)(2,1)} custom-call(s32[2,5]{1,0:T(2,128)S(1)} %pad_add_fusion.info, bf16[2048,768]{1,0:T(8,128)(2,1)} %get-tuple-element.444.qkv, f32[2048,256]{1,0:T(8,128)} %get-tuple-element.303.refs_0_.refs_11_.attended, f32[2048,256]{1,0:T(8,128)} %get-tuple-element.445.grad, f32[2,2048]{1,0:T(2,128)S(1)} %copy-done.3, ...), custom_call_target="tpu_custom_call" | custom-call | tf_op jit(solution)/shard_map/attend_back/pallas_call | solution.py:717
  618.2 10.4 %convolution_convert_fusion.2 = bf16[2048,768]{1,0:T(8,128)(2,1)} fusion(bf16[2048,2048]{1,0:T(8,128)(2,1)} %get-tuple-element.460, bf16[2048,768]{1,0:T(8,128)(2,1)S(1)} %copy-done.8), kind=kOutput, calls=%fused_computation.2 | convolution fusion | flops 6444023808 | bytes 14680064 | tf_op jit(solution)/shard_map/dot_general | solution.py:252
  631.7 8.6 %project_back_other.1 = (bf16[256,2048]{1,0:T(8,128)(2,1)}, bf16[256,2048]{1,0:T(8,128)(2,1)}, bf16[256,2048]{1,0:T(8,128)(2,1)}, bf16[256,2048]{1,0:T(8,128)(2,1)}) custom-call(bf16[2048,768]{1,0:T(8,128)(2,1)} %attend_back.1.refs_0_, bf16[2048,768]{1,0:T(8,128)(2,1)} %all-gather.5.cloned.1.call-done.refs_10_.refs_1_), custom_call_target="tpu_custom_call" | custom-call | tf_op jit(solution)/shard_map/project_back_other/pallas_call | solution.py:502
  674.2 8.0 %collective-permute-done.89 = bf16[256,1024]{1,0:T(8,128)(2,1)S(1)} collective-permute-done((bf16[256,1024]{1,0:T(8,128)(2,1)}, bf16[256,1024]{1,0:T(8,128)(2,1)S(1)}, u32[]{:S(2)}, u32[]{:S(2)}) %collective-permute-start.89) | collective-permute-done | bytes 524320 | tf_op jit(solution)/shard_map/ppermute | solution.py:57
  684.8 8.6 %collective-permute-done.91 = bf16[256,1024]{1,0:T(8,128)(2,1)S(1)} collective-permute-done((bf16[256,1024]{1,0:T(8,128)(2,1)S(1)}, bf16[256,1024]{1,0:T(8,128)(2,1)S(1)}, u32[]{:S(2)}, u32[]{:S(2)}) %collective-permute-start.91) | collective-permute-done | bytes 524320 | tf_op jit(solution)/shard_map/ppermute | solution.py:57
  726.6 18.4 %collective-permute-done.96.values = bf16[256,2048]{1,0:T(8,128)(2,1)S(1)} collective-permute-done((bf16[256,2048]{1,0:T(8,128)(2,1)S(1)}, bf16[256,2048]{1,0:T(8,128)(2,1)S(1)}, u32[]{:S(2)}, u32[]{:S(2)}) %collective-permute-start.96) | collective-permute-done | bytes 1048608 | tf_op jit(solution)/shard_map/ppermute | solution.py:966
  (597 shorter events, 332.0 us)
Async XLA Ops:
  13.9 40.2 %collective-permute-start = (bf16[256,2048]{1,0:T(8,128)(2,1)S(1)}, bf16[256,2048]{1,0:T(8,128)(2,1)S(1)}, u32[]{:S(2)}, u32[]{:S(2)}) collective-permute-start(bf16[256,2048]{1,0:T(8,128)(2,1)S(1)} %reorder.4), channel_id=1, source_target_pairs={{0,27},{1,19},{2,11},{3,3},{4,4},{5,12},{6,20},{7,28},{8,13},{9,5}... | collective-permute-start | bytes 3145736 | tf_op jit(solution)/shard_map/ppermute | solution.py:787
  19.2 28.2 %all-to-all-start = ((bf16[8,64,1024]{2,1,0:T(8,128)(2,1)}), bf16[8,64,1024]{2,1,0:T(8,128)(2,1)S(1)}, u32[]{:S(2)}, u32[]{:S(2)}) async-start(bf16[8,64,1024]{2,1,0:T(8,128)(2,1)} %pad_maximum_fusion.4), calls=%async_computation | async-start | bytes 2097152 | tf_op jit(solution)/shard_map/all_to_all | solution.py:157
  25.2 108.7 %all-gather.5.cloned.1.call-start = ((), (), s32[]{:S(2)}) async-start(), calls=%async_computation.9 | async-start | bytes 3932160 | tf_op jit(solution)/shard_map/all_gather | solution.py:162
  77.4 23.6 %collective-permute-start.7 = (bf16[256,2048]{1,0:T(8,128)(2,1)S(1)}, bf16[256,2048]{1,0:T(8,128)(2,1)S(1)}, u32[]{:S(2)}, u32[]{:S(2)}) collective-permute-start(bf16[256,2048]{1,0:T(8,128)(2,1)S(1)} %fusion.7.refs_0_), channel_id=1, source_target_pairs={{0,16},{4,20},{8,24},{12,28},{16,0},{20,4},{24,8},{28,12},{1,17},{... | collective-permute-start | bytes 3145736 | tf_op jit(solution)/shard_map/ppermute | solution.py:57
  79.4 23.1 %collective-permute-start.6 = (bf16[256,2048]{1,0:T(8,128)(2,1)S(1)}, bf16[256,2048]{1,0:T(8,128)(2,1)S(1)}, u32[]{:S(2)}, u32[]{:S(2)}) collective-permute-start(bf16[256,2048]{1,0:T(8,128)(2,1)S(1)} %fusion.7.refs_0_), channel_id=1, source_target_pairs={{0,8},{4,12},{8,0},{12,4},{16,24},{20,28},{24,16},{28,20},{1,9},{5... | collective-permute-start | bytes 3145736 | tf_op jit(solution)/shard_map/ppermute | solution.py:57
  122.9 61.8 %all-to-all-start.1 = ((bf16[8,64,2048]{2,1,0:T(8,128)(2,1)}), bf16[8,64,2048]{2,1,0:T(8,128)(2,1)}, u32[]{:S(2)}, u32[]{:S(2)}) async-start(bf16[8,64,2048]{2,1,0:T(8,128)(2,1)} %pad_maximum_fusion), calls=%async_computation.1 | async-start | bytes 4194304 | tf_op jit(solution)/shard_map/all_to_all | solution.py:157
  127.5 67.4 %all-gather.7.cloned.1.call-start = ((), (), s32[]{:S(2)}) async-start(), calls=%async_computation.10 | async-start | bytes 1310720 | tf_op jit(solution)/shard_map/all_gather | solution.py:162
  127.5 57.2 %collective-permute-start.15 = (bf16[256,2048]{1,0:T(8,128)(2,1)}, bf16[256,2048]{1,0:T(8,128)(2,1)}, u32[]{:S(2)}, u32[]{:S(2)}) collective-permute-start(bf16[256,2048]{1,0:T(8,128)(2,1)} %reorder.5), channel_id=1, source_target_pairs={{0,27},{1,19},{2,11},{3,3},{4,4},{5,12},{6,20},{7,28},{8,13},{9,5}... | collective-permute-start | bytes 3145736 | tf_op jit(solution)/shard_map/ppermute | solution.py:838
  133.3 169.6 %all-gather.9.cloned.1.call-start = ((), (), s32[]{:S(2)}) async-start(), calls=%async_computation.11 | async-start | bytes 5242880 | tf_op jit(solution)/shard_map/all_gather | solution.py:162
  189.4 164.4 %all-gather.11.cloned.1.call-start = ((), (), s32[]{:S(2)}) async-start(), calls=%async_computation.12 | async-start | bytes 5242880 | tf_op jit(solution)/shard_map/all_gather | solution.py:162
  212.4 26.7 %collective-permute-start.23 = (bf16[512,1024]{1,0:T(8,128)(2,1)}, bf16[512,1024]{1,0:T(8,128)(2,1)S(1)}, u32[]{:S(2)}, u32[]{:S(2)}) collective-permute-start(bf16[512,1024]{1,0:T(8,128)(2,1)} %get-tuple-element.318), channel_id=1, source_target_pairs={{0,8},{4,12},{8,0},{12,4},{16,24},{20,28},{24,16},{28,20},{1,9},{5... | collective-permute-start | bytes 3145736 | tf_op jit(solution)/shard_map/ppermute | solution.py:57
  256.1 23.5 %collective-permute-start.29 = (bf16[256,2048]{1,0:T(8,128)(2,1)}, bf16[256,2048]{1,0:T(8,128)(2,1)}, u32[]{:S(2)}, u32[]{:S(2)}) collective-permute-start(bf16[256,2048]{1,0:T(8,128)(2,1)} %add_convert_fusion.refs_0_), channel_id=1, source_target_pairs={{0,16},{4,20},{8,24},{12,28},{16,0},{20,4},{24,8},{28,12},{1,17},{... | collective-permute-start | bytes 3145736 | tf_op jit(solution)/shard_map/ppermute | solution.py:57
  256.4 23.4 %collective-permute-start.28 = (bf16[256,2048]{1,0:T(8,128)(2,1)}, bf16[256,2048]{1,0:T(8,128)(2,1)}, u32[]{:S(2)}, u32[]{:S(2)}) collective-permute-start(bf16[256,2048]{1,0:T(8,128)(2,1)} %add_convert_fusion.refs_0_), channel_id=1, source_target_pairs={{0,8},{4,12},{8,0},{12,4},{16,24},{20,28},{24,16},{28,20},{1,9},{5... | collective-permute-start | bytes 3145736 | tf_op jit(solution)/shard_map/ppermute | solution.py:57
  258.1 276.8 %reduce-scatter.5.cloned.1.call-start = ((), (), s32[]{:S(2)}) async-start(), calls=%async_computation.13 | async-start | bytes 5242880 | tf_op jit(solution)/shard_map/reduce_scatter | solution.py:166
  301.1 25.5 %collective-permute-start.38 = (bf16[256,2048]{1,0:T(8,128)(2,1)}, bf16[256,2048]{1,0:T(8,128)(2,1)}, u32[]{:S(2)}, u32[]{:S(2)}) collective-permute-start(bf16[256,2048]{1,0:T(8,128)(2,1)} %collective-permute-done.15.refs_0_), channel_id=1, source_target_pairs={{0,16},{4,20},{8,24},{12,28},{16,0},{20,4},{24,8},{28,12},{1,17},{... | collective-permute-start | bytes 3145736 | tf_op jit(solution)/shard_map/ppermute | solution.py:57
  302.2 25.2 %collective-permute-start.37 = (bf16[256,2048]{1,0:T(8,128)(2,1)}, bf16[256,2048]{1,0:T(8,128)(2,1)}, u32[]{:S(2)}, u32[]{:S(2)}) collective-permute-start(bf16[256,2048]{1,0:T(8,128)(2,1)} %collective-permute-done.15.refs_0_), channel_id=1, source_target_pairs={{0,8},{4,12},{8,0},{12,4},{16,24},{20,28},{24,16},{28,20},{1,9},{5... | collective-permute-start | bytes 3145736 | tf_op jit(solution)/shard_map/ppermute | solution.py:57
  330.5 22.0 %collective-permute-start.39 = (bf16[256,2048]{1,0:T(8,128)(2,1)}, bf16[256,2048]{1,0:T(8,128)(2,1)}, u32[]{:S(2)}, u32[]{:S(2)}) collective-permute-start(bf16[256,2048]{1,0:T(8,128)(2,1)} %collective-permute-done.15.refs_0_), channel_id=1, source_target_pairs={{0,4},{4,0},{8,12},{12,8},{16,20},{20,16},{24,28},{28,24},{1,5},{5... | collective-permute-start | bytes 3145736 | tf_op jit(solution)/shard_map/ppermute | solution.py:57
  399.3 169.2 %reduce-scatter.7.cloned.1.call-start = ((), (), s32[]{:S(2)}) async-start(), calls=%async_computation.14 | async-start | bytes 5242880 | tf_op jit(solution)/shard_map/reduce_scatter | solution.py:166
  440.3 24.8 %collective-permute-start.57 = (bf16[256,1024]{1,0:T(8,128)(2,1)}, bf16[256,1024]{1,0:T(8,128)(2,1)}, u32[]{:S(2)}, u32[]{:S(2)}) collective-permute-start(bf16[256,1024]{1,0:T(8,128)(2,1)} %get-tuple-element.378), channel_id=1, source_target_pairs={{0,16},{4,20},{8,24},{12,28},{16,0},{20,4},{24,8},{28,12},{1,17},{... | collective-permute-start | bytes 1572872 | tf_op jit(solution)/shard_map/ppermute | solution.py:57
  441.6 24.9 %collective-permute-start.56 = (bf16[512,1024]{1,0:T(8,128)(2,1)}, bf16[512,1024]{1,0:T(8,128)(2,1)}, u32[]{:S(2)}, u32[]{:S(2)}) collective-permute-start(bf16[512,1024]{1,0:T(8,128)(2,1)} %get-tuple-element.377), channel_id=1, source_target_pairs={{0,8},{4,12},{8,0},{12,4},{16,24},{20,28},{24,16},{28,20},{1,9},{5... | collective-permute-start | bytes 3145736 | tf_op jit(solution)/shard_map/ppermute | solution.py:57
  490.9 24.5 %collective-permute-start.66 = (bf16[256,2048]{1,0:T(8,128)(2,1)S(1)}, bf16[256,2048]{1,0:T(8,128)(2,1)S(1)}, u32[]{:S(2)}, u32[]{:S(2)}) collective-permute-start(bf16[256,2048]{1,0:T(8,128)(2,1)S(1)} %get-tuple-element.419.refs_0_), channel_id=1, source_target_pairs={{0,16},{4,20},{8,24},{12,28},{16,0},{20,4},{24,8},{28,12},{1,17},{... | collective-permute-start | bytes 3145736 | tf_op jit(solution)/shard_map/ppermute | solution.py:57
  491.8 24.9 %collective-permute-start.65 = (bf16[256,2048]{1,0:T(8,128)(2,1)S(1)}, bf16[256,2048]{1,0:T(8,128)(2,1)S(1)}, u32[]{:S(2)}, u32[]{:S(2)}) collective-permute-start(bf16[256,2048]{1,0:T(8,128)(2,1)S(1)} %get-tuple-element.419.refs_0_), channel_id=1, source_target_pairs={{0,8},{4,12},{8,0},{12,4},{16,24},{20,28},{24,16},{28,20},{1,9},{5... | collective-permute-start | bytes 3145736 | tf_op jit(solution)/shard_map/ppermute | solution.py:57
  539.5 92.2 %reduce-scatter.9.cloned.1.call-start = ((), (), s32[]{:S(2)}) async-start(), calls=%async_computation.15 | async-start | bytes 1310720 | tf_op jit(solution)/shard_map/reduce_scatter | solution.py:166
  568.6 42.3 %collective-permute-start.77 = (bf16[512,1024]{1,0:T(8,128)(2,1)}, bf16[512,1024]{1,0:T(8,128)(2,1)}, u32[]{:S(2)}, u32[]{:S(2)}) collective-permute-start(bf16[512,1024]{1,0:T(8,128)(2,1)} %get-tuple-element.441), channel_id=1, source_target_pairs={{0,8},{4,12},{8,0},{12,4},{16,24},{20,28},{24,16},{28,20},{1,9},{5... | collective-permute-start | bytes 3145736 | tf_op jit(solution)/shard_map/ppermute | solution.py:57
  569.1 41.8 %collective-permute-start.78 = (bf16[256,1024]{1,0:T(8,128)(2,1)}, bf16[256,1024]{1,0:T(8,128)(2,1)}, u32[]{:S(2)}, u32[]{:S(2)}) collective-permute-start(bf16[256,1024]{1,0:T(8,128)(2,1)} %get-tuple-element.442), channel_id=1, source_target_pairs={{0,16},{4,20},{8,24},{12,28},{16,0},{20,4},{24,8},{28,12},{1,17},{... | collective-permute-start | bytes 1572872 | tf_op jit(solution)/shard_map/ppermute | solution.py:57
  569.8 41.1 %collective-permute-start.79 = (bf16[256,1024]{1,0:T(8,128)(2,1)}, bf16[256,1024]{1,0:T(8,128)(2,1)}, u32[]{:S(2)}, u32[]{:S(2)}) collective-permute-start(bf16[256,1024]{1,0:T(8,128)(2,1)} %get-tuple-element.443), channel_id=1, source_target_pairs={{0,16},{4,20},{8,24},{12,28},{16,0},{20,4},{24,8},{28,12},{1,17},{... | collective-permute-start | bytes 1572872 | tf_op jit(solution)/shard_map/ppermute | solution.py:57
  575.0 53.6 %all-to-all-start.3 = ((bf16[8,64,1024]{2,1,0:T(8,128)(2,1)}), bf16[8,64,1024]{2,1,0:T(8,128)(2,1)}, u32[]{:S(2)}, u32[]{:S(2)}) async-start(bf16[8,64,1024]{2,1,0:T(8,128)(2,1)} %bitcast.134), calls=%async_computation.5 | async-start | bytes 2097152 | tf_op jit(solution)/shard_map/all_to_all | solution.py:157
  579.8 127.0 %reduce-scatter.11.cloned.1.call-start = ((), (), s32[]{:S(2)}) async-start(), calls=%async_computation.16 | async-start | bytes 3932160 | tf_op jit(solution)/shard_map/reduce_scatter | solution.py:166
  656.9 25.3 %collective-permute-start.87 = (bf16[512,1024]{1,0:T(8,128)(2,1)}, bf16[512,1024]{1,0:T(8,128)(2,1)S(1)}, u32[]{:S(2)}, u32[]{:S(2)}) collective-permute-start(bf16[512,1024]{1,0:T(8,128)(2,1)} %get-tuple-element.469), channel_id=1, source_target_pairs={{0,8},{4,12},{8,0},{12,4},{16,24},{20,28},{24,16},{28,20},{1,9},{5... | collective-permute-start | bytes 3145736 | tf_op jit(solution)/shard_map/ppermute | solution.py:57
  709.2 41.5 %all-to-all-start.4 = ((bf16[8,80,1024]{2,1,0:T(8,128)(2,1)}), bf16[8,80,1024]{2,1,0:T(8,128)(2,1)}, u32[]{:S(2)}, u32[]{:S(2)}) async-start(bf16[8,80,1024]{2,1,0:T(8,128)(2,1)} %pad_maximum_fusion.3), calls=%async_computation.8 | async-start | bytes 2621440 | tf_op jit(solution)/shard_map/all_to_all | solution.py:157
  714.4 30.6 %collective-permute-start.96 = (bf16[256,2048]{1,0:T(8,128)(2,1)S(1)}, bf16[256,2048]{1,0:T(8,128)(2,1)S(1)}, u32[]{:S(2)}, u32[]{:S(2)}) collective-permute-start(bf16[256,2048]{1,0:T(8,128)(2,1)S(1)} %copy-done.27), channel_id=1, source_target_pairs={{27,0},{19,1},{11,2},{3,3},{4,4},{12,5},{20,6},{28,7},{13,8},{5,9}... | collective-permute-start | bytes 3145736 | tf_op jit(solution)/shard_map/ppermute | solution.py:966
  721.3 46.1 %collective-permute-start.95 = (bf16[256,2048]{1,0:T(8,128)(2,1)}, bf16[256,2048]{1,0:T(8,128)(2,1)S(1)}, u32[]{:S(2)}, u32[]{:S(2)}) collective-permute-start(bf16[256,2048]{1,0:T(8,128)(2,1)} %fusion.12), channel_id=1, source_target_pairs={{27,0},{19,1},{11,2},{3,3},{4,4},{12,5},{20,6},{28,7},{13,8},{5,9}... | collective-permute-start | bytes 3145736 | tf_op jit(solution)/shard_map/ppermute | solution.py:975
  (161 other events, 1670.0 us)
Sparse Core Ops, SparseCore 0:
  59.4 64.7 all-gather.4
  133.4 39.1 all-gather.6
  189.5 80.4 all-gather.8
  271.4 79.2 all-gather.10
  399.4 76.5 reduce-scatter.4
  478.2 77.2 reduce-scatter.6
  575.1 27.8 reduce-scatter.8
  631.8 60.1 reduce-scatter.10

commit v6 on v5

--- a/solution.py
+++ b/solution.py
@@ -950,21 +950,18 @@
     for step in bits(ns)[:1]:
         vectors = vectors + swap_over(vectors, "seq", step, ns)
     state, (grad_proj, vectors) = reduce_first(plan, kept, grad_proj, vectors)
-    grad_proj, state = sync(grad_proj, state)
     grad_qkv = matmul(normed, grad_proj, (0, 0)).astype(LOW)
-    total, (grad_proj, grad_qkv, grad_up, grad_out) = reduce_last(
-        plan, state, grad_proj, grad_qkv, exchange(grad_up), grad_out
-    )
+    grad_proj, grad_qkv, grad_up, grad_out = sync(grad_proj, grad_qkv, exchange(grad_up), grad_out)
     grad_qkv = scatter_layers(plan, grad_qkv)
-    output = (resid_mid + total).astype(LOW)
+    output = (resid_mid + reduce_last(plan, state)[0]).astype(LOW)
     (kept,) = block_parts(
         plan, [(grad_proj, "rows")], qkv_w, (3 * hd, 0), plain_left, False, "project_back"
     )
+    state, (output, vectors) = reduce_first(plan, kept, output, vectors)
+    output = lax.ppermute(output, BOTH, plan.back)
     for step in bits(ns)[1:]:
         vectors = vectors + swap_over(vectors, "seq", step, ns)
-    state, (output, vectors) = reduce_first(plan, kept, output, vectors)
-    output = lax.ppermute(output, BOTH, plan.back)
-    grad_normed, _ = reduce_last(plan, state)
+    grad_normed, (vectors,) = reduce_last(plan, state, vectors)
     grad_resid, gain_attn_part, bias_attn_part = norm_back(
         grad_normed, ga, unit_attn, scale_attn
     )

time: 788 us -> 783 us (level)
    unnamed x170 -> x166, local copies, waits for them, and re-layouts: 20.1 us -> 21.2 us
  transfers between devices with their start and end apart: 110 -> 110, of which waited for: 63 -> 63; matrix products, arithmetic and copies ran while one was open for 15% -> 15% of each run, Pallas kernels for 26% -> 25%
where the time goes in v6:
time: 783 us; the launch traced here: 774 us
  waiting for transfers between devices  286 us (37%)
  Pallas kernels  224 us (29%)
  starting transfers between devices  99.9 us (13%)
  local copies, waits for them, and re-layouts  50.6 us (6%)
  matrix products  46.6 us (6%)
  other arithmetic  45.5 us (6%)
  between operations  20.9 us (3%)
    ppermute x93, waiting for transfers between devices, swap_over(): return lax.ppermute(value, axis, [(i, i ^ step) for i in range(size)])  216 us
    pallas_call x12, Pallas kernels, part_call(): pl.pallas_call(functools.partial(part_kernel, n_in=len(ins), make_left=ma...  98.2 us
    pallas_call x4, Pallas kernels, pieces_matmul(): pl.pallas_call(functools.partial(pieces_kernel, moves=moves, loads=loads,...  68.4 us
    ppermute x93, starting transfers between devices, swap_over(): return lax.ppermute(value, axis, [(i, i ^ step) for i in range(size)])  57.4 us
    dot_general x4, matrix products, matmul(): lax.dot_general(a, b, ((contract[:1], contract[1:]), ((), ())), preferred...  46.6 us
    pallas_call x1, Pallas kernels, attend_back(): pl.pallas_call(functools.partial(attend_back_kernel, ns=plan.ns, slots=sl...  29.5 us
    all_to_all x5, waiting for transfers between devices, exchange(): return lax.all_to_all(pieces, 'batch', 0, 0, tiled=True)  25.5 us
    all_to_all x5, starting transfers between devices, exchange(): return lax.all_to_all(pieces, 'batch', 0, 0, tiled=True)  25 us
  transfers between devices with their start and end apart: 110, of which 63 were waited for; matrix products, arithmetic and copies ran while one was open for 15% of the time, Pallas kernels for 25%

profile of v6, /device:TPU:4, one launch (start us, length us, event | category | flops | bytes accessed | tf_op | source)
XLA Modules:
  0.0 774.1 jit_solution(17963070996668060242)
XLA Ops:
  27.3 20.1 %all-to-all-done = bf16[8,64,1024]{2,1,0:T(8,128)(2,1)S(1)} async-done(((bf16[8,64,1024]{2,1,0:T(8,128)(2,1)}), bf16[8,64,1024]{2,1,0:T(8,128)(2,1)S(1)}, u32[]{:S(2)}, u32[]{:S(2)}) %all-to-all-start) | async-done | bytes 1048608 | tf_op jit(solution)/shard_map/all_to_all | solution.py:157
  85.4 15.6 %collective-permute-done.7.refs_2_ = bf16[256,2048]{1,0:T(8,128)(2,1)S(1)} collective-permute-done((bf16[256,2048]{1,0:T(8,128)(2,1)S(1)}, bf16[256,2048]{1,0:T(8,128)(2,1)S(1)}, u32[]{:S(2)}, u32[]{:S(2)}) %collective-permute-start.7) | collective-permute-done | bytes 1048608 | tf_op jit(solution)/shard_map/ppermute | solution.py:57
  104.8 12.6 %collective-permute-done.12.refs_4_ = bf16[128,2048]{1,0:T(8,128)(2,1)S(1)} collective-permute-done((bf16[128,2048]{1,0:T(8,128)(2,1)S(1)}, bf16[128,2048]{1,0:T(8,128)(2,1)S(1)}, u32[]{:S(2)}, u32[]{:S(2)}) %collective-permute-start.12) | collective-permute-done | bytes 524320 | tf_op jit(solution)/shard_map/ppermute | solution.py:57
  134.0 13.7 %project.1 = (bf16[2048,2048]{1,0:T(8,128)(2,1)}, f32[2048,768]{1,0:T(8,128)}) custom-call(bf16[256,2048]{1,0:T(8,128)(2,1)} %copy-done.13, bf16[256,2048]{1,0:T(8,128)(2,1)} %copy-done.18, bf16[256,2048]{1,0:T(8,128)(2,1)} %copy-done.17, bf16[128,2048]{1,0:T(8,128)(2,1)} %copy-done.53, bf16[128,2048]{1,0:T(8,128)(2,1)} %copy-done.52, ...), custom_call_target="tpu_custom_call" | custom-call | tf_op jit(solution)/shard_map/project/pallas_call | solution.py:371
  147.7 23.1 %attend.1 = (bf16[2048,768]{1,0:T(8,128)(2,1)}, f32[2048,256]{1,0:T(8,128)}, f32[2048,128]{1,0:T(8,128)S(1)}, f32[2,2048]{1,0:T(2,128)S(1)}) custom-call(s32[2,5]{1,0:T(2,128)S(1)} %pad_add_fusion.info, f32[2048,768]{1,0:T(8,128)} %get-tuple-element.293.proj, f32[1024,128]{1,0:T(8,128)S(1)} %get-tuple-element.294.cos_q, ...), custom_call_target="tpu_custom_call" | custom-call | tf_op jit(solution)/shard_map/attend/pallas_call | solution.py:683
  171.8 13.0 %collective-permute-done.15.refs_0_ = bf16[256,2048]{1,0:T(8,128)(2,1)} collective-permute-done((bf16[256,2048]{1,0:T(8,128)(2,1)}, bf16[256,2048]{1,0:T(8,128)(2,1)}, u32[]{:S(2)}, u32[]{:S(2)}) %collective-permute-start.15) | collective-permute-done | bytes 1048608 | tf_op jit(solution)/shard_map/ppermute | solution.py:838
  195.0 6.8 out_other.1
  229.0 10.1 %collective-permute-done.25 = bf16[256,1024]{1,0:T(8,128)(2,1)S(1)} collective-permute-done((bf16[256,1024]{1,0:T(8,128)(2,1)}, bf16[256,1024]{1,0:T(8,128)(2,1)S(1)}, u32[]{:S(2)}, u32[]{:S(2)}) %collective-permute-start.25) | collective-permute-done | bytes 524320 | tf_op jit(solution)/shard_map/ppermute | solution.py:57
  240.3 11.9 %collective-permute-done.26 = bf16[256,1024]{1,0:T(8,128)(2,1)S(1)} collective-permute-done((bf16[256,1024]{1,0:T(8,128)(2,1)S(1)}, bf16[256,1024]{1,0:T(8,128)(2,1)S(1)}, u32[]{:S(2)}, u32[]{:S(2)}) %collective-permute-start.26) | collective-permute-done | bytes 524320 | tf_op jit(solution)/shard_map/ppermute | solution.py:57
  258.5 21.2 %collective-permute-done.29.refs_2_ = bf16[256,2048]{1,0:T(8,128)(2,1)} collective-permute-done((bf16[256,2048]{1,0:T(8,128)(2,1)}, bf16[256,2048]{1,0:T(8,128)(2,1)}, u32[]{:S(2)}, u32[]{:S(2)}) %collective-permute-start.29) | collective-permute-done | bytes 1048608 | tf_op jit(solution)/shard_map/ppermute | solution.py:57
  285.4 11.6 %collective-permute-done.34.refs_4_ = bf16[128,2048]{1,0:T(8,128)(2,1)S(1)} collective-permute-done((bf16[128,2048]{1,0:T(8,128)(2,1)S(1)}, bf16[128,2048]{1,0:T(8,128)(2,1)S(1)}, u32[]{:S(2)}, u32[]{:S(2)}) %collective-permute-start.34) | collective-permute-done | bytes 524320 | tf_op jit(solution)/shard_map/ppermute | solution.py:57
  302.9 20.2 %up.1 = (bf16[2048,2048]{1,0:T(8,128)(2,1)}, f32[2048,1024]{1,0:T(8,128)}, f32[2048,1024]{1,0:T(8,128)}, f32[2,2048]{1,0:T(2,128)}) custom-call(bf16[256,2048]{1,0:T(8,128)(2,1)} %add_convert_fusion.refs_0_, bf16[256,2048]{1,0:T(8,128)(2,1)} %collective-permute-done.28.refs_1_, bf16[256,2048]{1,0:T(8,128)(2,1)} %collective-permute-done.29.refs_2_, ...), custom_call_target="tpu_custom_call" | custom-call | tf_op jit(solution)/shard_map/up/pallas_call | solution.py:371
  340.8 11.5 %collective-permute-done.43.refs_4_ = bf16[128,2048]{1,0:T(8,128)(2,1)} collective-permute-done((bf16[128,2048]{1,0:T(8,128)(2,1)}, bf16[128,2048]{1,0:T(8,128)(2,1)}, u32[]{:S(2)}, u32[]{:S(2)}) %collective-permute-start.43) | collective-permute-done | bytes 524320 | tf_op jit(solution)/shard_map/ppermute | solution.py:57
  355.8 21.5 %down_back.1 = (bf16[2048,2048]{1,0:T(8,128)(2,1)}, f32[2048,1024]{1,0:T(8,128)}, f32[2,2048]{1,0:T(2,128)}, f32[2,1024]{1,0:T(2,128)}, bf16[2048,1024]{1,0:T(8,128)(2,1)}) custom-call(bf16[256,2048]{1,0:T(8,128)(2,1)} %collective-permute-done.15.refs_0_, bf16[256,2048]{1,0:T(8,128)(2,1)} %collective-permute-done.37.refs_1_, ...), custom_call_target="tpu_custom_call" | custom-call | tf_op jit(solution)/shard_map/down_back/pallas_call | solution.py:371
  384.6 14.1 %convolution_convert_fusion.1 = bf16[2048,1024]{1,0:T(8,128)(2,1)} fusion(bf16[2048,2048]{1,0:T(8,128)(2,1)} %get-tuple-element.363, bf16[2048,1024]{1,0:T(8,128)(2,1)} %get-tuple-element.386.refs_0_), kind=kOutput, calls=%fused_computation.1 | convolution fusion | flops 8592031744 | bytes 16777216 | tf_op jit(solution)/shard_map/dot_general | solution.py:252
  399.8 13.6 %up_back_other.1 = (bf16[2048,1024]{1,0:T(8,128)(2,1)}, bf16[256,2048]{1,0:T(8,128)(2,1)}, bf16[256,2048]{1,0:T(8,128)(2,1)}, bf16[256,2048]{1,0:T(8,128)(2,1)}, bf16[256,2048]{1,0:T(8,128)(2,1)}) custom-call(f32[2048,1024]{1,0:T(8,128)} %get-tuple-element.360.refs_0_, f32[2048,1024]{1,0:T(8,128)} %get-tuple-element.356.refs_11_.refs_1_, ...), custom_call_target="tpu_custom_call" | custom-call | tf_op jit(solution)/shard_map/up_back_other/pallas_call | solution.py:502
  418.9 9.6 %up_back_own_x.1 = (bf16[2048,1024]{1,0:T(8,128)(2,1)}, bf16[512,1024]{1,0:T(8,128)(2,1)}, bf16[256,1024]{1,0:T(8,128)(2,1)}, f32[256,1024]{1,0:T(8,128)}) custom-call(f32[2048,1024]{1,0:T(8,128)} %get-tuple-element.360.refs_0_, f32[2048,1024]{1,0:T(8,128)} %get-tuple-element.356.refs_11_.refs_1_, ...), custom_call_target="tpu_custom_call", output_to_operand_aliasing={{0}: (9, {})} | custom-call | tf_op jit(solution)/shard_map/up_back_own_x/pallas_call | solution.py:502
  429.7 9.8 %up_back_own_y.1 = (bf16[2048,1024]{1,0:T(8,128)(2,1)}, bf16[256,1024]{1,0:T(8,128)(2,1)}, f32[256,2048]{1,0:T(8,128)}, f32[256,1024]{1,0:T(8,128)}) custom-call(f32[2048,1024]{1,0:T(8,128)} %get-tuple-element.360.refs_0_, f32[2048,1024]{1,0:T(8,128)} %get-tuple-element.356.refs_11_.refs_1_, ...), custom_call_target="tpu_custom_call", output_to_operand_aliasing={{0}: (9, {})} | custom-call | tf_op jit(solution)/shard_map/up_back_own_y/pallas_call | solution.py:502
  443.0 14.1 %convolution_convert_fusion = bf16[2048,1024]{1,0:T(8,128)(2,1)} fusion(bf16[2048,2048]{1,0:T(8,128)(2,1)} %get-tuple-element.376, bf16[2048,1024]{1,0:T(8,128)(2,1)} %get-tuple-element.377), kind=kOutput, calls=%fused_computation | convolution fusion | flops 8592031744 | bytes 16777216 | tf_op jit(solution)/shard_map/dot_general | solution.py:252
  457.1 8.0 %collective-permute-done.57 = bf16[256,1024]{1,0:T(8,128)(2,1)} collective-permute-done((bf16[256,1024]{1,0:T(8,128)(2,1)}, bf16[256,1024]{1,0:T(8,128)(2,1)}, u32[]{:S(2)}, u32[]{:S(2)}) %collective-permute-start.57) | collective-permute-done | bytes 524320 | tf_op jit(solution)/shard_map/ppermute | solution.py:57
  472.5 10.2 %down_other.1 = (bf16[256,2048]{1,0:T(8,128)(2,1)}, bf16[256,2048]{1,0:T(8,128)(2,1)}, bf16[256,2048]{1,0:T(8,128)(2,1)}, bf16[256,2048]{1,0:T(8,128)(2,1)}) custom-call(bf16[2048,1024]{1,0:T(8,128)(2,1)} %get-tuple-element.386.refs_0_, bf16[2048,1024]{1,0:T(8,128)(2,1)} %all-gather.11.cloned.1.call-done.refs_10_.refs_1_), custom_call_target="tpu_custom_call" | custom-call | tf_op jit(solution)/shard_map/down_other/pallas_call | solution.py:502
  492.2 7.5 down_own_x.1
  500.7 7.7 %down_own_y.1 = (bf16[256,1024]{1,0:T(8,128)(2,1)}, f32[256,2048]{1,0:T(8,128)}, f32[256,1024]{1,0:T(8,128)}) custom-call(bf16[2048,1024]{1,0:T(8,128)(2,1)} %get-tuple-element.386.refs_0_, bf16[2048,1024]{1,0:T(8,128)(2,1)} %all-gather.11.cloned.1.call-done.refs_10_.refs_1_, bf16[256,2048]{1,0:T(8,128)(2,1)} %copy-done.24, ...), custom_call_target="tpu_custom_call" | custom-call | tf_op jit(solution)/shard_map/down_own_y/pallas_call | solution.py:502
  508.4 7.0 collective-permute-done.66.refs_2_
  518.3 13.4 %collective-permute-done.71.refs_4_ = bf16[128,2048]{1,0:T(8,128)(2,1)S(1)} collective-permute-done((bf16[128,2048]{1,0:T(8,128)(2,1)S(1)}, bf16[128,2048]{1,0:T(8,128)(2,1)S(1)}, u32[]{:S(2)}, u32[]{:S(2)}) %collective-permute-start.71) | collective-permute-done | bytes 524320 | tf_op jit(solution)/shard_map/ppermute | solution.py:57
  539.6 12.9 %out_back.1 = (bf16[2048,2048]{1,0:T(8,128)(2,1)}, f32[2048,256]{1,0:T(8,128)}, f32[2,2048]{1,0:T(2,128)}, f32[2,256]{1,0:T(2,128)}) custom-call(bf16[256,2048]{1,0:T(8,128)(2,1)} %copy-done.12, bf16[256,2048]{1,0:T(8,128)(2,1)} %copy-done.16, bf16[256,2048]{1,0:T(8,128)(2,1)} %copy-done.15, bf16[128,2048]{1,0:T(8,128)(2,1)} %copy-done.58, ...), custom_call_target="tpu_custom_call" | custom-call | tf_op jit(solution)/shard_map/out_back/pallas_call | solution.py:371
  561.4 7.1 convolution_convert_fusion.3
  581.0 29.5 %attend_back.1.refs_0_ = bf16[2048,768]{1,0:T(8,128)(2,1)} custom-call(s32[2,5]{1,0:T(2,128)S(1)} %pad_add_fusion.info, bf16[2048,768]{1,0:T(8,128)(2,1)} %get-tuple-element.440.qkv, f32[2048,256]{1,0:T(8,128)} %get-tuple-element.299.refs_0_.refs_11_.attended, f32[2048,256]{1,0:T(8,128)} %get-tuple-element.441.grad, f32[2,2048]{1,0:T(2,128)S(1)} %copy-done.3, ...), custom_call_target="tpu_custom_call" | custom-call | tf_op jit(solution)/shard_map/attend_back/pallas_call | solution.py:717
  610.6 11.4 %convolution_convert_fusion.2 = bf16[2048,768]{1,0:T(8,128)(2,1)} fusion(bf16[2048,2048]{1,0:T(8,128)(2,1)} %get-tuple-element.447, bf16[2048,768]{1,0:T(8,128)(2,1)} %attend_back.1.refs_0_), kind=kOutput, calls=%fused_computation.2 | convolution fusion | flops 6444023808 | bytes 14680064 | tf_op jit(solution)/shard_map/dot_general | solution.py:252
  621.9 8.6 %project_back_other.1 = (bf16[256,2048]{1,0:T(8,128)(2,1)}, bf16[256,2048]{1,0:T(8,128)(2,1)}, bf16[256,2048]{1,0:T(8,128)(2,1)}, bf16[256,2048]{1,0:T(8,128)(2,1)}) custom-call(bf16[2048,768]{1,0:T(8,128)(2,1)} %attend_back.1.refs_0_, bf16[2048,768]{1,0:T(8,128)(2,1)} %all-gather.5.cloned.1.call-done.refs_10_.refs_1_), custom_call_target="tpu_custom_call" | custom-call | tf_op jit(solution)/shard_map/project_back_other/pallas_call | solution.py:502
  668.9 9.4 %collective-permute-done.87 = bf16[256,1024]{1,0:T(8,128)(2,1)S(1)} collective-permute-done((bf16[256,1024]{1,0:T(8,128)(2,1)}, bf16[256,1024]{1,0:T(8,128)(2,1)S(1)}, u32[]{:S(2)}, u32[]{:S(2)}) %collective-permute-start.87) | collective-permute-done | bytes 524320 | tf_op jit(solution)/shard_map/ppermute | solution.py:57
  722.4 19.1 %collective-permute-done.96.values = bf16[256,2048]{1,0:T(8,128)(2,1)S(1)} collective-permute-done((bf16[256,2048]{1,0:T(8,128)(2,1)S(1)}, bf16[256,2048]{1,0:T(8,128)(2,1)S(1)}, u32[]{:S(2)}, u32[]{:S(2)}) %collective-permute-start.96) | collective-permute-done | bytes 1048608 | tf_op jit(solution)/shard_map/ppermute | solution.py:961
  (592 shorter events, 327.4 us)
Async XLA Ops:
  13.9 40.2 %collective-permute-start = (bf16[256,2048]{1,0:T(8,128)(2,1)S(1)}, bf16[256,2048]{1,0:T(8,128)(2,1)S(1)}, u32[]{:S(2)}, u32[]{:S(2)}) collective-permute-start(bf16[256,2048]{1,0:T(8,128)(2,1)S(1)} %reorder.4), channel_id=1, source_target_pairs={{0,27},{1,19},{2,11},{3,3},{4,4},{5,12},{6,20},{7,28},{8,13},{9,5}... | collective-permute-start | bytes 3145736 | tf_op jit(solution)/shard_map/ppermute | solution.py:787
  19.2 28.2 %all-to-all-start = ((bf16[8,64,1024]{2,1,0:T(8,128)(2,1)}), bf16[8,64,1024]{2,1,0:T(8,128)(2,1)S(1)}, u32[]{:S(2)}, u32[]{:S(2)}) async-start(bf16[8,64,1024]{2,1,0:T(8,128)(2,1)} %pad_maximum_fusion.4), calls=%async_computation | async-start | bytes 2097152 | tf_op jit(solution)/shard_map/all_to_all | solution.py:157
  25.2 108.7 %all-gather.5.cloned.1.call-start = ((), (), s32[]{:S(2)}) async-start(), calls=%async_computation.9 | async-start | bytes 3932160 | tf_op jit(solution)/shard_map/all_gather | solution.py:162
  77.4 23.6 %collective-permute-start.7 = (bf16[256,2048]{1,0:T(8,128)(2,1)S(1)}, bf16[256,2048]{1,0:T(8,128)(2,1)S(1)}, u32[]{:S(2)}, u32[]{:S(2)}) collective-permute-start(bf16[256,2048]{1,0:T(8,128)(2,1)S(1)} %fusion.7.refs_0_), channel_id=1, source_target_pairs={{0,16},{4,20},{8,24},{12,28},{16,0},{20,4},{24,8},{28,12},{1,17},{... | collective-permute-start | bytes 3145736 | tf_op jit(solution)/shard_map/ppermute | solution.py:57
  79.4 23.1 %collective-permute-start.6 = (bf16[256,2048]{1,0:T(8,128)(2,1)S(1)}, bf16[256,2048]{1,0:T(8,128)(2,1)S(1)}, u32[]{:S(2)}, u32[]{:S(2)}) collective-permute-start(bf16[256,2048]{1,0:T(8,128)(2,1)S(1)} %fusion.7.refs_0_), channel_id=1, source_target_pairs={{0,8},{4,12},{8,0},{12,4},{16,24},{20,28},{24,16},{28,20},{1,9},{5... | collective-permute-start | bytes 3145736 | tf_op jit(solution)/shard_map/ppermute | solution.py:57
  123.0 61.8 %all-to-all-start.1 = ((bf16[8,64,2048]{2,1,0:T(8,128)(2,1)}), bf16[8,64,2048]{2,1,0:T(8,128)(2,1)}, u32[]{:S(2)}, u32[]{:S(2)}) async-start(bf16[8,64,2048]{2,1,0:T(8,128)(2,1)} %pad_maximum_fusion), calls=%async_computation.1 | async-start | bytes 4194304 | tf_op jit(solution)/shard_map/all_to_all | solution.py:157
  127.6 67.4 %all-gather.7.cloned.1.call-start = ((), (), s32[]{:S(2)}) async-start(), calls=%async_computation.10 | async-start | bytes 1310720 | tf_op jit(solution)/shard_map/all_gather | solution.py:162
  127.6 57.2 %collective-permute-start.15 = (bf16[256,2048]{1,0:T(8,128)(2,1)}, bf16[256,2048]{1,0:T(8,128)(2,1)}, u32[]{:S(2)}, u32[]{:S(2)}) collective-permute-start(bf16[256,2048]{1,0:T(8,128)(2,1)} %reorder.5), channel_id=1, source_target_pairs={{0,27},{1,19},{2,11},{3,3},{4,4},{5,12},{6,20},{7,28},{8,13},{9,5}... | collective-permute-start | bytes 3145736 | tf_op jit(solution)/shard_map/ppermute | solution.py:838
  133.3 169.6 %all-gather.9.cloned.1.call-start = ((), (), s32[]{:S(2)}) async-start(), calls=%async_computation.11 | async-start | bytes 5242880 | tf_op jit(solution)/shard_map/all_gather | solution.py:162
  189.5 164.4 %all-gather.11.cloned.1.call-start = ((), (), s32[]{:S(2)}) async-start(), calls=%async_computation.12 | async-start | bytes 5242880 | tf_op jit(solution)/shard_map/all_gather | solution.py:162
  212.4 26.7 %collective-permute-start.23 = (bf16[512,1024]{1,0:T(8,128)(2,1)}, bf16[512,1024]{1,0:T(8,128)(2,1)S(1)}, u32[]{:S(2)}, u32[]{:S(2)}) collective-permute-start(bf16[512,1024]{1,0:T(8,128)(2,1)} %get-tuple-element.314), channel_id=1, source_target_pairs={{0,8},{4,12},{8,0},{12,4},{16,24},{20,28},{24,16},{28,20},{1,9},{5... | collective-permute-start | bytes 3145736 | tf_op jit(solution)/shard_map/ppermute | solution.py:57
  256.1 23.5 %collective-permute-start.29 = (bf16[256,2048]{1,0:T(8,128)(2,1)}, bf16[256,2048]{1,0:T(8,128)(2,1)}, u32[]{:S(2)}, u32[]{:S(2)}) collective-permute-start(bf16[256,2048]{1,0:T(8,128)(2,1)} %add_convert_fusion.refs_0_), channel_id=1, source_target_pairs={{0,16},{4,20},{8,24},{12,28},{16,0},{20,4},{24,8},{28,12},{1,17},{... | collective-permute-start | bytes 3145736 | tf_op jit(solution)/shard_map/ppermute | solution.py:57
  256.5 23.5 %collective-permute-start.28 = (bf16[256,2048]{1,0:T(8,128)(2,1)}, bf16[256,2048]{1,0:T(8,128)(2,1)}, u32[]{:S(2)}, u32[]{:S(2)}) collective-permute-start(bf16[256,2048]{1,0:T(8,128)(2,1)} %add_convert_fusion.refs_0_), channel_id=1, source_target_pairs={{0,8},{4,12},{8,0},{12,4},{16,24},{20,28},{24,16},{28,20},{1,9},{5... | collective-permute-start | bytes 3145736 | tf_op jit(solution)/shard_map/ppermute | solution.py:57
  258.2 276.8 %reduce-scatter.5.cloned.1.call-start = ((), (), s32[]{:S(2)}) async-start(), calls=%async_computation.13 | async-start | bytes 5242880 | tf_op jit(solution)/shard_map/reduce_scatter | solution.py:166
  301.1 25.5 %collective-permute-start.38 = (bf16[256,2048]{1,0:T(8,128)(2,1)}, bf16[256,2048]{1,0:T(8,128)(2,1)}, u32[]{:S(2)}, u32[]{:S(2)}) collective-permute-start(bf16[256,2048]{1,0:T(8,128)(2,1)} %collective-permute-done.15.refs_0_), channel_id=1, source_target_pairs={{0,16},{4,20},{8,24},{12,28},{16,0},{20,4},{24,8},{28,12},{1,17},{... | collective-permute-start | bytes 3145736 | tf_op jit(solution)/shard_map/ppermute | solution.py:57
  302.3 25.2 %collective-permute-start.37 = (bf16[256,2048]{1,0:T(8,128)(2,1)}, bf16[256,2048]{1,0:T(8,128)(2,1)}, u32[]{:S(2)}, u32[]{:S(2)}) collective-permute-start(bf16[256,2048]{1,0:T(8,128)(2,1)} %collective-permute-done.15.refs_0_), channel_id=1, source_target_pairs={{0,8},{4,12},{8,0},{12,4},{16,24},{20,28},{24,16},{28,20},{1,9},{5... | collective-permute-start | bytes 3145736 | tf_op jit(solution)/shard_map/ppermute | solution.py:57
  330.6 22.1 %collective-permute-start.39 = (bf16[256,2048]{1,0:T(8,128)(2,1)}, bf16[256,2048]{1,0:T(8,128)(2,1)}, u32[]{:S(2)}, u32[]{:S(2)}) collective-permute-start(bf16[256,2048]{1,0:T(8,128)(2,1)} %collective-permute-done.15.refs_0_), channel_id=1, source_target_pairs={{0,4},{4,0},{8,12},{12,8},{16,20},{20,16},{24,28},{28,24},{1,5},{5... | collective-permute-start | bytes 3145736 | tf_op jit(solution)/shard_map/ppermute | solution.py:57
  399.4 169.2 %reduce-scatter.7.cloned.1.call-start = ((), (), s32[]{:S(2)}) async-start(), calls=%async_computation.14 | async-start | bytes 5242880 | tf_op jit(solution)/shard_map/reduce_scatter | solution.py:166
  440.3 24.8 %collective-permute-start.57 = (bf16[256,1024]{1,0:T(8,128)(2,1)}, bf16[256,1024]{1,0:T(8,128)(2,1)}, u32[]{:S(2)}, u32[]{:S(2)}) collective-permute-start(bf16[256,1024]{1,0:T(8,128)(2,1)} %get-tuple-element.374), channel_id=1, source_target_pairs={{0,16},{4,20},{8,24},{12,28},{16,0},{20,4},{24,8},{28,12},{1,17},{... | collective-permute-start | bytes 1572872 | tf_op jit(solution)/shard_map/ppermute | solution.py:57
  441.6 24.9 %collective-permute-start.56 = (bf16[512,1024]{1,0:T(8,128)(2,1)}, bf16[512,1024]{1,0:T(8,128)(2,1)}, u32[]{:S(2)}, u32[]{:S(2)}) collective-permute-start(bf16[512,1024]{1,0:T(8,128)(2,1)} %get-tuple-element.373), channel_id=1, source_target_pairs={{0,8},{4,12},{8,0},{12,4},{16,24},{20,28},{24,16},{28,20},{1,9},{5... | collective-permute-start | bytes 3145736 | tf_op jit(solution)/shard_map/ppermute | solution.py:57
  491.0 24.5 %collective-permute-start.66 = (bf16[256,2048]{1,0:T(8,128)(2,1)S(1)}, bf16[256,2048]{1,0:T(8,128)(2,1)S(1)}, u32[]{:S(2)}, u32[]{:S(2)}) collective-permute-start(bf16[256,2048]{1,0:T(8,128)(2,1)S(1)} %get-tuple-element.415.refs_0_), channel_id=1, source_target_pairs={{0,16},{4,20},{8,24},{12,28},{16,0},{20,4},{24,8},{28,12},{1,17},{... | collective-permute-start | bytes 3145736 | tf_op jit(solution)/shard_map/ppermute | solution.py:57
  491.8 25.0 %collective-permute-start.65 = (bf16[256,2048]{1,0:T(8,128)(2,1)S(1)}, bf16[256,2048]{1,0:T(8,128)(2,1)S(1)}, u32[]{:S(2)}, u32[]{:S(2)}) collective-permute-start(bf16[256,2048]{1,0:T(8,128)(2,1)S(1)} %get-tuple-element.415.refs_0_), channel_id=1, source_target_pairs={{0,8},{4,12},{8,0},{12,4},{16,24},{20,28},{24,16},{28,20},{1,9},{5... | collective-permute-start | bytes 3145736 | tf_op jit(solution)/shard_map/ppermute | solution.py:57
  539.6 82.4 %reduce-scatter.9.cloned.1.call-start = ((), (), s32[]{:S(2)}) async-start(), calls=%async_computation.15 | async-start | bytes 1310720 | tf_op jit(solution)/shard_map/reduce_scatter | solution.py:166
  568.6 42.0 %collective-permute-start.77 = (bf16[512,1024]{1,0:T(8,128)(2,1)}, bf16[512,1024]{1,0:T(8,128)(2,1)}, u32[]{:S(2)}, u32[]{:S(2)}) collective-permute-start(bf16[512,1024]{1,0:T(8,128)(2,1)} %get-tuple-element.437), channel_id=1, source_target_pairs={{0,8},{4,12},{8,0},{12,4},{16,24},{20,28},{24,16},{28,20},{1,9},{5... | collective-permute-start | bytes 3145736 | tf_op jit(solution)/shard_map/ppermute | solution.py:57
  569.2 41.4 %collective-permute-start.78 = (bf16[256,1024]{1,0:T(8,128)(2,1)}, bf16[256,1024]{1,0:T(8,128)(2,1)}, u32[]{:S(2)}, u32[]{:S(2)}) collective-permute-start(bf16[256,1024]{1,0:T(8,128)(2,1)} %get-tuple-element.438), channel_id=1, source_target_pairs={{0,16},{4,20},{8,24},{12,28},{16,0},{20,4},{24,8},{28,12},{1,17},{... | collective-permute-start | bytes 1572872 | tf_op jit(solution)/shard_map/ppermute | solution.py:57
  569.8 40.7 %collective-permute-start.79 = (bf16[256,1024]{1,0:T(8,128)(2,1)}, bf16[256,1024]{1,0:T(8,128)(2,1)}, u32[]{:S(2)}, u32[]{:S(2)}) collective-permute-start(bf16[256,1024]{1,0:T(8,128)(2,1)} %get-tuple-element.439), channel_id=1, source_target_pairs={{0,16},{4,20},{8,24},{12,28},{16,0},{20,4},{24,8},{28,12},{1,17},{... | collective-permute-start | bytes 1572872 | tf_op jit(solution)/shard_map/ppermute | solution.py:57
  575.0 47.0 %all-to-all-start.3 = ((bf16[8,64,1024]{2,1,0:T(8,128)(2,1)}), bf16[8,64,1024]{2,1,0:T(8,128)(2,1)}, u32[]{:S(2)}, u32[]{:S(2)}) async-start(bf16[8,64,1024]{2,1,0:T(8,128)(2,1)} %bitcast.134), calls=%async_computation.5 | async-start | bytes 2097152 | tf_op jit(solution)/shard_map/all_to_all | solution.py:157
  579.8 123.5 %reduce-scatter.11.cloned.1.call-start = ((), (), s32[]{:S(2)}) async-start(), calls=%async_computation.16 | async-start | bytes 3932160 | tf_op jit(solution)/shard_map/reduce_scatter | solution.py:166
  646.4 31.8 %collective-permute-start.85 = (bf16[512,1024]{1,0:T(8,128)(2,1)}, bf16[512,1024]{1,0:T(8,128)(2,1)S(1)}, u32[]{:S(2)}, u32[]{:S(2)}) collective-permute-start(bf16[512,1024]{1,0:T(8,128)(2,1)} %get-tuple-element.456), channel_id=1, source_target_pairs={{0,8},{4,12},{8,0},{12,4},{16,24},{20,28},{24,16},{28,20},{1,9},{5... | collective-permute-start | bytes 3145736 | tf_op jit(solution)/shard_map/ppermute | solution.py:57
  705.8 41.3 %all-to-all-start.4 = ((bf16[8,80,1024]{2,1,0:T(8,128)(2,1)}), bf16[8,80,1024]{2,1,0:T(8,128)(2,1)}, u32[]{:S(2)}, u32[]{:S(2)}) async-start(bf16[8,80,1024]{2,1,0:T(8,128)(2,1)} %pad_maximum_fusion.3), calls=%async_computation.8 | async-start | bytes 2621440 | tf_op jit(solution)/shard_map/all_to_all | solution.py:157
  710.8 30.6 %collective-permute-start.96 = (bf16[256,2048]{1,0:T(8,128)(2,1)S(1)}, bf16[256,2048]{1,0:T(8,128)(2,1)S(1)}, u32[]{:S(2)}, u32[]{:S(2)}) collective-permute-start(bf16[256,2048]{1,0:T(8,128)(2,1)S(1)} %copy-done.23), channel_id=1, source_target_pairs={{27,0},{19,1},{11,2},{3,3},{4,4},{12,5},{20,6},{28,7},{13,8},{5,9}... | collective-permute-start | bytes 3145736 | tf_op jit(solution)/shard_map/ppermute | solution.py:961
  717.1 46.4 %collective-permute-start.95 = (bf16[256,2048]{1,0:T(8,128)(2,1)}, bf16[256,2048]{1,0:T(8,128)(2,1)S(1)}, u32[]{:S(2)}, u32[]{:S(2)}) collective-permute-start(bf16[256,2048]{1,0:T(8,128)(2,1)} %fusion.12), channel_id=1, source_target_pairs={{27,0},{19,1},{11,2},{3,3},{4,4},{12,5},{20,6},{28,7},{13,8},{5,9}... | collective-permute-start | bytes 3145736 | tf_op jit(solution)/shard_map/ppermute | solution.py:972
  (159 other events, 1615.0 us)
Sparse Core Ops, SparseCore 0:
  59.4 64.7 all-gather.4
  133.5 39.1 all-gather.6
  189.6 80.4 all-gather.8
  271.5 79.2 all-gather.10
  399.5 76.5 reduce-scatter.4
  478.3 77.2 reduce-scatter.6
  571.3 27.8 reduce-scatter.8
  630.8 61.1 reduce-scatter.10

commit v7 on v4

--- a/solution.py
+++ b/solution.py
@@ -350,7 +350,7 @@
 
 
 def pieces_matmul(arrays, weights, columns, end, extra, outs, name):
-    step = ROWS_AT_ONCE
+    step = 2 * ROWS_AT_ONCE
     moves, total = moves_of(arrays, step)
     loads, inner = [], 0
     for index, weight in enumerate(weights):

time: 783 us -> 782 us (level)
  transfers between devices with their start and end apart: 110 -> 110, of which waited for: 62 -> 62; matrix products, arithmetic and copies ran while one was open for 15% -> 15% of each run, Pallas kernels for 25% -> 24%
where the time goes in v7:
time: 782 us; the launch traced here: 773 us
  waiting for transfers between devices  291 us (37%)
  Pallas kernels  221 us (28%)
  starting transfers between devices  99.1 us (13%)
  local copies, waits for them, and re-layouts  49.3 us (6%)
  matrix products  46.6 us (6%)
  other arithmetic  45.5 us (6%)
  between operations  20.9 us (3%)
    ppermute x93, waiting for transfers between devices, swap_over(): return lax.ppermute(value, axis, [(i, i ^ step) for i in range(size)])  218 us
    pallas_call x12, Pallas kernels, part_call(): pl.pallas_call(functools.partial(part_kernel, n_in=len(ins), make_left=ma...  98.6 us
    pallas_call x4, Pallas kernels, pieces_matmul(): pl.pallas_call(functools.partial(pieces_kernel, moves=moves, loads=loads,...  64.6 us
    ppermute x93, starting transfers between devices, swap_over(): return lax.ppermute(value, axis, [(i, i ^ step) for i in range(size)])  56.9 us
    dot_general x4, matrix products, matmul(): lax.dot_general(a, b, ((contract[:1], contract[1:]), ((), ())), preferred...  46.6 us
    pallas_call x1, Pallas kernels, attend_back(): pl.pallas_call(functools.partial(attend_back_kernel, ns=plan.ns, slots=sl...  29.5 us
    all_to_all x5, waiting for transfers between devices, exchange(): return lax.all_to_all(pieces, 'batch', 0, 0, tiled=True)  27.1 us
    all_to_all x5, starting transfers between devices, exchange(): return lax.all_to_all(pieces, 'batch', 0, 0, tiled=True)  25.1 us
  transfers between devices with their start and end apart: 110, of which 62 were waited for; matrix products, arithmetic and copies ran while one was open for 15% of the time, Pallas kernels for 24%

profile of v7, /device:TPU:4, one launch (start us, length us, event | category | flops | bytes accessed | tf_op | source)
XLA Modules:
  0.0 773.3 jit_solution(17045565377871234758)
XLA Ops:
  27.3 20.1 %all-to-all-done = bf16[8,64,1024]{2,1,0:T(8,128)(2,1)S(1)} async-done(((bf16[8,64,1024]{2,1,0:T(8,128)(2,1)}), bf16[8,64,1024]{2,1,0:T(8,128)(2,1)S(1)}, u32[]{:S(2)}, u32[]{:S(2)}) %all-to-all-start) | async-done | bytes 1048608 | tf_op jit(solution)/shard_map/all_to_all | solution.py:156
  85.4 15.6 %collective-permute-done.7.refs_2_ = bf16[256,2048]{1,0:T(8,128)(2,1)S(1)} collective-permute-done((bf16[256,2048]{1,0:T(8,128)(2,1)S(1)}, bf16[256,2048]{1,0:T(8,128)(2,1)S(1)}, u32[]{:S(2)}, u32[]{:S(2)}) %collective-permute-start.7) | collective-permute-done | bytes 1048608 | tf_op jit(solution)/shard_map/ppermute | solution.py:57
  104.8 12.6 %collective-permute-done.12.refs_4_ = bf16[128,2048]{1,0:T(8,128)(2,1)S(1)} collective-permute-done((bf16[128,2048]{1,0:T(8,128)(2,1)S(1)}, bf16[128,2048]{1,0:T(8,128)(2,1)S(1)}, u32[]{:S(2)}, u32[]{:S(2)}) %collective-permute-start.12) | collective-permute-done | bytes 524320 | tf_op jit(solution)/shard_map/ppermute | solution.py:57
  134.0 12.8 %project.1 = (bf16[2048,2048]{1,0:T(8,128)(2,1)}, f32[2048,768]{1,0:T(8,128)}) custom-call(bf16[256,2048]{1,0:T(8,128)(2,1)} %copy-done.13, bf16[256,2048]{1,0:T(8,128)(2,1)} %copy-done.18, bf16[256,2048]{1,0:T(8,128)(2,1)} %copy-done.17, bf16[128,2048]{1,0:T(8,128)(2,1)} %copy-done.53, bf16[128,2048]{1,0:T(8,128)(2,1)} %copy-done.52, ...), custom_call_target="tpu_custom_call" | custom-call | tf_op jit(solution)/shard_map/project/pallas_call | solution.py:370
  146.8 23.1 %attend.1 = (bf16[2048,768]{1,0:T(8,128)(2,1)}, f32[2048,256]{1,0:T(8,128)}, f32[2048,128]{1,0:T(8,128)S(1)}, f32[2,2048]{1,0:T(2,128)S(1)}) custom-call(s32[2,5]{1,0:T(2,128)S(1)} %pad_add_fusion.info, f32[2048,768]{1,0:T(8,128)} %get-tuple-element.292.proj, f32[1024,128]{1,0:T(8,128)S(1)} %get-tuple-element.293.cos_q, ...), custom_call_target="tpu_custom_call" | custom-call | tf_op jit(solution)/shard_map/attend/pallas_call | solution.py:682
  170.9 13.9 %collective-permute-done.15.refs_0_ = bf16[256,2048]{1,0:T(8,128)(2,1)} collective-permute-done((bf16[256,2048]{1,0:T(8,128)(2,1)}, bf16[256,2048]{1,0:T(8,128)(2,1)}, u32[]{:S(2)}, u32[]{:S(2)}) %collective-permute-start.15) | collective-permute-done | bytes 1048608 | tf_op jit(solution)/shard_map/ppermute | solution.py:837
  229.0 10.1 %collective-permute-done.25 = bf16[256,1024]{1,0:T(8,128)(2,1)S(1)} collective-permute-done((bf16[256,1024]{1,0:T(8,128)(2,1)}, bf16[256,1024]{1,0:T(8,128)(2,1)S(1)}, u32[]{:S(2)}, u32[]{:S(2)}) %collective-permute-start.25) | collective-permute-done | bytes 524320 | tf_op jit(solution)/shard_map/ppermute | solution.py:57
  240.3 11.9 %collective-permute-done.26 = bf16[256,1024]{1,0:T(8,128)(2,1)S(1)} collective-permute-done((bf16[256,1024]{1,0:T(8,128)(2,1)S(1)}, bf16[256,1024]{1,0:T(8,128)(2,1)S(1)}, u32[]{:S(2)}, u32[]{:S(2)}) %collective-permute-start.26) | collective-permute-done | bytes 524320 | tf_op jit(solution)/shard_map/ppermute | solution.py:57
  258.5 21.2 %collective-permute-done.29.refs_2_ = bf16[256,2048]{1,0:T(8,128)(2,1)} collective-permute-done((bf16[256,2048]{1,0:T(8,128)(2,1)}, bf16[256,2048]{1,0:T(8,128)(2,1)}, u32[]{:S(2)}, u32[]{:S(2)}) %collective-permute-start.29) | collective-permute-done | bytes 1048608 | tf_op jit(solution)/shard_map/ppermute | solution.py:57
  285.4 11.6 %collective-permute-done.34.refs_4_ = bf16[128,2048]{1,0:T(8,128)(2,1)S(1)} collective-permute-done((bf16[128,2048]{1,0:T(8,128)(2,1)S(1)}, bf16[128,2048]{1,0:T(8,128)(2,1)S(1)}, u32[]{:S(2)}, u32[]{:S(2)}) %collective-permute-start.34) | collective-permute-done | bytes 524320 | tf_op jit(solution)/shard_map/ppermute | solution.py:57
  302.9 19.8 %up.1 = (bf16[2048,2048]{1,0:T(8,128)(2,1)}, f32[2048,1024]{1,0:T(8,128)}, f32[2048,1024]{1,0:T(8,128)}, f32[2,2048]{1,0:T(2,128)}) custom-call(bf16[256,2048]{1,0:T(8,128)(2,1)} %add_convert_fusion.refs_0_, bf16[256,2048]{1,0:T(8,128)(2,1)} %collective-permute-done.28.refs_1_, bf16[256,2048]{1,0:T(8,128)(2,1)} %collective-permute-done.29.refs_2_, ...), custom_call_target="tpu_custom_call" | custom-call | tf_op jit(solution)/shard_map/up/pallas_call | solution.py:370
  340.8 11.5 %collective-permute-done.43.refs_4_ = bf16[128,2048]{1,0:T(8,128)(2,1)} collective-permute-done((bf16[128,2048]{1,0:T(8,128)(2,1)}, bf16[128,2048]{1,0:T(8,128)(2,1)}, u32[]{:S(2)}, u32[]{:S(2)}) %collective-permute-start.43) | collective-permute-done | bytes 524320 | tf_op jit(solution)/shard_map/ppermute | solution.py:57
  355.8 20.8 %down_back.1 = (bf16[2048,2048]{1,0:T(8,128)(2,1)}, f32[2048,1024]{1,0:T(8,128)}, f32[2,2048]{1,0:T(2,128)}, f32[2,1024]{1,0:T(2,128)}, bf16[2048,1024]{1,0:T(8,128)(2,1)}) custom-call(bf16[256,2048]{1,0:T(8,128)(2,1)} %collective-permute-done.15.refs_0_, bf16[256,2048]{1,0:T(8,128)(2,1)} %collective-permute-done.37.refs_1_, ...), custom_call_target="tpu_custom_call" | custom-call | tf_op jit(solution)/shard_map/down_back/pallas_call | solution.py:370
  383.8 14.0 %convolution_convert_fusion.1 = bf16[2048,1024]{1,0:T(8,128)(2,1)} fusion(bf16[2048,2048]{1,0:T(8,128)(2,1)} %get-tuple-element.362, bf16[2048,1024]{1,0:T(8,128)(2,1)} %get-tuple-element.385.refs_0_), kind=kOutput, calls=%fused_computation.1 | convolution fusion | flops 8592031744 | bytes 16777216 | tf_op jit(solution)/shard_map/dot_general | solution.py:251
  398.6 14.0 %up_back_other.1 = (bf16[2048,1024]{1,0:T(8,128)(2,1)}, bf16[256,2048]{1,0:T(8,128)(2,1)}, bf16[256,2048]{1,0:T(8,128)(2,1)}, bf16[256,2048]{1,0:T(8,128)(2,1)}, bf16[256,2048]{1,0:T(8,128)(2,1)}) custom-call(f32[2048,1024]{1,0:T(8,128)} %get-tuple-element.359.refs_0_, f32[2048,1024]{1,0:T(8,128)} %get-tuple-element.355.refs_11_.refs_1_, ...), custom_call_target="tpu_custom_call" | custom-call | tf_op jit(solution)/shard_map/up_back_other/pallas_call | solution.py:501
  418.1 9.6 %up_back_own_x.1 = (bf16[2048,1024]{1,0:T(8,128)(2,1)}, bf16[512,1024]{1,0:T(8,128)(2,1)}, bf16[256,1024]{1,0:T(8,128)(2,1)}, f32[256,1024]{1,0:T(8,128)}) custom-call(f32[2048,1024]{1,0:T(8,128)} %get-tuple-element.359.refs_0_, f32[2048,1024]{1,0:T(8,128)} %get-tuple-element.355.refs_11_.refs_1_, ...), custom_call_target="tpu_custom_call", output_to_operand_aliasing={{0}: (9, {})} | custom-call | tf_op jit(solution)/shard_map/up_back_own_x/pallas_call | solution.py:501
  429.0 9.8 %up_back_own_y.1 = (bf16[2048,1024]{1,0:T(8,128)(2,1)}, bf16[256,1024]{1,0:T(8,128)(2,1)}, f32[256,2048]{1,0:T(8,128)}, f32[256,1024]{1,0:T(8,128)}) custom-call(f32[2048,1024]{1,0:T(8,128)} %get-tuple-element.359.refs_0_, f32[2048,1024]{1,0:T(8,128)} %get-tuple-element.355.refs_11_.refs_1_, ...), custom_call_target="tpu_custom_call", output_to_operand_aliasing={{0}: (9, {})} | custom-call | tf_op jit(solution)/shard_map/up_back_own_y/pallas_call | solution.py:501
  442.3 14.1 %convolution_convert_fusion = bf16[2048,1024]{1,0:T(8,128)(2,1)} fusion(bf16[2048,2048]{1,0:T(8,128)(2,1)} %get-tuple-element.375, bf16[2048,1024]{1,0:T(8,128)(2,1)} %get-tuple-element.376), kind=kOutput, calls=%fused_computation | convolution fusion | flops 8592031744 | bytes 16777216 | tf_op jit(solution)/shard_map/dot_general | solution.py:251
  456.3 8.0 %collective-permute-done.57 = bf16[256,1024]{1,0:T(8,128)(2,1)} collective-permute-done((bf16[256,1024]{1,0:T(8,128)(2,1)}, bf16[256,1024]{1,0:T(8,128)(2,1)}, u32[]{:S(2)}, u32[]{:S(2)}) %collective-permute-start.57) | collective-permute-done | bytes 524320 | tf_op jit(solution)/shard_map/ppermute | solution.py:57
  471.7 10.2 %down_other.1 = (bf16[256,2048]{1,0:T(8,128)(2,1)}, bf16[256,2048]{1,0:T(8,128)(2,1)}, bf16[256,2048]{1,0:T(8,128)(2,1)}, bf16[256,2048]{1,0:T(8,128)(2,1)}) custom-call(bf16[2048,1024]{1,0:T(8,128)(2,1)} %get-tuple-element.385.refs_0_, bf16[2048,1024]{1,0:T(8,128)(2,1)} %all-gather.11.cloned.1.call-done.refs_10_.refs_1_), custom_call_target="tpu_custom_call" | custom-call | tf_op jit(solution)/shard_map/down_other/pallas_call | solution.py:501
  491.5 7.5 down_own_x.1
  499.9 7.7 %down_own_y.1 = (bf16[256,1024]{1,0:T(8,128)(2,1)}, f32[256,2048]{1,0:T(8,128)}, f32[256,1024]{1,0:T(8,128)}) custom-call(bf16[2048,1024]{1,0:T(8,128)(2,1)} %get-tuple-element.385.refs_0_, bf16[2048,1024]{1,0:T(8,128)(2,1)} %all-gather.11.cloned.1.call-done.refs_10_.refs_1_, bf16[256,2048]{1,0:T(8,128)(2,1)} %copy-done.24, ...), custom_call_target="tpu_custom_call" | custom-call | tf_op jit(solution)/shard_map/down_own_y/pallas_call | solution.py:501
  507.7 7.0 collective-permute-done.66.refs_2_
  517.5 13.4 %collective-permute-done.71.refs_4_ = bf16[128,2048]{1,0:T(8,128)(2,1)S(1)} collective-permute-done((bf16[128,2048]{1,0:T(8,128)(2,1)S(1)}, bf16[128,2048]{1,0:T(8,128)(2,1)S(1)}, u32[]{:S(2)}, u32[]{:S(2)}) %collective-permute-start.71) | collective-permute-done | bytes 524320 | tf_op jit(solution)/shard_map/ppermute | solution.py:57
  538.8 11.3 %out_back.1 = (bf16[2048,2048]{1,0:T(8,128)(2,1)}, f32[2048,256]{1,0:T(8,128)}, f32[2,2048]{1,0:T(2,128)}, f32[2,256]{1,0:T(2,128)}) custom-call(bf16[256,2048]{1,0:T(8,128)(2,1)} %copy-done.12, bf16[256,2048]{1,0:T(8,128)(2,1)} %copy-done.16, bf16[256,2048]{1,0:T(8,128)(2,1)} %copy-done.15, bf16[128,2048]{1,0:T(8,128)(2,1)} %copy-done.58, ...), custom_call_target="tpu_custom_call" | custom-call | tf_op jit(solution)/shard_map/out_back/pallas_call | solution.py:370
  560.6 7.1 convolution_convert_fusion.3
  580.3 29.5 %attend_back.1.refs_0_ = bf16[2048,768]{1,0:T(8,128)(2,1)} custom-call(s32[2,5]{1,0:T(2,128)S(1)} %pad_add_fusion.info, bf16[2048,768]{1,0:T(8,128)(2,1)} %get-tuple-element.439.qkv, f32[2048,256]{1,0:T(8,128)} %get-tuple-element.298.refs_0_.refs_11_.attended, f32[2048,256]{1,0:T(8,128)} %get-tuple-element.440.grad, f32[2,2048]{1,0:T(2,128)S(1)} %copy-done.3, ...), custom_call_target="tpu_custom_call" | custom-call | tf_op jit(solution)/shard_map/attend_back/pallas_call | solution.py:716
  609.8 11.4 %convolution_convert_fusion.2 = bf16[2048,768]{1,0:T(8,128)(2,1)} fusion(bf16[2048,2048]{1,0:T(8,128)(2,1)} %get-tuple-element.446, bf16[2048,768]{1,0:T(8,128)(2,1)} %attend_back.1.refs_0_), kind=kOutput, calls=%fused_computation.2 | convolution fusion | flops 6444023808 | bytes 14680064 | tf_op jit(solution)/shard_map/dot_general | solution.py:251
  621.2 8.6 %project_back_other.1 = (bf16[256,2048]{1,0:T(8,128)(2,1)}, bf16[256,2048]{1,0:T(8,128)(2,1)}, bf16[256,2048]{1,0:T(8,128)(2,1)}, bf16[256,2048]{1,0:T(8,128)(2,1)}) custom-call(bf16[2048,768]{1,0:T(8,128)(2,1)} %attend_back.1.refs_0_, bf16[2048,768]{1,0:T(8,128)(2,1)} %all-gather.5.cloned.1.call-done.refs_10_.refs_1_), custom_call_target="tpu_custom_call" | custom-call | tf_op jit(solution)/shard_map/project_back_other/pallas_call | solution.py:501
  668.1 9.4 %collective-permute-done.87 = bf16[256,1024]{1,0:T(8,128)(2,1)S(1)} collective-permute-done((bf16[256,1024]{1,0:T(8,128)(2,1)}, bf16[256,1024]{1,0:T(8,128)(2,1)S(1)}, u32[]{:S(2)}, u32[]{:S(2)}) %collective-permute-start.87) | collective-permute-done | bytes 524320 | tf_op jit(solution)/shard_map/ppermute | solution.py:57
  678.9 10.9 %collective-permute-done.91 = bf16[256,1024]{1,0:T(8,128)(2,1)S(1)} collective-permute-done((bf16[256,1024]{1,0:T(8,128)(2,1)S(1)}, bf16[256,1024]{1,0:T(8,128)(2,1)S(1)}, u32[]{:S(2)}, u32[]{:S(2)}) %collective-permute-start.91) | collective-permute-done | bytes 524320 | tf_op jit(solution)/shard_map/ppermute | solution.py:57
  721.6 19.1 %collective-permute-done.96.values = bf16[256,2048]{1,0:T(8,128)(2,1)S(1)} collective-permute-done((bf16[256,2048]{1,0:T(8,128)(2,1)S(1)}, bf16[256,2048]{1,0:T(8,128)(2,1)S(1)}, u32[]{:S(2)}, u32[]{:S(2)}) %collective-permute-start.96) | collective-permute-done | bytes 1048608 | tf_op jit(solution)/shard_map/ppermute | solution.py:962
  (592 shorter events, 324.9 us)
Async XLA Ops:
  13.9 40.2 %collective-permute-start = (bf16[256,2048]{1,0:T(8,128)(2,1)S(1)}, bf16[256,2048]{1,0:T(8,128)(2,1)S(1)}, u32[]{:S(2)}, u32[]{:S(2)}) collective-permute-start(bf16[256,2048]{1,0:T(8,128)(2,1)S(1)} %reorder.4), channel_id=1, source_target_pairs={{0,27},{1,19},{2,11},{3,3},{4,4},{5,12},{6,20},{7,28},{8,13},{9,5}... | collective-permute-start | bytes 3145736 | tf_op jit(solution)/shard_map/ppermute | solution.py:786
  19.2 28.2 %all-to-all-start = ((bf16[8,64,1024]{2,1,0:T(8,128)(2,1)}), bf16[8,64,1024]{2,1,0:T(8,128)(2,1)S(1)}, u32[]{:S(2)}, u32[]{:S(2)}) async-start(bf16[8,64,1024]{2,1,0:T(8,128)(2,1)} %pad_maximum_fusion.4), calls=%async_computation | async-start | bytes 2097152 | tf_op jit(solution)/shard_map/all_to_all | solution.py:156
  25.2 108.7 %all-gather.5.cloned.1.call-start = ((), (), s32[]{:S(2)}) async-start(), calls=%async_computation.9 | async-start | bytes 3932160 | tf_op jit(solution)/shard_map/all_gather | solution.py:161
  77.4 23.6 %collective-permute-start.7 = (bf16[256,2048]{1,0:T(8,128)(2,1)S(1)}, bf16[256,2048]{1,0:T(8,128)(2,1)S(1)}, u32[]{:S(2)}, u32[]{:S(2)}) collective-permute-start(bf16[256,2048]{1,0:T(8,128)(2,1)S(1)} %fusion.7.refs_0_), channel_id=1, source_target_pairs={{0,16},{4,20},{8,24},{12,28},{16,0},{20,4},{24,8},{28,12},{1,17},{... | collective-permute-start | bytes 3145736 | tf_op jit(solution)/shard_map/ppermute | solution.py:57
  79.4 23.1 %collective-permute-start.6 = (bf16[256,2048]{1,0:T(8,128)(2,1)S(1)}, bf16[256,2048]{1,0:T(8,128)(2,1)S(1)}, u32[]{:S(2)}, u32[]{:S(2)}) collective-permute-start(bf16[256,2048]{1,0:T(8,128)(2,1)S(1)} %fusion.7.refs_0_), channel_id=1, source_target_pairs={{0,8},{4,12},{8,0},{12,4},{16,24},{20,28},{24,16},{28,20},{1,9},{5... | collective-permute-start | bytes 3145736 | tf_op jit(solution)/shard_map/ppermute | solution.py:57
  123.0 61.8 %all-to-all-start.1 = ((bf16[8,64,2048]{2,1,0:T(8,128)(2,1)}), bf16[8,64,2048]{2,1,0:T(8,128)(2,1)}, u32[]{:S(2)}, u32[]{:S(2)}) async-start(bf16[8,64,2048]{2,1,0:T(8,128)(2,1)} %pad_maximum_fusion), calls=%async_computation.1 | async-start | bytes 4194304 | tf_op jit(solution)/shard_map/all_to_all | solution.py:156
  127.6 67.4 %all-gather.7.cloned.1.call-start = ((), (), s32[]{:S(2)}) async-start(), calls=%async_computation.10 | async-start | bytes 1310720 | tf_op jit(solution)/shard_map/all_gather | solution.py:161
  127.6 57.2 %collective-permute-start.15 = (bf16[256,2048]{1,0:T(8,128)(2,1)}, bf16[256,2048]{1,0:T(8,128)(2,1)}, u32[]{:S(2)}, u32[]{:S(2)}) collective-permute-start(bf16[256,2048]{1,0:T(8,128)(2,1)} %reorder.5), channel_id=1, source_target_pairs={{0,27},{1,19},{2,11},{3,3},{4,4},{5,12},{6,20},{7,28},{8,13},{9,5}... | collective-permute-start | bytes 3145736 | tf_op jit(solution)/shard_map/ppermute | solution.py:837
  133.3 169.6 %all-gather.9.cloned.1.call-start = ((), (), s32[]{:S(2)}) async-start(), calls=%async_computation.11 | async-start | bytes 5242880 | tf_op jit(solution)/shard_map/all_gather | solution.py:161
  189.5 164.4 %all-gather.11.cloned.1.call-start = ((), (), s32[]{:S(2)}) async-start(), calls=%async_computation.12 | async-start | bytes 5242880 | tf_op jit(solution)/shard_map/all_gather | solution.py:161
  212.4 26.7 %collective-permute-start.23 = (bf16[512,1024]{1,0:T(8,128)(2,1)}, bf16[512,1024]{1,0:T(8,128)(2,1)S(1)}, u32[]{:S(2)}, u32[]{:S(2)}) collective-permute-start(bf16[512,1024]{1,0:T(8,128)(2,1)} %get-tuple-element.313), channel_id=1, source_target_pairs={{0,8},{4,12},{8,0},{12,4},{16,24},{20,28},{24,16},{28,20},{1,9},{5... | collective-permute-start | bytes 3145736 | tf_op jit(solution)/shard_map/ppermute | solution.py:57
  256.1 23.5 %collective-permute-start.29 = (bf16[256,2048]{1,0:T(8,128)(2,1)}, bf16[256,2048]{1,0:T(8,128)(2,1)}, u32[]{:S(2)}, u32[]{:S(2)}) collective-permute-start(bf16[256,2048]{1,0:T(8,128)(2,1)} %add_convert_fusion.refs_0_), channel_id=1, source_target_pairs={{0,16},{4,20},{8,24},{12,28},{16,0},{20,4},{24,8},{28,12},{1,17},{... | collective-permute-start | bytes 3145736 | tf_op jit(solution)/shard_map/ppermute | solution.py:57
  256.5 23.5 %collective-permute-start.28 = (bf16[256,2048]{1,0:T(8,128)(2,1)}, bf16[256,2048]{1,0:T(8,128)(2,1)}, u32[]{:S(2)}, u32[]{:S(2)}) collective-permute-start(bf16[256,2048]{1,0:T(8,128)(2,1)} %add_convert_fusion.refs_0_), channel_id=1, source_target_pairs={{0,8},{4,12},{8,0},{12,4},{16,24},{20,28},{24,16},{28,20},{1,9},{5... | collective-permute-start | bytes 3145736 | tf_op jit(solution)/shard_map/ppermute | solution.py:57
  258.2 276.0 %reduce-scatter.5.cloned.1.call-start = ((), (), s32[]{:S(2)}) async-start(), calls=%async_computation.13 | async-start | bytes 5242880 | tf_op jit(solution)/shard_map/reduce_scatter | solution.py:165
  301.1 25.5 %collective-permute-start.38 = (bf16[256,2048]{1,0:T(8,128)(2,1)}, bf16[256,2048]{1,0:T(8,128)(2,1)}, u32[]{:S(2)}, u32[]{:S(2)}) collective-permute-start(bf16[256,2048]{1,0:T(8,128)(2,1)} %collective-permute-done.15.refs_0_), channel_id=1, source_target_pairs={{0,16},{4,20},{8,24},{12,28},{16,0},{20,4},{24,8},{28,12},{1,17},{... | collective-permute-start | bytes 3145736 | tf_op jit(solution)/shard_map/ppermute | solution.py:57
  302.3 25.2 %collective-permute-start.37 = (bf16[256,2048]{1,0:T(8,128)(2,1)}, bf16[256,2048]{1,0:T(8,128)(2,1)}, u32[]{:S(2)}, u32[]{:S(2)}) collective-permute-start(bf16[256,2048]{1,0:T(8,128)(2,1)} %collective-permute-done.15.refs_0_), channel_id=1, source_target_pairs={{0,8},{4,12},{8,0},{12,4},{16,24},{20,28},{24,16},{28,20},{1,9},{5... | collective-permute-start | bytes 3145736 | tf_op jit(solution)/shard_map/ppermute | solution.py:57
  330.6 22.1 %collective-permute-start.39 = (bf16[256,2048]{1,0:T(8,128)(2,1)}, bf16[256,2048]{1,0:T(8,128)(2,1)}, u32[]{:S(2)}, u32[]{:S(2)}) collective-permute-start(bf16[256,2048]{1,0:T(8,128)(2,1)} %collective-permute-done.15.refs_0_), channel_id=1, source_target_pairs={{0,4},{4,0},{8,12},{12,8},{16,20},{20,16},{24,28},{28,24},{1,5},{5... | collective-permute-start | bytes 3145736 | tf_op jit(solution)/shard_map/ppermute | solution.py:57
  398.6 169.2 %reduce-scatter.7.cloned.1.call-start = ((), (), s32[]{:S(2)}) async-start(), calls=%async_computation.14 | async-start | bytes 5242880 | tf_op jit(solution)/shard_map/reduce_scatter | solution.py:165
  439.6 24.7 %collective-permute-start.57 = (bf16[256,1024]{1,0:T(8,128)(2,1)}, bf16[256,1024]{1,0:T(8,128)(2,1)}, u32[]{:S(2)}, u32[]{:S(2)}) collective-permute-start(bf16[256,1024]{1,0:T(8,128)(2,1)} %get-tuple-element.373), channel_id=1, source_target_pairs={{0,16},{4,20},{8,24},{12,28},{16,0},{20,4},{24,8},{28,12},{1,17},{... | collective-permute-start | bytes 1572872 | tf_op jit(solution)/shard_map/ppermute | solution.py:57
  440.9 24.9 %collective-permute-start.56 = (bf16[512,1024]{1,0:T(8,128)(2,1)}, bf16[512,1024]{1,0:T(8,128)(2,1)}, u32[]{:S(2)}, u32[]{:S(2)}) collective-permute-start(bf16[512,1024]{1,0:T(8,128)(2,1)} %get-tuple-element.372), channel_id=1, source_target_pairs={{0,8},{4,12},{8,0},{12,4},{16,24},{20,28},{24,16},{28,20},{1,9},{5... | collective-permute-start | bytes 3145736 | tf_op jit(solution)/shard_map/ppermute | solution.py:57
  490.2 24.5 %collective-permute-start.66 = (bf16[256,2048]{1,0:T(8,128)(2,1)S(1)}, bf16[256,2048]{1,0:T(8,128)(2,1)S(1)}, u32[]{:S(2)}, u32[]{:S(2)}) collective-permute-start(bf16[256,2048]{1,0:T(8,128)(2,1)S(1)} %get-tuple-element.414.refs_0_), channel_id=1, source_target_pairs={{0,16},{4,20},{8,24},{12,28},{16,0},{20,4},{24,8},{28,12},{1,17},{... | collective-permute-start | bytes 3145736 | tf_op jit(solution)/shard_map/ppermute | solution.py:57
  491.0 24.9 %collective-permute-start.65 = (bf16[256,2048]{1,0:T(8,128)(2,1)S(1)}, bf16[256,2048]{1,0:T(8,128)(2,1)S(1)}, u32[]{:S(2)}, u32[]{:S(2)}) collective-permute-start(bf16[256,2048]{1,0:T(8,128)(2,1)S(1)} %get-tuple-element.414.refs_0_), channel_id=1, source_target_pairs={{0,8},{4,12},{8,0},{12,4},{16,24},{20,28},{24,16},{28,20},{1,9},{5... | collective-permute-start | bytes 3145736 | tf_op jit(solution)/shard_map/ppermute | solution.py:57
  538.8 82.4 %reduce-scatter.9.cloned.1.call-start = ((), (), s32[]{:S(2)}) async-start(), calls=%async_computation.15 | async-start | bytes 1310720 | tf_op jit(solution)/shard_map/reduce_scatter | solution.py:165
  567.8 42.0 %collective-permute-start.77 = (bf16[512,1024]{1,0:T(8,128)(2,1)}, bf16[512,1024]{1,0:T(8,128)(2,1)}, u32[]{:S(2)}, u32[]{:S(2)}) collective-permute-start(bf16[512,1024]{1,0:T(8,128)(2,1)} %get-tuple-element.436), channel_id=1, source_target_pairs={{0,8},{4,12},{8,0},{12,4},{16,24},{20,28},{24,16},{28,20},{1,9},{5... | collective-permute-start | bytes 3145736 | tf_op jit(solution)/shard_map/ppermute | solution.py:57
  568.4 41.4 %collective-permute-start.78 = (bf16[256,1024]{1,0:T(8,128)(2,1)}, bf16[256,1024]{1,0:T(8,128)(2,1)}, u32[]{:S(2)}, u32[]{:S(2)}) collective-permute-start(bf16[256,1024]{1,0:T(8,128)(2,1)} %get-tuple-element.437), channel_id=1, source_target_pairs={{0,16},{4,20},{8,24},{12,28},{16,0},{20,4},{24,8},{28,12},{1,17},{... | collective-permute-start | bytes 1572872 | tf_op jit(solution)/shard_map/ppermute | solution.py:57
  569.0 40.7 %collective-permute-start.79 = (bf16[256,1024]{1,0:T(8,128)(2,1)}, bf16[256,1024]{1,0:T(8,128)(2,1)}, u32[]{:S(2)}, u32[]{:S(2)}) collective-permute-start(bf16[256,1024]{1,0:T(8,128)(2,1)} %get-tuple-element.438), channel_id=1, source_target_pairs={{0,16},{4,20},{8,24},{12,28},{16,0},{20,4},{24,8},{28,12},{1,17},{... | collective-permute-start | bytes 1572872 | tf_op jit(solution)/shard_map/ppermute | solution.py:57
  574.2 47.0 %all-to-all-start.3 = ((bf16[8,64,1024]{2,1,0:T(8,128)(2,1)}), bf16[8,64,1024]{2,1,0:T(8,128)(2,1)}, u32[]{:S(2)}, u32[]{:S(2)}) async-start(bf16[8,64,1024]{2,1,0:T(8,128)(2,1)} %bitcast.134), calls=%async_computation.5 | async-start | bytes 2097152 | tf_op jit(solution)/shard_map/all_to_all | solution.py:156
  579.0 123.5 %reduce-scatter.11.cloned.1.call-start = ((), (), s32[]{:S(2)}) async-start(), calls=%async_computation.16 | async-start | bytes 3932160 | tf_op jit(solution)/shard_map/reduce_scatter | solution.py:165
  645.9 31.5 %collective-permute-start.85 = (bf16[512,1024]{1,0:T(8,128)(2,1)}, bf16[512,1024]{1,0:T(8,128)(2,1)S(1)}, u32[]{:S(2)}, u32[]{:S(2)}) collective-permute-start(bf16[512,1024]{1,0:T(8,128)(2,1)} %get-tuple-element.455), channel_id=1, source_target_pairs={{0,8},{4,12},{8,0},{12,4},{16,24},{20,28},{24,16},{28,20},{1,9},{5... | collective-permute-start | bytes 3145736 | tf_op jit(solution)/shard_map/ppermute | solution.py:57
  705.0 41.3 %all-to-all-start.4 = ((bf16[8,80,1024]{2,1,0:T(8,128)(2,1)}), bf16[8,80,1024]{2,1,0:T(8,128)(2,1)}, u32[]{:S(2)}, u32[]{:S(2)}) async-start(bf16[8,80,1024]{2,1,0:T(8,128)(2,1)} %pad_maximum_fusion.3), calls=%async_computation.8 | async-start | bytes 2621440 | tf_op jit(solution)/shard_map/all_to_all | solution.py:156
  710.1 30.6 %collective-permute-start.96 = (bf16[256,2048]{1,0:T(8,128)(2,1)S(1)}, bf16[256,2048]{1,0:T(8,128)(2,1)S(1)}, u32[]{:S(2)}, u32[]{:S(2)}) collective-permute-start(bf16[256,2048]{1,0:T(8,128)(2,1)S(1)} %copy-done.23), channel_id=1, source_target_pairs={{27,0},{19,1},{11,2},{3,3},{4,4},{12,5},{20,6},{28,7},{13,8},{5,9}... | collective-permute-start | bytes 3145736 | tf_op jit(solution)/shard_map/ppermute | solution.py:962
  716.3 46.4 %collective-permute-start.95 = (bf16[256,2048]{1,0:T(8,128)(2,1)}, bf16[256,2048]{1,0:T(8,128)(2,1)S(1)}, u32[]{:S(2)}, u32[]{:S(2)}) collective-permute-start(bf16[256,2048]{1,0:T(8,128)(2,1)} %fusion.12), channel_id=1, source_target_pairs={{27,0},{19,1},{11,2},{3,3},{4,4},{12,5},{20,6},{28,7},{13,8},{5,9}... | collective-permute-start | bytes 3145736 | tf_op jit(solution)/shard_map/ppermute | solution.py:971
  (159 other events, 1618.2 us)
Sparse Core Ops, SparseCore 0:
  59.4 64.7 all-gather.4
  133.5 39.1 all-gather.6
  189.6 80.4 all-gather.8
  271.5 79.2 all-gather.10
  398.7 76.4 reduce-scatter.4
  477.5 77.2 reduce-scatter.6
  570.6 27.8 reduce-scatter.8
  630.1 61.1 reduce-scatter.10
